TPU v7x, 256 devices: a whole 4x4x8 slice. The times are simulated.
256 devices in a mesh: row: 32 (over x, y, core), col: 8 (over z).
Axes of the slice: x: 4, y: 4, z: 8, core: 2. Of those that a mesh axis runs over, the one named last changes fastest.
Arguments:
- features: bfloat16 [65536, 512], P(('row', 'col')), may hold values from -6 to 6
- tile_values: bfloat16 [512, 8, 128, 4, 128], P('row', 'col'), may hold values from -0.09375 to 0.09375
- slot_refs: int32 [512, 8, 4], P('row', 'col'), may hold values from 0 to 31, as said below
- wanted: int32 [32, 8, 32, 1], P('row', 'col'), may hold values from 0 to 1, as said below
- time_ids: int32 [65536], P(('row', 'col')), may hold values from 0 to 127
- cond_ids: int32 [65536], P(('row', 'col')), may hold values from 0 to 15
- time_table: bfloat16 [128, 512], replicated, may hold values from -3 to 3
- cond_table: bfloat16 [16, 512], replicated, may hold values from -2.5 to 2.5
- gains: float32 [2, 512], replicated, may hold values from 0.1 to 1.9
- w_in: bfloat16 [2, 512, 2048], replicated, may hold values from -0.25 to 0.25
- w_out: bfloat16 [2, 2048, 512], replicated, may hold values from -0.125 to 0.125
Outputs:
- denoised: bfloat16 [65536, 512], P(('row', 'col'))
Inputs may be any that keep to these rules, and one draw needn't show every extreme that they name: `slot_refs`: every value 0 to 31 is named by some slot among the rows of one device and one column block. `wanted`: the 1 offsets of one device for one peer are distinct.
All inputs are finite; a program needn't handle non-finite values.
Results may differ from a plain program's by a relative error of at most 0.006.
Values may be sent and summed in bfloat16 or wider, within the bound.
No kernel may reach another device: no remote copies, remote signals or barrier semaphores. Data moves between devices by JAX's collectives and lax.ppermute only.
A program may use at most 64 MiB of HBM per device.

v0:
```python
import jax
import jax.numpy as jnp
from jax import lax
from jax.sharding import PartitionSpec as P

LAYERS = 2


epsilon = 1e-06


def lookup(ids, table):
    onehot = (ids[:, None] == jnp.arange(table.shape[0], dtype=jnp.int32)[None, :]).astype(
        jnp.bfloat16
    )
    return jnp.dot(onehot, table, preferred_element_type=jnp.float32)


def local(
    features,
    tile_values,
    slot_refs,
    wanted,
    time_ids,
    cond_ids,
    time_table,
    cond_table,
    gains,
    w_in,
    w_out,
):
    row_count = lax.axis_size("row")
    span, width = features.shape
    tile = tile_values.shape[-1]
    slots = tile_values.shape[3]
    per_span = span // tile
    row_tiles = tile_values.shape[0]
    refer = wanted.shape[-1]
    matrix = tile_values.reshape(row_tiles, tile, slots * tile)
    slot_index = slot_refs.reshape(row_tiles, slots)
    wanted_local = wanted.reshape(row_count, refer)
    cond_rows = lookup(cond_ids, cond_table)
    time_rows = lookup(time_ids, time_table)
    state = features
    for layer in range(LAYERS):
        column = lax.all_gather(state, "row", axis=0, tiled=True).reshape(
            row_count * per_span, tile, width
        )
        place = (jnp.arange(row_count, dtype=jnp.int32)[:, None] * per_span + wanted_local).reshape(
            -1
        )
        source = column[place]
        count = lax.axis_size("col") * span
        number = count // tile
        right = source[slot_index.reshape(-1)].reshape(number, slots * tile, width)
        product = jnp.einsum("tik,tkf->tif", matrix, right, preferred_element_type=jnp.float32)
        aggregate = lax.psum_scatter(
            product.reshape(count, width), "col", scatter_dimension=0, tiled=True
        )
        pre = state.astype(jnp.float32) + aggregate
        scale = lax.rsqrt(jnp.mean(pre * pre, axis=-1, keepdims=True) + epsilon)
        normed = (pre * scale * gains[layer] * (1.0 + cond_rows) + time_rows).astype(jnp.bfloat16)
        inner = jnp.dot(normed, w_in[layer], preferred_element_type=jnp.float32)
        hidden = jax.nn.silu(inner).astype(jnp.bfloat16)
        state = (pre + jnp.dot(hidden, w_out[layer], preferred_element_type=jnp.float32)).astype(
            jnp.bfloat16
        )
    return state


def solution(mesh):
    return jax.shard_map(
        local,
        mesh=mesh,
        in_specs=(
            P(("row", "col"), None),
            P("row", "col", None, None, None),
            P("row", "col", None),
            P("row", "col", None, None),
            P(("row", "col")),
            P(("row", "col")),
            P(),
            P(),
            P(),
            P(),
            P(),
        ),
        out_specs=P(("row", "col"), None),
        check_vma=False,
    )
```

profile of v0, /device:TPU:1, one launch (start us, length us, event | category | flops | bytes accessed | tf_op | source)
XLA Modules:
  0.0 298.4 jit_solution(2763270349611351940)
XLA Ops:
  6.5 0.0 copy-start
  6.5 0.0 copy-start.6
  6.5 0.0 all-gather.3.cloned.1.call-start
  6.5 0.7 all-gather.3.cloned.1.call-update
  7.3 0.0 reduce-scatter.3.cloned.1.call-start
  7.3 0.8 copy.13
  8.1 0.1 reshape_reshape.4
  8.2 2.8 reshape.107
  10.9 0.0 copy-done.6
  11.0 61.1 %all-gather.3.cloned.1.call-done = bf16[8192,512]{1,0:T(8,128)(2,1)} async-done(((bf16[256,512]{1,0:T(8,128)(2,1)}), bf16[8192,512]{1,0:T(8,128)(2,1)}) %all-gather.3.cloned.1.call-update) | async-done | bytes 8388624 | tf_op jit(solution)/shard_map/all_gather | solution.py:46
  72.1 6.2 %gather_fusion = bf16[32,128,512]{2,1,0:T(8,128)(2,1)} fusion(bf16[64,128,512]{2,1,0:T(8,128)(2,1)} %bitcast.60, s32[1024]{0:T(1024)S(1)} %pad_clamp_fusion.1), kind=kCustom, calls=%fused_computation | custom fusion | bytes 8388736 | tf_op jit(solution)/shard_map/gather | solution.py:52
  78.2 7.7 %gather_fusion.1 = bf16[64,128,512]{2,1,0:T(8,128)(2,1)} fusion(bf16[32,128,512]{2,1,0:T(8,128)(2,1)} %gather_fusion, s32[1024]{0:T(1024)S(1)} %pad_clamp_fusion), kind=kCustom, calls=%fused_computation.1 | custom fusion | bytes 16777472 | tf_op jit(solution)/shard_map/gather | solution.py:55
  86.0 6.6 %fusion.48 = f32[16,512,128]{1,2,0:T(8,128)} fusion(bf16[16,128,512]{2,1,0:T(8,128)(2,1)S(1)} %reshape.107, bf16[16,512,512]{2,1,0:T(8,128)(2,1)} %bitcast.57), kind=kOutput, calls=%fused_computation.50 | convolution fusion | flops 1073741824 | bytes 14680064 | tf_op jit(solution)/shard_map/tik,tkf->tif/dot_general | solution.py:56
  92.6 0.0 copy-start.4
  92.6 0.0 copy-start.3
  92.6 0.0 copy-start.5
  92.6 0.0 copy-start.1
  92.6 0.0 reduce-scatter.3.cloned.1.call-update
  92.6 0.0 all-gather.5.cloned.1.call-start
  92.6 0.6 copy-done.4
  93.3 0.0 copy-done.3
  93.3 0.0 copy-done.5
  93.3 0.3 convolution_add_fusion
  93.6 0.0 copy-done
  93.6 0.9 fusion.40
  94.5 52.8 %reduce-scatter.3.cloned.1.call-done = f32[256,512]{1,0:T(8,128)} async-done(((f32[2048,512]{1,0:T(8,128)}), f32[256,512]{1,0:T(8,128)}) %reduce-scatter.3.cloned.1.call-update) | async-done | bytes 524304 | tf_op jit(solution)/shard_map/reduce_scatter | solution.py:57
  147.4 0.0 copy-done.1
  147.4 1.2 multiply_reduce_fusion.1
  148.5 0.6 add_rsqrt_fusion.1
  149.1 4.6 %fusion.25 = bf16[256,512]{1,0:T(8,128)(2,1)} fusion(bf16[2,2048,512]{2,1,0:T(8,128)(2,1)} %param.21, bf16[2,512,2048]{2,1,0:T(8,128)(2,1)} %param.20, f32[256,512]{1,0:T(8,128)S(1)} %fusion.40, f32[256,512]{1,0:T(8,128)S(1)} %convolution_add_fusion, f32[256,512]{1,0:T(8,128)} %reduce-scatter.3.cloned.1.call-done, bf16[256,512]{1,0:T(8,128)(2,1)S(1)} %copy-done.1, ...), kind=kOutput, calls=%fused_computation.22 | convolution fusion | flops 1077805056 | bytes 7080960 | tf_op jit(solution)/shard_map/dot_general | solution.py:65
  153.7 0.0 all-gather.5.cloned.1.call-update
  153.8 0.0 reduce-scatter.5.cloned.1.call-start
  153.8 57.0 %all-gather.5.cloned.1.call-done = bf16[8192,512]{1,0:T(8,128)(2,1)} async-done(((bf16[256,512]{1,0:T(8,128)(2,1)}), bf16[8192,512]{1,0:T(8,128)(2,1)}) %all-gather.5.cloned.1.call-update) | async-done | bytes 8388624 | tf_op jit(solution)/shard_map/all_gather | solution.py:46
  210.8 6.2 %gather_fusion.2 = bf16[32,128,512]{2,1,0:T(8,128)(2,1)} fusion(bf16[64,128,512]{2,1,0:T(8,128)(2,1)} %bitcast.61, s32[1024]{0:T(1024)S(1)} %pad_clamp_fusion.1), kind=kCustom, calls=%fused_computation.2 | custom fusion | bytes 8388736 | tf_op jit(solution)/shard_map/gather | solution.py:52
  217.0 7.7 %gather_fusion.3 = bf16[64,128,512]{2,1,0:T(8,128)(2,1)} fusion(bf16[32,128,512]{2,1,0:T(8,128)(2,1)} %gather_fusion.2, s32[1024]{0:T(1024)S(1)} %pad_clamp_fusion), kind=kCustom, calls=%fused_computation.3 | custom fusion | bytes 16777472 | tf_op jit(solution)/shard_map/gather | solution.py:55
  224.7 6.6 %fusion.49 = f32[16,512,128]{1,2,0:T(8,128)} fusion(bf16[16,128,512]{2,1,0:T(8,128)(2,1)S(1)} %reshape.107, bf16[16,512,512]{2,1,0:T(8,128)(2,1)} %bitcast.56), kind=kOutput, calls=%fused_computation.51 | convolution fusion | flops 1073741824 | bytes 14680064 | tf_op jit(solution)/shard_map/tik,tkf->tif/dot_general | solution.py:56
  231.3 0.0 copy-start.2
  231.3 0.0 reduce-scatter.5.cloned.1.call-update
  231.3 54.7 %reduce-scatter.5.cloned.1.call-done = f32[256,512]{1,0:T(8,128)} async-done(((f32[2048,512]{1,0:T(8,128)}), f32[256,512]{1,0:T(8,128)}) %reduce-scatter.5.cloned.1.call-update) | async-done | bytes 524304 | tf_op jit(solution)/shard_map/reduce_scatter | solution.py:57
  286.1 0.0 copy-done.2
  286.1 1.2 multiply_reduce_fusion
  287.3 4.6 %fusion.22 = bf16[256,512]{1,0:T(8,128)(2,1)} fusion(bf16[2,2048,512]{2,1,0:T(8,128)(2,1)} %param.21, bf16[2,512,2048]{2,1,0:T(8,128)(2,1)} %param.20, f32[256,512]{1,0:T(8,128)S(1)} %fusion.40, f32[256,512]{1,0:T(8,128)S(1)} %convolution_add_fusion, f32[256,512]{1,0:T(8,128)} %reduce-scatter.5.cloned.1.call-done, bf16[256,512]{1,0:T(8,128)(2,1)S(1)} %copy-done.2, ...), kind=kOutput, calls=%fused_computation.21 | convolution fusion | flops 1077805056 | bytes 7080960 | tf_op jit(solution)/shard_map/dot_general | solution.py:65
  (6 shorter events, 0.0 us)
Async XLA Ops:
  6.5 87.0 %copy-start = (bf16[128,512]{1,0:T(8,128)(2,1)S(1)}, bf16[128,512]{1,0:T(8,128)(2,1)}, u32[]{:S(2)}) copy-start(bf16[128,512]{1,0:T(8,128)(2,1)} %param.17) | copy-start | bytes 393220
  6.5 4.4 %copy-start.6 = (s32[1,1,32,1]{2,3,1,0:T(1,128)S(1)}, s32[1,1,32,1]{2,3,1,0:T(1,128)}, u32[]{:S(2)}) copy-start(s32[1,1,32,1]{2,3,1,0:T(1,128)} %param.14) | copy-start | bytes 388
  6.5 65.5 %all-gather.3.cloned.1.call-start = ((), (), s32[]{:S(2)}) async-start(), calls=%async_computation.2 | async-start | bytes 8650752 | tf_op jit(solution)/shard_map/all_gather | solution.py:46
  7.3 140.1 %reduce-scatter.3.cloned.1.call-start = ((), (), s32[]{:S(2)}) async-start(), calls=%async_computation.3 | async-start | bytes 4718592 | tf_op jit(solution)/shard_map/reduce_scatter | solution.py:57
  92.6 0.7 copy-start.4
  92.6 0.7 copy-start.3
  92.6 0.7 copy-start.5
  92.6 54.8 %copy-start.1 = (bf16[256,512]{1,0:T(8,128)(2,1)S(1)}, bf16[256,512]{1,0:T(8,128)(2,1)}, u32[]{:S(2)}) copy-start(bf16[256,512]{1,0:T(8,128)(2,1)} %param.11) | copy-start | bytes 786436
  92.6 118.2 %all-gather.5.cloned.1.call-start = ((), (), s32[]{:S(2)}) async-start(), calls=%async_computation.4 | async-start | bytes 8650752 | tf_op jit(solution)/shard_map/all_gather | solution.py:46
  153.8 132.3 %reduce-scatter.5.cloned.1.call-start = ((), (), s32[]{:S(2)}) async-start(), calls=%async_computation.5 | async-start | bytes 4718592 | tf_op jit(solution)/shard_map/reduce_scatter | solution.py:57
  231.3 54.8 %copy-start.2 = (bf16[256,512]{1,0:T(8,128)(2,1)S(1)}, bf16[256,512]{1,0:T(8,128)(2,1)}, u32[]{:S(2)}) copy-start(bf16[256,512]{1,0:T(8,128)(2,1)} %fusion.25) | copy-start | bytes 786436
Sparse Core Ops, SparseCore 0:
  9.9 62.1 all-gather.2
  92.7 54.5 reduce-scatter.2
  153.9 56.8 all-gather.4
  231.4 54.5 reduce-scatter.4
where the time goes:
time: 299 us; the launch traced here: 298 us
  waiting for transfers between devices  226 us (76%)
  local copies, waits for them, and re-layouts  32 us (11%)
  matrix products  23.6 us (8%)
  between operations  13.2 us (4%)
  other arithmetic  2.99 us (1%)
    all_gather x2, waiting for transfers between devices, local(): lax.all_gather(state, 'row', axis=0, tiled=True)  118 us
    reduce_scatter x2, waiting for transfers between devices, local(): lax.psum_scatter(product.reshape(count, width), 'col', scatter_dimension=...  108 us
    gather x2, local copies, waits for them, and re-layouts, local(): right = source[slot_index.reshape(-1)].reshape(number, slots * tile, width)  15.4 us
    dot_general x2, matrix products, local(): jnp.einsum('tik,tkf->tif', matrix, right, preferred_element_type=jnp.floa...  13.2 us
    gather x2, local copies, waits for them, and re-layouts, local(): source = column[place]  12.3 us
    dot_general x2, matrix products, local(): jnp.dot(hidden, w_out[layer], preferred_element_type=jnp.float32)  9.21 us
  transfers between devices with their start and end apart: 4, of which 4 were waited for; matrix products, arithmetic and copies ran while one was open for 2% of the time, Pallas kernels for 0%

commit v1 on v0

v1 whole, which is shorter than its diff:
```python
import jax
import jax.numpy as jnp
from jax import lax
from jax.experimental import pallas as pl
from jax.experimental.pallas import tpu as pltpu
from jax.sharding import PartitionSpec as P

LAYERS = 2
VMEM_LIMIT = 40 * 1024 * 1024

epsilon = 1e-06


def lookup(ids, table):
    onehot = (ids[:, None] == jnp.arange(table.shape[0], dtype=jnp.int32)[None, :]).astype(
        jnp.bfloat16
    )
    return jnp.dot(onehot, table, preferred_element_type=jnp.float32)


def aggregate_tiles(matrix, sources, source_row, source_slot, slot_index, order, split):
    row_tiles, tile, depth = matrix.shape
    slots = depth // tile
    width = sources[0].shape[-1]
    gathered = source_row.shape[0]
    blocks = order.shape[0]
    per_block = row_tiles // blocks
    n_src = len(sources)
    n_out = blocks if split else 1
    rows = per_block * tile

    def body(row_ref, slot_ref, index_ref, order_ref, matrix_ref, *refs):
        src = refs[:n_src]
        outs = refs[n_src : n_src + n_out]
        tiles, left, result, tile_sem, left_sem, out_sem = refs[n_src + n_out :]

        def tile_copy(b):
            start = pl.multiple_of(row_ref[b], tile)
            return pltpu.make_async_copy(
                src[b % n_src].at[pl.ds(start, tile)], tiles.at[slot_ref[b]], tile_sem.at[b]
            )

        def left_copy(k):
            return pltpu.make_async_copy(
                matrix_ref.at[pl.ds(order_ref[k] * per_block, per_block)], left.at[k], left_sem.at[k]
            )

        def out_copy(k):
            target = outs[k] if split else outs[0].at[pl.ds(k * rows, rows)]
            return pltpu.make_async_copy(result.at[k], target, out_sem.at[k])

        left_copy(0).start()
        for b in range(gathered):
            tile_copy(b).start()
        for k in range(1, blocks):
            left_copy(k).start()
        for b in range(gathered):
            tile_copy(b).wait()
        for k in range(blocks):
            left_copy(k).wait()
            for j in range(per_block):
                first = (order_ref[k] * per_block + j) * slots
                right = jnp.concatenate([tiles[index_ref[first + s]] for s in range(slots)], axis=0)
                value = jnp.dot(left[k, j], right, preferred_element_type=jnp.float32)
                result[k, j * tile : (j + 1) * tile, :] = value.astype(result.dtype)
            out_copy(k).start()
        for k in range(blocks):
            out_copy(k).wait()

    smem = pl.BlockSpec(memory_space=pltpu.SMEM)
    hbm = pl.BlockSpec(memory_space=pl.ANY)
    return pl.pallas_call(
        body,
        in_specs=[smem] * 4 + [hbm] * (1 + n_src),
        out_specs=[hbm] * n_out,
        out_shape=[jax.ShapeDtypeStruct((blocks * rows // n_out, width), jnp.bfloat16)] * n_out,
        scratch_shapes=[
            pltpu.VMEM((gathered, tile, width), jnp.bfloat16),
            pltpu.VMEM((blocks, per_block, tile, depth), jnp.bfloat16),
            pltpu.VMEM((blocks, rows, width), jnp.bfloat16),
            pltpu.SemaphoreType.DMA((gathered,)),
            pltpu.SemaphoreType.DMA((blocks,)),
            pltpu.SemaphoreType.DMA((blocks,)),
        ],
        compiler_params=pltpu.CompilerParams(vmem_limit_bytes=VMEM_LIMIT),
        name="aggregate_tiles",
    )(source_row, source_slot, slot_index, order, matrix, *sources)


def node_mlp(layer, state, parts, scale_rows, shift_rows, w_in, w_out):
    rows, width = state.shape
    hidden_units = w_in.shape[-1]
    chunks = 4
    chunk = hidden_units // chunks
    n_parts = len(parts)

    def body(state_ref, scale_ref, shift_ref, *refs):
        part_refs = refs[:n_parts]
        w_in_ref, w_out_ref, out_ref, up, down, up_sem, down_sem = refs[n_parts:]

        def up_copy(k):
            return pltpu.make_async_copy(
                w_in_ref.at[layer, :, pl.ds(k * chunk, chunk)], up.at[k], up_sem.at[k]
            )

        def down_copy(k):
            return pltpu.make_async_copy(
                w_out_ref.at[layer, pl.ds(k * chunk, chunk)], down.at[k], down_sem.at[k]
            )

        for k in range(chunks):
            up_copy(k).start()
            down_copy(k).start()
        pre = state_ref[...].astype(jnp.float32)
        for part in part_refs:
            pre = pre + part[...].astype(jnp.float32)
        scale = lax.rsqrt(jnp.mean(pre * pre, axis=-1, keepdims=True) + epsilon)
        normed = (pre * scale * scale_ref[...] + shift_ref[...].astype(jnp.float32)).astype(
            jnp.bfloat16
        )
        total = pre
        for k in range(chunks):
            up_copy(k).wait()
            inner = jnp.dot(normed, up[k], preferred_element_type=jnp.float32)
            hidden = (inner / (1.0 + jnp.exp(-inner))).astype(jnp.bfloat16)
            down_copy(k).wait()
            total = total + jnp.dot(hidden, down[k], preferred_element_type=jnp.float32)
        out_ref[...] = total.astype(out_ref.dtype)

    vmem = pl.BlockSpec(memory_space=pltpu.VMEM)
    hbm = pl.BlockSpec(memory_space=pl.ANY)
    return pl.pallas_call(
        body,
        in_specs=[vmem] * (3 + n_parts) + [hbm] * 2,
        out_specs=vmem,
        out_shape=jax.ShapeDtypeStruct((rows, width), jnp.bfloat16),
        scratch_shapes=[
            pltpu.VMEM((chunks, width, chunk), jnp.bfloat16),
            pltpu.VMEM((chunks, chunk, width), jnp.bfloat16),
            pltpu.SemaphoreType.DMA((chunks,)),
            pltpu.SemaphoreType.DMA((chunks,)),
        ],
        compiler_params=pltpu.CompilerParams(vmem_limit_bytes=VMEM_LIMIT),
        name="node_mlp",
    )(state, scale_rows, shift_rows, *parts, w_in, w_out)


def local(
    features,
    tile_values,
    slot_refs,
    wanted,
    time_ids,
    cond_ids,
    time_table,
    cond_table,
    gains,
    w_in,
    w_out,
):
    row_count = lax.axis_size("row")
    col_count = lax.axis_size("col")
    span, width = features.shape
    tile = tile_values.shape[-1]
    slots = tile_values.shape[3]
    row_tiles = tile_values.shape[0]
    refer = wanted.shape[-1]
    matrix = tile_values.reshape(row_tiles, tile, slots * tile)
    slot_index = slot_refs.reshape(-1)
    peers = jnp.arange(row_count, dtype=jnp.int32)[:, None]
    source_row = (peers * span + wanted.reshape(row_count, refer) * tile).reshape(-1)
    source_slot = jnp.arange(row_count * refer, dtype=jnp.int32)
    order = jnp.arange(col_count, dtype=jnp.int32)
    scale_rows = gains[:, None, :] * (1.0 + lookup(cond_ids, cond_table))[None]
    shift_rows = lookup(time_ids, time_table).astype(jnp.bfloat16)
    state = features
    for layer in range(LAYERS):
        column = lax.all_gather(state, "row", axis=0, tiled=True)
        (product,) = aggregate_tiles(matrix, [column], source_row, source_slot, slot_index, order, False)
        aggregate = lax.psum_scatter(product, "col", scatter_dimension=0, tiled=True)
        state = node_mlp(layer, state, [aggregate], scale_rows[layer], shift_rows, w_in, w_out)
    return state


def solution(mesh):
    return jax.shard_map(
        local,
        mesh=mesh,
        in_specs=(
            P(("row", "col"), None),
            P("row", "col", None, None, None),
            P("row", "col", None),
            P("row", "col", None, None),
            P(("row", "col")),
            P(("row", "col")),
            P(),
            P(),
            P(),
            P(),
            P(),
        ),
        out_specs=P(("row", "col"), None),
        check_vma=False,
    )
```

time: 299 us -> 267 us (0.89)
  waiting for transfers between devices: 226 us -> 198 us
  Pallas kernels: 0 us -> 27.4 us
  matrix products: 23.6 us -> 0.53 us
  local copies, waits for them, and re-layouts: 32 us -> 24 us
    reduce_scatter x2, waiting for transfers between devices: 108 us -> 73.8 us  [local(): lax.psum_scatter(product, 'col', scatter_dimension=0, tiled=True)]
    gather x4 -> x0, local copies, waits for them, and re-layouts: 27.7 us -> none  [the longest x2 15.4 us: local(): right = source[slot_index.reshape(-1)].reshape(number, slots * tile, width)]
    pallas_call x0 -> x4, Pallas kernels: none -> 27.4 us  [the longest x2 18.8 us: aggregate_tiles(): pl.pallas_call(body, in_specs=[smem] * 4 + [hbm] * (1 + n_src), out_specs...]
    dot_general x4 -> x0, matrix products: 22.4 us -> none  [the longest x2 13.2 us: local(): jnp.einsum('tik,tkf->tif', matrix, right, preferred_element_type=jnp.floa...]
    unnamed x15 -> x37, local copies, waits for them, and re-layouts: 1.42 us -> 21.1 us
    all_gather x2, waiting for transfers between devices: 118 us -> 123 us  [local(): column = lax.all_gather(state, 'row', axis=0, tiled=True)]
  transfers between devices with their start and end apart: 4 -> 4, of which waited for: 4 -> 4; matrix products, arithmetic and copies ran while one was open for 2% -> 1% of each run, Pallas kernels for 0% -> 0%
where the time goes in v1:
time: 267 us; the launch traced here: 263 us
  waiting for transfers between devices  198 us (74%)
  Pallas kernels  27.4 us (10%)
  local copies, waits for them, and re-layouts  24 us (9%)
  between operations  13.3 us (5%)
    all_gather x2, waiting for transfers between devices, local(): column = lax.all_gather(state, 'row', axis=0, tiled=True)  123 us
    reduce_scatter x2, waiting for transfers between devices, local(): lax.psum_scatter(product, 'col', scatter_dimension=0, tiled=True)  73.8 us
    unnamed x37, local copies, waits for them, and re-layouts  21.1 us
    pallas_call x2, Pallas kernels, aggregate_tiles(): pl.pallas_call(body, in_specs=[smem] * 4 + [hbm] * (1 + n_src), out_specs...  18.8 us
    pallas_call x2, Pallas kernels, node_mlp(): pl.pallas_call(body, in_specs=[vmem] * (3 + n_parts) + [hbm] * 2, out_spe...  8.64 us
  transfers between devices with their start and end apart: 4, of which 4 were waited for; matrix products, arithmetic and copies ran while one was open for 1% of the time, Pallas kernels for 0%

profile of v1, /device:TPU:1, one launch (start us, length us, event | category | flops | bytes accessed | tf_op | source)
XLA Modules:
  0.0 263.4 jit_solution(14641433357668195147)
XLA Ops:
  6.5 0.0 copy-start
  6.5 0.0 copy-start.14
  6.5 0.0 copy-start.17
  6.5 0.0 all-gather.3.cloned.1.call-start
  6.5 0.7 all-gather.3.cloned.1.call-update
  7.3 0.0 reduce-scatter.3.cloned.1.call-start
  7.3 2.7 %reshape.23.matrix_ref = bf16[16,128,512]{2,1,0:T(8,128)(2,1)S(1)} reshape(bf16[16,1,128,4,128]{4,3,2,1,0:T(4,128)(2,1)} %param.12) | data formatting | bytes 4194304 | tf_op jit(solution)/shard_map/reshape | solution.py:168
  10.1 0.0 copy-done.14
  10.1 0.1 copy.13
  10.2 0.1 reshape.22.index_ref
  10.2 0.0 copy-done.17
  10.3 61.8 %all-gather.3.cloned.1.call-done.refs_0_ = bf16[8192,512]{1,0:T(8,128)(2,1)} async-done(((bf16[256,512]{1,0:T(8,128)(2,1)}), bf16[8192,512]{1,0:T(8,128)(2,1)}) %all-gather.3.cloned.1.call-update) | async-done | bytes 8388624 | tf_op jit(solution)/shard_map/all_gather | solution.py:178
  72.1 0.0 copy-start.5
  72.1 3.4 %copy-done.5 = bf16[8192,512]{1,0:T(8,128)(2,1)S(1)} copy-done((bf16[8192,512]{1,0:T(8,128)(2,1)S(1)}, bf16[8192,512]{1,0:T(8,128)(2,1)}, u32[]{:S(2)}) %copy-start.5) | copy-done | bytes 8388632
  75.5 0.0 copy-start.15
  75.5 0.0 copy-start.12
  75.5 0.0 copy-start.16
  75.5 0.0 copy-start.13
  75.5 9.4 %aggregate_tiles.2 = bf16[2048,512]{1,0:T(8,128)(2,1)S(1)} custom-call(s32[32]{0:T(128)S(1)} %bitcast_add_fusion.row_ref, s32[32]{0:T(128)S(1)} %iota.24.slot_ref, s32[64]{0:T(128)S(1)} %reshape.22.index_ref, s32[8]{0:T(128)S(1)} %iota.25.order_ref, bf16[16,128,512]{2,1,0:T(8,128)(2,1)S(1)} %reshape.23.matrix_ref, bf16[8192,512]{1,0:T(8,128)(2,1)S(1)} %copy-done.5), custom_call_target="tpu_custom_call" | custom-call | tf_op jit(solution)/shard_map/aggregate_tiles/pallas_call | solution.py:72
  84.9 0.0 copy-start.7
  84.9 1.3 copy-done.7
  86.2 0.0 reduce-scatter.3.cloned.1.call-update
  86.2 0.0 all-gather.5.cloned.1.call-start
  86.3 0.0 copy-done
  86.3 0.0 copy-done.15
  86.3 0.3 convolution_convert_fusion.shift_ref
  86.6 0.0 copy-done.12
  86.6 0.0 copy-done.16
  86.6 0.3 convolution_add_fusion
  86.9 0.0 copy-done.13
  86.9 0.1 broadcast_multiply_fusion
  87.0 0.1 slice_bitcast_fusion
  87.1 36.5 %reduce-scatter.3.cloned.1.call-done.refs_0_ = bf16[256,512]{1,0:T(8,128)(2,1)} async-done(((bf16[2048,512]{1,0:T(8,128)(2,1)}), bf16[256,512]{1,0:T(8,128)(2,1)}) %reduce-scatter.3.cloned.1.call-update) | async-done | bytes 262160 | tf_op jit(solution)/shard_map/reduce_scatter | solution.py:180
  123.6 0.0 copy-start.1
  123.6 2.2 copy-done.1
  125.8 0.0 copy-start.3
  125.8 2.2 copy-done.3
  127.9 0.0 copy-start.9
  128.0 0.9 copy-done.9
  128.9 0.0 copy-start.10
  128.9 0.9 copy-done.10
  129.8 3.8 %node_mlp.2.state_ref = bf16[256,512]{1,0:T(8,128)(2,1)} custom-call(bf16[256,512]{1,0:T(8,128)(2,1)S(1)} %copy-done.9, f32[256,512]{1,0:T(8,128)S(1)} %get-tuple-element.6.scale_ref, bf16[256,512]{1,0:T(8,128)(2,1)S(1)} %convolution_convert_fusion.shift_ref, bf16[256,512]{1,0:T(8,128)(2,1)S(1)} %copy-done.10, bf16[2,512,2048]{2,1,0:T(8,128)(2,1)S(1)} %copy-done.1, ...), custom_call_target="tpu_custom_call" | custom-call | tf_op jit(solution)/shard_map/node_mlp/pallas_call | solution.py:132
  133.7 0.0 all-gather.5.cloned.1.call-update
  133.7 0.0 reduce-scatter.5.cloned.1.call-start
  133.8 61.5 %all-gather.5.cloned.1.call-done.refs_0_ = bf16[8192,512]{1,0:T(8,128)(2,1)} async-done(((bf16[256,512]{1,0:T(8,128)(2,1)}), bf16[8192,512]{1,0:T(8,128)(2,1)}) %all-gather.5.cloned.1.call-update) | async-done | bytes 8388624 | tf_op jit(solution)/shard_map/all_gather | solution.py:178
  195.2 0.0 copy-start.6
  195.3 3.4 %copy-done.6 = bf16[8192,512]{1,0:T(8,128)(2,1)S(1)} copy-done((bf16[8192,512]{1,0:T(8,128)(2,1)S(1)}, bf16[8192,512]{1,0:T(8,128)(2,1)}, u32[]{:S(2)}) %copy-start.6) | copy-done | bytes 8388632
  198.6 9.4 %aggregate_tiles.3 = bf16[2048,512]{1,0:T(8,128)(2,1)S(1)} custom-call(s32[32]{0:T(128)S(1)} %bitcast_add_fusion.row_ref, s32[32]{0:T(128)S(1)} %iota.26.slot_ref, s32[64]{0:T(128)S(1)} %reshape.22.index_ref, s32[8]{0:T(128)S(1)} %iota.27.order_ref, bf16[16,128,512]{2,1,0:T(8,128)(2,1)S(1)} %reshape.23.matrix_ref, bf16[8192,512]{1,0:T(8,128)(2,1)S(1)} %copy-done.6), custom_call_target="tpu_custom_call" | custom-call | tf_op jit(solution)/shard_map/aggregate_tiles/pallas_call | solution.py:72
  208.0 0.0 copy-start.8
  208.0 1.3 copy-done.8
  209.4 0.0 reduce-scatter.5.cloned.1.call-update
  209.4 37.4 %reduce-scatter.5.cloned.1.call-done.refs_0_ = bf16[256,512]{1,0:T(8,128)(2,1)} async-done(((bf16[2048,512]{1,0:T(8,128)(2,1)}), bf16[256,512]{1,0:T(8,128)(2,1)}) %reduce-scatter.5.cloned.1.call-update) | async-done | bytes 262160 | tf_op jit(solution)/shard_map/reduce_scatter | solution.py:180
  246.8 0.0 copy-start.2
  246.8 2.2 copy-done.2
  249.0 0.0 copy-start.4
  249.0 2.2 copy-done.4
  251.2 0.0 copy-start.11
  251.2 0.9 copy-done.11
  252.1 4.8 %node_mlp.3 = bf16[256,512]{1,0:T(8,128)(2,1)} custom-call(bf16[256,512]{1,0:T(8,128)(2,1)} %node_mlp.2.state_ref, f32[256,512]{1,0:T(8,128)S(1)} %get-tuple-element.5.scale_ref, bf16[256,512]{1,0:T(8,128)(2,1)S(1)} %convolution_convert_fusion.shift_ref, bf16[256,512]{1,0:T(8,128)(2,1)S(1)} %copy-done.11, bf16[2,512,2048]{2,1,0:T(8,128)(2,1)S(1)} %copy-done.2, ...), custom_call_target="tpu_custom_call" | custom-call | tf_op jit(solution)/shard_map/node_mlp/pallas_call | solution.py:132
  (5 shorter events, 0.0 us)
Async XLA Ops:
  6.5 79.8 %copy-start = (bf16[128,512]{1,0:T(8,128)(2,1)S(1)}, bf16[128,512]{1,0:T(8,128)(2,1)}, u32[]{:S(2)}) copy-start(bf16[128,512]{1,0:T(8,128)(2,1)} %param.17) | copy-start | bytes 393220
  6.5 3.5 %copy-start.14 = (s32[16,1,4]{0,2,1:T(4,128)S(1)}, s32[16,1,4]{0,2,1:T(4,128)}, u32[]{:S(2)}) copy-start(s32[16,1,4]{0,2,1:T(4,128)} %param.13) | copy-start | bytes 772
  6.5 3.7 %copy-start.17 = (s32[1,1,32,1]{2,3,1,0:T(1,128)S(1)}, s32[1,1,32,1]{2,3,1,0:T(1,128)}, u32[]{:S(2)}) copy-start(s32[1,1,32,1]{2,3,1,0:T(1,128)} %param.14) | copy-start | bytes 388
  6.5 65.5 %all-gather.3.cloned.1.call-start = ((), (), s32[]{:S(2)}) async-start(), calls=%async_computation.2 | async-start | bytes 8650752 | tf_op jit(solution)/shard_map/all_gather | solution.py:178
  7.3 116.3 %reduce-scatter.3.cloned.1.call-start = ((), (), s32[]{:S(2)}) async-start(), calls=%async_computation.3 | async-start | bytes 2359296 | tf_op jit(solution)/shard_map/reduce_scatter | solution.py:180
  72.1 3.4 %copy-start.5 = (bf16[8192,512]{1,0:T(8,128)(2,1)S(1)}, bf16[8192,512]{1,0:T(8,128)(2,1)}, u32[]{:S(2)}) copy-start(bf16[8192,512]{1,0:T(8,128)(2,1)} %all-gather.3.cloned.1.call-done.refs_0_) | copy-start | bytes 25165828
  75.5 10.8 %copy-start.15 = (s32[256]{0:T(256)S(1)}, s32[256]{0:T(256)}, u32[]{:S(2)}) copy-start(s32[256]{0:T(256)} %param.15) | copy-start | bytes 3076
  75.5 11.1 %copy-start.12 = (bf16[16,512]{1,0:T(8,128)(2,1)S(1)}, bf16[16,512]{1,0:T(8,128)(2,1)}, u32[]{:S(2)}) copy-start(bf16[16,512]{1,0:T(8,128)(2,1)} %param.18) | copy-start | bytes 49156
  75.5 11.1 %copy-start.16 = (s32[256]{0:T(256)S(1)}, s32[256]{0:T(256)}, u32[]{:S(2)}) copy-start(s32[256]{0:T(256)} %param.16) | copy-start | bytes 3076
  75.5 11.4 %copy-start.13 = (f32[2,512]{1,0:T(2,128)S(1)}, f32[2,512]{1,0:T(2,128)}, u32[]{:S(2)}) copy-start(f32[2,512]{1,0:T(2,128)} %param.19) | copy-start | bytes 12292
  84.9 1.3 copy-start.7
  86.2 109.0 %all-gather.5.cloned.1.call-start = ((), (), s32[]{:S(2)}) async-start(), calls=%async_computation.4 | async-start | bytes 8650752 | tf_op jit(solution)/shard_map/all_gather | solution.py:178
  123.6 2.2 copy-start.1
  125.8 2.2 copy-start.3
  127.9 0.9 copy-start.9
  128.9 0.9 copy-start.10
  133.7 113.0 %reduce-scatter.5.cloned.1.call-start = ((), (), s32[]{:S(2)}) async-start(), calls=%async_computation.5 | async-start | bytes 2359296 | tf_op jit(solution)/shard_map/reduce_scatter | solution.py:180
  195.2 3.4 %copy-start.6 = (bf16[8192,512]{1,0:T(8,128)(2,1)S(1)}, bf16[8192,512]{1,0:T(8,128)(2,1)}, u32[]{:S(2)}) copy-start(bf16[8192,512]{1,0:T(8,128)(2,1)} %all-gather.5.cloned.1.call-done.refs_0_) | copy-start | bytes 25165828
  208.0 1.3 copy-start.8
  246.8 2.2 copy-start.2
  249.0 2.2 copy-start.4
  251.2 0.9 copy-start.11
Sparse Core Ops, SparseCore 0:
  9.9 62.1 all-gather.2
  86.4 37.1 reduce-scatter.2
  133.9 61.3 all-gather.4
  209.5 37.2 reduce-scatter.4

commit v2 on v0

v2 whole, which is shorter than its diff:
```python
import jax
import jax.numpy as jnp
from jax import lax
from jax.experimental import pallas as pl
from jax.experimental.pallas import tpu as pltpu
from jax.sharding import PartitionSpec as P

LAYERS = 2
PIECES = 1
VMEM_LIMIT = 22 * 1024 * 1024

epsilon = 1e-06


def lookup(ids, table):
    onehot = (ids[:, None] == jnp.arange(table.shape[0], dtype=jnp.int32)[None, :]).astype(
        jnp.bfloat16
    )
    return jnp.dot(onehot, table, preferred_element_type=jnp.float32)


def aggregate_tiles(matrix, sources, source_of, source_row, source_slot, slot_index, order):
    row_tiles, tile, depth = matrix.shape
    slots = depth // tile
    width = sources[0].shape[-1]
    gathered = source_row.shape[0]
    blocks = order.shape[0]
    per_block = row_tiles // blocks
    n_src = len(sources)
    rows = per_block * tile

    def body(row_ref, slot_ref, index_ref, order_ref, matrix_ref, *refs):
        src = refs[:n_src]
        outs = refs[n_src : n_src + blocks]
        (tiles,) = refs[n_src + blocks :]
        for b in range(gathered):
            start = pl.multiple_of(row_ref[b], tile)
            tiles[slot_ref[b]] = src[source_of[b]][pl.ds(start, tile), :]
        for k in range(blocks):
            for j in range(per_block):
                t = order_ref[k] * per_block + j
                right = jnp.concatenate(
                    [tiles[index_ref[t * slots + s]] for s in range(slots)], axis=0
                )
                value = jnp.dot(matrix_ref[t], right, preferred_element_type=jnp.float32)
                outs[k][j * tile : (j + 1) * tile, :] = value.astype(jnp.bfloat16)

    smem = pl.BlockSpec(memory_space=pltpu.SMEM)
    vmem = pl.BlockSpec(memory_space=pltpu.VMEM)
    return pl.pallas_call(
        body,
        in_specs=[smem] * 4 + [vmem] * (1 + n_src),
        out_specs=[vmem] * blocks,
        out_shape=[jax.ShapeDtypeStruct((rows, width), jnp.bfloat16)] * blocks,
        scratch_shapes=[pltpu.VMEM((gathered, tile, width), jnp.bfloat16)],
        compiler_params=pltpu.CompilerParams(vmem_limit_bytes=VMEM_LIMIT),
        name="aggregate_tiles",
    )(source_row, source_slot, slot_index, order, matrix, *sources)


def node_mlp(layer, states, parts, scale_rows, shift_rows, w_in, w_out, pieces):
    rows = states[0].shape[0]
    width = w_out.shape[-1]
    hidden_units = w_in.shape[-1]
    chunks = 4
    chunk = hidden_units // chunks
    given = [[state, *addends] for state, addends in zip(states, parts, strict=True)]
    flat = [value for group in given for value in group]

    def body(scale_ref, shift_ref, w_in_ref, w_out_ref, *refs):
        inputs, outs = list(refs[: len(flat)]), refs[len(flat) :]
        sums = []
        for group in given:
            total = inputs.pop(0)[...].astype(jnp.float32)
            for _ in group[1:]:
                total = total + inputs.pop(0)[...].astype(jnp.float32)
            sums.append(total)
        pre = jnp.concatenate(sums, axis=1)
        scale = lax.rsqrt(jnp.mean(pre * pre, axis=-1, keepdims=True) + epsilon)
        normed = (
            pre * scale * scale_ref[layer] + shift_ref[...].astype(jnp.float32)
        ).astype(jnp.bfloat16)
        total = pre
        for k in range(chunks):
            units = pl.ds(k * chunk, chunk)
            inner = jnp.dot(
                normed, w_in_ref[layer, :, units], preferred_element_type=jnp.float32
            )
            hidden = (0.5 * inner * (1.0 + jnp.tanh(0.5 * inner))).astype(jnp.bfloat16)
            total = total + jnp.dot(
                hidden, w_out_ref[layer, units, :], preferred_element_type=jnp.float32
            )
        piece = width // pieces
        for p in range(pieces):
            outs[p][...] = total[:, p * piece : (p + 1) * piece].astype(jnp.bfloat16)

    vmem = pl.BlockSpec(memory_space=pltpu.VMEM)
    return pl.pallas_call(
        body,
        in_specs=[vmem] * (4 + len(flat)),
        out_specs=[vmem] * pieces,
        out_shape=[jax.ShapeDtypeStruct((rows, width // pieces), jnp.bfloat16)] * pieces,
        compiler_params=pltpu.CompilerParams(vmem_limit_bytes=VMEM_LIMIT),
        name="node_mlp",
    )(scale_rows, shift_rows, w_in, w_out, *flat)


SIDE = 4
NEAR = (1, -1, 2)


def held_blocks():
    offsets = [[(e, d) for e in (0, *NEAR)] for d in (0, *NEAR)]
    count = len(offsets)
    return [
        (a + swapped * count, k, e, d, swapped)
        for swapped in (0, 1)
        for a, held in enumerate(offsets)
        for k, (e, d) in enumerate(held)
    ]


BLOCKS = held_blocks()


def place(x, y, core):
    return ((x % SIDE) * SIDE + y % SIDE) * 2 + core


def pull(value, first, distance):
    pairs = []
    for x in range(SIDE):
        for y in range(SIDE):
            for core in range(2):
                step = (distance, 0) if (core == 0) == first else (0, distance)
                pairs.append((place(x + step[0], y + step[1], core), place(x, y, core)))
    return lax.ppermute(value, "row", pairs)


def swap(value):
    count = 2 * SIDE * SIDE
    return lax.ppermute(value, "row", [(i, i ^ 1) for i in range(count)])


def gather_blocks(own):
    line = jnp.concatenate([own] + [pull(own, True, e) for e in NEAR], axis=0)
    arrays = [line] + [pull(line, False, d) for d in NEAR]
    return arrays + [swap(v) for v in arrays]


def send(value, distance):
    count = lax.axis_size("col")
    return lax.ppermute(value, "col", [(i, (i + distance) % count) for i in range(count)])


def sum_columns(near, own):
    half = own.shape[0] // 2
    far_up = send(near[4][:half], 2)
    far_down = send(near[4][half:], -2)
    up = send(near[3], 1)
    down = send(near[5], -1)
    next_up = send(near[1], 1)
    next_down = send(near[7], -1)
    f32 = jnp.float32
    relay_up = near[2].astype(f32) + up.astype(f32)
    relay_up = jnp.concatenate([relay_up[:half] + far_up.astype(f32), relay_up[half:]], axis=0)
    relay_down = near[6].astype(f32) + down.astype(f32)
    relay_down = jnp.concatenate(
        [relay_down[:half], relay_down[half:] + far_down.astype(f32)], axis=0
    )
    last_up = send(relay_up.astype(jnp.bfloat16), 2)
    last_down = send(relay_down.astype(jnp.bfloat16), -2)
    return [own, next_up, next_down, last_up, last_down]


def local(
    features,
    tile_values,
    slot_refs,
    wanted,
    time_ids,
    cond_ids,
    time_table,
    cond_table,
    gains,
    w_in,
    w_out,
):
    col_count = lax.axis_size("col")
    span = features.shape[0]
    tile = tile_values.shape[-1]
    slots = tile_values.shape[3]
    row_tiles = tile_values.shape[0]
    matrix = tile_values.reshape(row_tiles, tile, slots * tile)
    slot_index = slot_refs.reshape(-1)
    row = lax.axis_index("row")
    x, y, core = row // (2 * SIDE), row // 2 % SIDE, row % 2
    order = (lax.axis_index("col") + jnp.arange(col_count, dtype=jnp.int32)) % col_count
    scale_rows = gains[:, None, :] * (1.0 + lookup(cond_ids, cond_table))[None]
    shift_rows = lookup(time_ids, time_table).astype(jnp.bfloat16)
    table = jnp.array(BLOCKS, dtype=jnp.int32)
    base, first, second, held = table[:, 1] * span, table[:, 2], table[:, 3], core ^ table[:, 4]
    source_slot = jnp.where(
        held == 0, place(x + first, y + second, 0), place(x + second, y + first, 1)
    )
    source_row = base + wanted.reshape(-1)[source_slot] * tile
    piece = features.shape[1] // PIECES
    states = [features[:, p * piece : (p + 1) * piece] for p in range(PIECES)]
    for layer in range(LAYERS):
        parts = []
        for state in states:
            near = aggregate_tiles(
                matrix,
                gather_blocks(state),
                [b[0] for b in BLOCKS],
                source_row,
                source_slot,
                slot_index,
                order,
            )
            parts.append(sum_columns(near, near[0]))
        last = layer == LAYERS - 1
        states = node_mlp(
            layer,
            states,
            parts,
            scale_rows,
            shift_rows,
            w_in,
            w_out,
            1 if last else PIECES,
        )
    return states[0]


def solution(mesh):
    return jax.shard_map(
        local,
        mesh=mesh,
        in_specs=(
            P(("row", "col"), None),
            P("row", "col", None, None, None),
            P("row", "col", None),
            P("row", "col", None, None),
            P(("row", "col")),
            P(("row", "col")),
            P(),
            P(),
            P(),
            P(),
            P(),
        ),
        out_specs=P(("row", "col"), None),
        check_vma=False,
    )
```

time: 299 us -> 184 us (0.62)
  the two profiles are of different devices: /device:TPU:1 before, /device:TPU:98 now
where the time goes in v2:
time: 184 us
  waiting for transfers between devices  108 us (59%)
  starting transfers between devices  57.4 us (31%)
  Pallas kernels  11.6 us (6%)
  local copies, waits for them, and re-layouts  4.9 us (3%)
    ppermute x12, waiting for transfers between devices, pull(): return lax.ppermute(value, 'row', pairs)  54.6 us
    ppermute x16, waiting for transfers between devices, send(): lax.ppermute(value, 'col', [(i, (i + distance) % count) for i in range(co...  50.5 us
    ppermute x12, starting transfers between devices, pull(): return lax.ppermute(value, 'row', pairs)  31.7 us
    ppermute x16, starting transfers between devices, send(): lax.ppermute(value, 'col', [(i, (i + distance) % count) for i in range(co...  24.2 us
    pallas_call x2, Pallas kernels, aggregate_tiles(): pl.pallas_call(body, in_specs=[smem] * 4 + [vmem] * (1 + n_src), out_spec...  7.01 us
    pallas_call x2, Pallas kernels, node_mlp(): pl.pallas_call(body, in_specs=[vmem] * (4 + len(flat)), out_specs=[vmem]...  4.62 us
  transfers between devices with their start and end apart: 36, of which 23 were waited for; matrix products, arithmetic and copies ran while one was open for 3% of the time, Pallas kernels for 0%

profile of v2, /device:TPU:98, one launch (start us, length us, event | category | flops | bytes accessed | tf_op | source)
XLA Modules:
  0.0 183.5 jit_solution(6440883432158548639)
XLA Ops:
  0.0 0.5 collective-permute-start
  0.5 1.5 collective-permute-start.1
  2.0 3.3 %collective-permute-start.2 = (bf16[256,512]{1,0:T(8,128)(2,1)}, bf16[256,512]{1,0:T(8,128)(2,1)S(1)}, u32[]{:S(2)}, u32[]{:S(2)}) collective-permute-start(bf16[256,512]{1,0:T(8,128)(2,1)} %refs_0_.1), channel_id=1, source_target_pairs={{128,0},{40,8},{144,16},{56,24},{160,32},{8,40},{176,48},{24,56},{... | collective-permute-start | bytes 786440 | tf_op jit(solution)/shard_map/ppermute | solution.py:137
  5.4 1.0 constant_dynamic-update-slice_fusion.3
  6.4 0.2 collective-permute-done
  6.6 1.3 collective-permute-done.1
  7.9 2.4 %collective-permute-done.2 = bf16[256,512]{1,0:T(8,128)(2,1)S(1)} collective-permute-done((bf16[256,512]{1,0:T(8,128)(2,1)}, bf16[256,512]{1,0:T(8,128)(2,1)S(1)}, u32[]{:S(2)}, u32[]{:S(2)}) %collective-permute-start.2) | collective-permute-done | bytes 262176 | tf_op jit(solution)/shard_map/ppermute | solution.py:137
  10.3 3.3 %collective-permute-start.5 = (bf16[1024,512]{1,0:T(8,128)(2,1)S(1)}, bf16[1024,512]{1,0:T(8,128)(2,1)}, u32[]{:S(2)}, u32[]{:S(2)}) collective-permute-start(bf16[1024,512]{1,0:T(8,128)(2,1)S(1)} %constant_dynamic-update-slice_fusion.refs_0_), channel_id=1, source_target_pairs={{32,0},{136,8},{48,16},{152,24},{0,32},{168,40},{16,48},{184,56},{... | collective-permute-start | bytes 3145736 | tf_op jit(solution)/shard_map/ppermute | solution.py:137
  13.6 0.7 collective-permute-start.4
  14.3 2.6 %collective-permute-start.3 = (bf16[1024,512]{1,0:T(8,128)(2,1)S(1)}, bf16[1024,512]{1,0:T(8,128)(2,1)}, u32[]{:S(2)}, u32[]{:S(2)}) collective-permute-start(bf16[1024,512]{1,0:T(8,128)(2,1)S(1)} %constant_dynamic-update-slice_fusion.refs_0_), channel_id=1, source_target_pairs={{16,0},{72,8},{32,16},{88,24},{48,32},{104,40},{0,48},{120,56},{80... | collective-permute-start | bytes 3145736 | tf_op jit(solution)/shard_map/ppermute | solution.py:137
  16.9 10.1 %collective-permute-done.5.refs_3_ = bf16[1024,512]{1,0:T(8,128)(2,1)} collective-permute-done((bf16[1024,512]{1,0:T(8,128)(2,1)S(1)}, bf16[1024,512]{1,0:T(8,128)(2,1)}, u32[]{:S(2)}, u32[]{:S(2)}) %collective-permute-start.5) | collective-permute-done | bytes 1048608 | tf_op jit(solution)/shard_map/ppermute | solution.py:137
  26.9 0.8 collective-permute-start.9
  27.8 10.3 %collective-permute-done.4.refs_2_ = bf16[1024,512]{1,0:T(8,128)(2,1)} collective-permute-done((bf16[1024,512]{1,0:T(8,128)(2,1)S(1)}, bf16[1024,512]{1,0:T(8,128)(2,1)}, u32[]{:S(2)}, u32[]{:S(2)}) %collective-permute-start.4) | collective-permute-done | bytes 1048608 | tf_op jit(solution)/shard_map/ppermute | solution.py:137
  38.1 0.7 collective-permute-start.8
  38.8 0.1 copy.14
  38.8 0.1 reshape.28.index_ref
  39.0 2.8 %reshape.29.matrix_ref = bf16[16,128,512]{2,1,0:T(8,128)(2,1)S(1)} reshape(bf16[16,1,128,4,128]{4,3,2,1,0:T(4,128)(2,1)} %param.13) | data formatting | bytes 4194304 | tf_op jit(solution)/shard_map/reshape | solution.py:194
  41.9 0.7 gather_fusion
  42.7 0.3 convolution_add_fusion
  43.0 4.9 %aggregate_tiles.2 = (bf16[256,512]{1,0:T(8,128)(2,1)S(1)}, bf16[256,512]{1,0:T(8,128)(2,1)S(1)}, bf16[256,512]{1,0:T(8,128)(2,1)S(1)}, bf16[256,512]{1,0:T(8,12...) custom-call(s32[32]{0:T(128)S(1)} %get-tuple-element.42.row_ref, ...), custom_call_target="tpu_custom_call" | custom-call | tf_op jit(solution)/shard_map/aggregate_tiles/pallas_call | solution.py:50
  47.9 3.2 %collective-permute-start.12 = (bf16[256,512]{1,0:T(8,128)(2,1)S(1)}, bf16[256,512]{1,0:T(8,128)(2,1)S(1)}, u32[]{:S(2)}, u32[]{:S(2)}) collective-permute-start(bf16[256,512]{1,0:T(8,128)(2,1)S(1)} %get-tuple-element.25), channel_id=1, source_target_pairs={{0,1},{1,2},{2,3},{3,4},{4,5},{5,6},{6,7},{7,0},{8,9},{9,10},{10,1... | collective-permute-start | bytes 786440 | tf_op jit(solution)/shard_map/ppermute | solution.py:153
  51.1 0.3 convolution_convert_fusion.shift_ref
  51.4 0.1 collective-permute-start.16
  51.5 4.1 %collective-permute-start.13 = (bf16[128,512]{1,0:T(8,128)(2,1)S(1)}, bf16[128,512]{1,0:T(8,128)(2,1)S(1)}, u32[]{:S(2)}, u32[]{:S(2)}) collective-permute-start(bf16[128,512]{1,0:T(8,128)(2,1)S(1)} %get-tuple-element.40), channel_id=1, source_target_pairs={{0,2},{1,3},{2,4},{3,5},{4,6},{5,7},{6,0},{7,1},{8,10},{9,11},{10,... | collective-permute-start | bytes 393224 | tf_op jit(solution)/shard_map/ppermute | solution.py:153
  55.6 2.0 %collective-permute-start.11 = (bf16[256,512]{1,0:T(8,128)(2,1)S(1)}, bf16[256,512]{1,0:T(8,128)(2,1)S(1)}, u32[]{:S(2)}, u32[]{:S(2)}) collective-permute-start(bf16[256,512]{1,0:T(8,128)(2,1)S(1)} %get-tuple-element.23), channel_id=1, source_target_pairs={{0,7},{1,0},{2,1},{3,2},{4,3},{5,4},{6,5},{7,6},{8,15},{9,8},{10,9... | collective-permute-start | bytes 786440 | tf_op jit(solution)/shard_map/ppermute | solution.py:153
  57.6 2.5 %collective-permute-done.12 = bf16[256,512]{1,0:T(8,128)(2,1)S(1)} collective-permute-done((bf16[256,512]{1,0:T(8,128)(2,1)S(1)}, bf16[256,512]{1,0:T(8,128)(2,1)S(1)}, u32[]{:S(2)}, u32[]{:S(2)}) %collective-permute-start.12) | collective-permute-done | bytes 262176 | tf_op jit(solution)/shard_map/ppermute | solution.py:153
  60.2 3.1 %collective-permute-done.13 = bf16[128,512]{1,0:T(8,128)(2,1)S(1)} collective-permute-done((bf16[128,512]{1,0:T(8,128)(2,1)S(1)}, bf16[128,512]{1,0:T(8,128)(2,1)S(1)}, u32[]{:S(2)}, u32[]{:S(2)}) %collective-permute-start.13) | collective-permute-done | bytes 131104 | tf_op jit(solution)/shard_map/ppermute | solution.py:153
  63.4 4.7 %collective-permute-start.14 = (bf16[256,512]{1,0:T(8,128)(2,1)S(1)}, bf16[256,512]{1,0:T(8,128)(2,1)S(1)}, u32[]{:S(2)}, u32[]{:S(2)}) collective-permute-start(bf16[256,512]{1,0:T(8,128)(2,1)S(1)} %pad_maximum_fusion.1), channel_id=1, source_target_pairs={{0,2},{1,3},{2,4},{3,5},{4,6},{5,7},{6,0},{7,1},{8,10},{9,11},{10,... | collective-permute-start | bytes 786440 | tf_op jit(solution)/shard_map/ppermute | solution.py:153
  68.1 2.8 %collective-permute-done.15 = bf16[256,512]{1,0:T(8,128)(2,1)S(1)} collective-permute-done((bf16[256,512]{1,0:T(8,128)(2,1)S(1)}, bf16[256,512]{1,0:T(8,128)(2,1)S(1)}, u32[]{:S(2)}, u32[]{:S(2)}) %collective-permute-start.15) | collective-permute-done | bytes 262176 | tf_op jit(solution)/shard_map/ppermute | solution.py:153
  70.9 0.1 convert_add_fusion.2
  71.1 1.3 collective-permute-start.17
  72.4 0.1 broadcast_multiply_fusion.scale_ref
  72.5 1.5 collective-permute-done.10.refs_2_
  74.0 5.8 %collective-permute-done.14.refs_4_ = bf16[256,512]{1,0:T(8,128)(2,1)S(1)} collective-permute-done((bf16[256,512]{1,0:T(8,128)(2,1)S(1)}, bf16[256,512]{1,0:T(8,128)(2,1)S(1)}, u32[]{:S(2)}, u32[]{:S(2)}) %collective-permute-start.14) | collective-permute-done | bytes 262176 | tf_op jit(solution)/shard_map/ppermute | solution.py:153
  79.8 6.3 %collective-permute-done.17.refs_5_ = bf16[256,512]{1,0:T(8,128)(2,1)S(1)} collective-permute-done((bf16[256,512]{1,0:T(8,128)(2,1)S(1)}, bf16[256,512]{1,0:T(8,128)(2,1)S(1)}, u32[]{:S(2)}, u32[]{:S(2)}) %collective-permute-start.17) | collective-permute-done | bytes 262176 | tf_op jit(solution)/shard_map/ppermute | solution.py:153
  86.1 2.0 %node_mlp.2.refs_0_ = bf16[256,512]{1,0:T(8,128)(2,1)S(1)} custom-call(f32[2,256,512]{2,1,0:T(8,128)S(1)} %broadcast_multiply_fusion.scale_ref, bf16[256,512]{1,0:T(8,128)(2,1)S(1)} %convolution_convert_fusion.shift_ref, bf16[2,512,2048]{2,1,0:T(8,128)(2,1)S(1)} %copy-done.1, bf16[2,2048,512]{2,1,0:T(8,128)(2,1)S(1)} %copy-done.2, ...), custom_call_target="tpu_custom_call" | custom-call | tf_op jit(solution)/shard_map/node_mlp/pallas_call | solution.py:98
  88.1 2.9 %collective-permute-start.20 = (bf16[256,512]{1,0:T(8,128)(2,1)S(1)}, bf16[256,512]{1,0:T(8,128)(2,1)S(1)}, u32[]{:S(2)}, u32[]{:S(2)}) collective-permute-start(bf16[256,512]{1,0:T(8,128)(2,1)S(1)} %node_mlp.2.refs_0_), channel_id=1, source_target_pairs={{128,0},{40,8},{144,16},{56,24},{160,32},{8,40},{176,48},{24,56},{... | collective-permute-start | bytes 786440 | tf_op jit(solution)/shard_map/ppermute | solution.py:137
  90.9 2.0 %collective-permute-start.19 = (bf16[256,512]{1,0:T(8,128)(2,1)S(1)}, bf16[256,512]{1,0:T(8,128)(2,1)S(1)}, u32[]{:S(2)}, u32[]{:S(2)}) collective-permute-start(bf16[256,512]{1,0:T(8,128)(2,1)S(1)} %node_mlp.2.refs_0_), channel_id=1, source_target_pairs={{192,0},{56,8},{208,16},{8,24},{224,32},{24,40},{240,48},{40,56},{... | collective-permute-start | bytes 786440 | tf_op jit(solution)/shard_map/ppermute | solution.py:137
  92.9 0.1 collective-permute-start.18
  93.0 3.1 %collective-permute-done.20 = bf16[256,512]{1,0:T(8,128)(2,1)S(1)} collective-permute-done((bf16[256,512]{1,0:T(8,128)(2,1)S(1)}, bf16[256,512]{1,0:T(8,128)(2,1)S(1)}, u32[]{:S(2)}, u32[]{:S(2)}) %collective-permute-start.20) | collective-permute-done | bytes 262176 | tf_op jit(solution)/shard_map/ppermute | solution.py:137
  96.0 2.8 %collective-permute-done.19 = bf16[256,512]{1,0:T(8,128)(2,1)S(1)} collective-permute-done((bf16[256,512]{1,0:T(8,128)(2,1)S(1)}, bf16[256,512]{1,0:T(8,128)(2,1)S(1)}, u32[]{:S(2)}, u32[]{:S(2)}) %collective-permute-start.19) | collective-permute-done | bytes 262176 | tf_op jit(solution)/shard_map/ppermute | solution.py:137
  98.9 0.4 collective-permute-done.18
  99.3 0.1 pad_maximum_fusion.refs_0_
  99.3 1.9 %collective-permute-start.23 = (bf16[1024,512]{1,0:T(8,128)(2,1)S(1)}, bf16[1024,512]{1,0:T(8,128)(2,1)S(1)}, u32[]{:S(2)}, u32[]{:S(2)}) collective-permute-start(bf16[1024,512]{1,0:T(8,128)(2,1)S(1)} %pad_maximum_fusion.refs_0_), channel_id=1, source_target_pairs={{32,0},{136,8},{48,16},{152,24},{0,32},{168,40},{16,48},{184,56},{... | collective-permute-start | bytes 3145736 | tf_op jit(solution)/shard_map/ppermute | solution.py:137
  101.3 13.0 %collective-permute-start.22 = (bf16[1024,512]{1,0:T(8,128)(2,1)S(1)}, bf16[1024,512]{1,0:T(8,128)(2,1)S(1)}, u32[]{:S(2)}, u32[]{:S(2)}) collective-permute-start(bf16[1024,512]{1,0:T(8,128)(2,1)S(1)} %pad_maximum_fusion.refs_0_), channel_id=1, source_target_pairs={{48,0},{200,8},{0,16},{216,24},{16,32},{232,40},{32,48},{248,56},{... | collective-permute-start | bytes 3145736 | tf_op jit(solution)/shard_map/ppermute | solution.py:137
  114.3 1.5 collective-permute-done.23.refs_3_
  115.8 11.2 %collective-permute-done.22.refs_2_ = bf16[1024,512]{1,0:T(8,128)(2,1)S(1)} collective-permute-done((bf16[1024,512]{1,0:T(8,128)(2,1)S(1)}, bf16[1024,512]{1,0:T(8,128)(2,1)S(1)}, u32[]{:S(2)}, u32[]{:S(2)}) %collective-permute-start.22) | collective-permute-done | bytes 1048608 | tf_op jit(solution)/shard_map/ppermute | solution.py:137
  127.0 11.4 %collective-permute-done.21.refs_1_ = bf16[1024,512]{1,0:T(8,128)(2,1)S(1)} collective-permute-done((bf16[1024,512]{1,0:T(8,128)(2,1)S(1)}, bf16[1024,512]{1,0:T(8,128)(2,1)S(1)}, u32[]{:S(2)}, u32[]{:S(2)}) %collective-permute-start.21) | collective-permute-done | bytes 1048608 | tf_op jit(solution)/shard_map/ppermute | solution.py:137
  138.3 2.6 %collective-permute-done.25.refs_5_ = bf16[1024,512]{1,0:T(8,128)(2,1)S(1)} collective-permute-done((bf16[1024,512]{1,0:T(8,128)(2,1)S(1)}, bf16[1024,512]{1,0:T(8,128)(2,1)S(1)}, u32[]{:S(2)}, u32[]{:S(2)}) %collective-permute-start.25) | collective-permute-done | bytes 1048608 | tf_op jit(solution)/shard_map/ppermute | solution.py:142
  141.0 2.2 %aggregate_tiles.3 = (bf16[256,512]{1,0:T(8,128)(2,1)S(1)}, bf16[256,512]{1,0:T(8,128)(2,1)S(1)}, bf16[256,512]{1,0:T(8,128)(2,1)S(1)}, bf16[256,512]{1,0:T(8,12...) custom-call(s32[32]{0:T(128)S(1)} %get-tuple-element.42.row_ref, ...), custom_call_target="tpu_custom_call" | custom-call | tf_op jit(solution)/shard_map/aggregate_tiles/pallas_call | solution.py:50
  143.1 0.3 collective-permute-start.30
  143.5 0.1 collective-permute-start.34
  143.6 4.1 %collective-permute-start.31 = (bf16[128,512]{1,0:T(8,128)(2,1)S(1)}, bf16[128,512]{1,0:T(8,128)(2,1)S(1)}, u32[]{:S(2)}, u32[]{:S(2)}) collective-permute-start(bf16[128,512]{1,0:T(8,128)(2,1)S(1)} %get-tuple-element.38), channel_id=1, source_target_pairs={{0,2},{1,3},{2,4},{3,5},{4,6},{5,7},{6,0},{7,1},{8,10},{9,11},{10,... | collective-permute-start | bytes 393224 | tf_op jit(solution)/shard_map/ppermute | solution.py:153
  147.7 0.5 collective-permute-start.28
  148.2 1.5 collective-permute-start.29
  149.7 5.7 %collective-permute-done.30 = bf16[256,512]{1,0:T(8,128)(2,1)S(1)} collective-permute-done((bf16[256,512]{1,0:T(8,128)(2,1)S(1)}, bf16[256,512]{1,0:T(8,128)(2,1)S(1)}, u32[]{:S(2)}, u32[]{:S(2)}) %collective-permute-start.30) | collective-permute-done | bytes 262176 | tf_op jit(solution)/shard_map/ppermute | solution.py:153
  155.4 0.1 convert_add_fusion.1
  155.6 2.2 %collective-permute-start.32 = (bf16[256,512]{1,0:T(8,128)(2,1)S(1)}, bf16[256,512]{1,0:T(8,128)(2,1)S(1)}, u32[]{:S(2)}, u32[]{:S(2)}) collective-permute-start(bf16[256,512]{1,0:T(8,128)(2,1)S(1)} %pad_maximum_fusion.3), channel_id=1, source_target_pairs={{0,2},{1,3},{2,4},{3,5},{4,6},{5,7},{6,0},{7,1},{8,10},{9,11},{10,... | collective-permute-start | bytes 786440 | tf_op jit(solution)/shard_map/ppermute | solution.py:153
  157.7 7.5 %collective-permute-done.33 = bf16[256,512]{1,0:T(8,128)(2,1)S(1)} collective-permute-done((bf16[256,512]{1,0:T(8,128)(2,1)S(1)}, bf16[256,512]{1,0:T(8,128)(2,1)S(1)}, u32[]{:S(2)}, u32[]{:S(2)}) %collective-permute-start.33) | collective-permute-done | bytes 262176 | tf_op jit(solution)/shard_map/ppermute | solution.py:153
  165.4 0.1 collective-permute-start.35
  165.5 0.5 collective-permute-done.28.refs_2_
  166.1 3.9 %collective-permute-done.32.refs_4_ = bf16[256,512]{1,0:T(8,128)(2,1)S(1)} collective-permute-done((bf16[256,512]{1,0:T(8,128)(2,1)S(1)}, bf16[256,512]{1,0:T(8,128)(2,1)S(1)}, u32[]{:S(2)}, u32[]{:S(2)}) %collective-permute-start.32) | collective-permute-done | bytes 262176 | tf_op jit(solution)/shard_map/ppermute | solution.py:153
  169.9 10.9 %collective-permute-done.35.refs_5_ = bf16[256,512]{1,0:T(8,128)(2,1)S(1)} collective-permute-done((bf16[256,512]{1,0:T(8,128)(2,1)S(1)}, bf16[256,512]{1,0:T(8,128)(2,1)S(1)}, u32[]{:S(2)}, u32[]{:S(2)}) %collective-permute-start.35) | collective-permute-done | bytes 262176 | tf_op jit(solution)/shard_map/ppermute | solution.py:153
  180.9 2.7 %node_mlp.3 = bf16[256,512]{1,0:T(8,128)(2,1)} custom-call(f32[2,256,512]{2,1,0:T(8,128)S(1)} %broadcast_multiply_fusion.scale_ref, bf16[256,512]{1,0:T(8,128)(2,1)S(1)} %convolution_convert_fusion.shift_ref, bf16[2,512,2048]{2,1,0:T(8,128)(2,1)S(1)} %copy-done.1, bf16[2,2048,512]{2,1,0:T(8,128)(2,1)S(1)} %copy-done.2, ...), custom_call_target="tpu_custom_call" | custom-call | tf_op jit(solution)/shard_map/node_mlp/pallas_call | solution.py:98
  (74 shorter events, 0.7 us)
Async XLA Ops:
  0.0 51.1 %copy-start = (bf16[128,512]{1,0:T(8,128)(2,1)S(1)}, bf16[128,512]{1,0:T(8,128)(2,1)}, u32[]{:S(2)}) copy-start(bf16[128,512]{1,0:T(8,128)(2,1)} %param.18) | copy-start | bytes 393220
  0.0 38.8 %copy-start.7 = (s32[16,1,4]{0,2,1:T(4,128)S(1)}, s32[16,1,4]{0,2,1:T(4,128)}, u32[]{:S(2)}) copy-start(s32[16,1,4]{0,2,1:T(4,128)} %param.14) | copy-start | bytes 772
  0.0 6.6 %collective-permute-start = (bf16[256,512]{1,0:T(8,128)(2,1)}, bf16[256,512]{1,0:T(8,128)(2,1)S(1)}, u32[]{:S(2)}, u32[]{:S(2)}) collective-permute-start(bf16[256,512]{1,0:T(8,128)(2,1)} %refs_0_.1), channel_id=1, source_target_pairs={{64,0},{24,8},{80,16},{40,24},{96,32},{56,40},{112,48},{8,56},{128... | collective-permute-start | bytes 786440 | tf_op jit(solution)/shard_map/ppermute | solution.py:137
  0.5 7.4 %collective-permute-start.1 = (bf16[256,512]{1,0:T(8,128)(2,1)}, bf16[256,512]{1,0:T(8,128)(2,1)S(1)}, u32[]{:S(2)}, u32[]{:S(2)}) collective-permute-start(bf16[256,512]{1,0:T(8,128)(2,1)} %refs_0_.1), channel_id=1, source_target_pairs={{192,0},{56,8},{208,16},{8,24},{224,32},{24,40},{240,48},{40,56},{... | collective-permute-start | bytes 786440 | tf_op jit(solution)/shard_map/ppermute | solution.py:137
  2.0 8.3 %collective-permute-start.2 = (bf16[256,512]{1,0:T(8,128)(2,1)}, bf16[256,512]{1,0:T(8,128)(2,1)S(1)}, u32[]{:S(2)}, u32[]{:S(2)}) collective-permute-start(bf16[256,512]{1,0:T(8,128)(2,1)} %refs_0_.1), channel_id=1, source_target_pairs={{128,0},{40,8},{144,16},{56,24},{160,32},{8,40},{176,48},{24,56},{... | collective-permute-start | bytes 786440 | tf_op jit(solution)/shard_map/ppermute | solution.py:137
  10.3 16.6 %collective-permute-start.5 = (bf16[1024,512]{1,0:T(8,128)(2,1)S(1)}, bf16[1024,512]{1,0:T(8,128)(2,1)}, u32[]{:S(2)}, u32[]{:S(2)}) collective-permute-start(bf16[1024,512]{1,0:T(8,128)(2,1)S(1)} %constant_dynamic-update-slice_fusion.refs_0_), channel_id=1, source_target_pairs={{32,0},{136,8},{48,16},{152,24},{0,32},{168,40},{16,48},{184,56},{... | collective-permute-start | bytes 3145736 | tf_op jit(solution)/shard_map/ppermute | solution.py:137
  13.6 24.4 %collective-permute-start.4 = (bf16[1024,512]{1,0:T(8,128)(2,1)S(1)}, bf16[1024,512]{1,0:T(8,128)(2,1)}, u32[]{:S(2)}, u32[]{:S(2)}) collective-permute-start(bf16[1024,512]{1,0:T(8,128)(2,1)S(1)} %constant_dynamic-update-slice_fusion.refs_0_), channel_id=1, source_target_pairs={{48,0},{200,8},{0,16},{216,24},{16,32},{232,40},{32,48},{248,56},{... | collective-permute-start | bytes 3145736 | tf_op jit(solution)/shard_map/ppermute | solution.py:137
  14.3 24.4 %collective-permute-start.3 = (bf16[1024,512]{1,0:T(8,128)(2,1)S(1)}, bf16[1024,512]{1,0:T(8,128)(2,1)}, u32[]{:S(2)}, u32[]{:S(2)}) collective-permute-start(bf16[1024,512]{1,0:T(8,128)(2,1)S(1)} %constant_dynamic-update-slice_fusion.refs_0_), channel_id=1, source_target_pairs={{16,0},{72,8},{32,16},{88,24},{48,32},{104,40},{0,48},{120,56},{80... | collective-permute-start | bytes 3145736 | tf_op jit(solution)/shard_map/ppermute | solution.py:137
  16.9 26.1 %collective-permute-start.6 = (bf16[1024,512]{1,0:T(8,128)(2,1)S(1)}, bf16[1024,512]{1,0:T(8,128)(2,1)}, u32[]{:S(2)}, u32[]{:S(2)}) collective-permute-start(bf16[1024,512]{1,0:T(8,128)(2,1)S(1)} %constant_dynamic-update-slice_fusion.refs_0_), channel_id=1, source_target_pairs={{0,8},{8,0},{16,24},{24,16},{32,40},{40,32},{48,56},{56,48},{64,72... | collective-permute-start | bytes 3145736 | tf_op jit(solution)/shard_map/ppermute | solution.py:142
  26.9 16.0 %collective-permute-start.9 = (bf16[1024,512]{1,0:T(8,128)(2,1)}, bf16[1024,512]{1,0:T(8,128)(2,1)}, u32[]{:S(2)}, u32[]{:S(2)}) collective-permute-start(bf16[1024,512]{1,0:T(8,128)(2,1)} %collective-permute-done.5.refs_3_), channel_id=1, source_target_pairs={{0,8},{8,0},{16,24},{24,16},{32,40},{40,32},{48,56},{56,48},{64,72... | collective-permute-start | bytes 3145736 | tf_op jit(solution)/shard_map/ppermute | solution.py:142
  38.1 4.9 %collective-permute-start.8 = (bf16[1024,512]{1,0:T(8,128)(2,1)}, bf16[1024,512]{1,0:T(8,128)(2,1)}, u32[]{:S(2)}, u32[]{:S(2)}) collective-permute-start(bf16[1024,512]{1,0:T(8,128)(2,1)} %collective-permute-done.4.refs_2_), channel_id=1, source_target_pairs={{0,8},{8,0},{16,24},{24,16},{32,40},{40,32},{48,56},{56,48},{64,72... | collective-permute-start | bytes 3145736 | tf_op jit(solution)/shard_map/ppermute | solution.py:142
  38.7 4.2 %collective-permute-start.7 = (bf16[1024,512]{1,0:T(8,128)(2,1)}, bf16[1024,512]{1,0:T(8,128)(2,1)}, u32[]{:S(2)}, u32[]{:S(2)}) collective-permute-start(bf16[1024,512]{1,0:T(8,128)(2,1)} %collective-permute-done.3.refs_1_), channel_id=1, source_target_pairs={{0,8},{8,0},{16,24},{24,16},{32,40},{40,32},{48,56},{56,48},{64,72... | collective-permute-start | bytes 3145736 | tf_op jit(solution)/shard_map/ppermute | solution.py:142
  38.9 2.9 %copy-start.8 = (s32[32,1]{0,1:T(1,128)S(1)}, s32[32,1]{0,1:T(1,128)}, u32[]{:S(2)}) copy-start(s32[32,1]{0,1:T(1,128)} %constant.119) | copy-start | bytes 388
  38.9 2.9 %copy-start.9 = (s32[32,1]{0,1:T(1,128)S(1)}, s32[32,1]{0,1:T(1,128)}, u32[]{:S(2)}) copy-start(s32[32,1]{0,1:T(1,128)} %constant.118) | copy-start | bytes 388
  39.0 2.9 %copy-start.10 = (s32[32,1]{0,1:T(1,128)S(1)}, s32[32,1]{0,1:T(1,128)}, u32[]{:S(2)}) copy-start(s32[32,1]{0,1:T(1,128)} %constant.117) | copy-start | bytes 388
  39.0 2.9 %copy-start.4 = (s32[1,1,32,1]{2,3,1,0:T(1,128)S(1)}, s32[1,1,32,1]{2,3,1,0:T(1,128)}, u32[]{:S(2)}) copy-start(s32[1,1,32,1]{2,3,1,0:T(1,128)} %param.15) | copy-start | bytes 388
  39.0 3.6 %copy-start.13 = (s32[32]{0:T(128)S(1)}, s32[32]{0:T(128)}, u32[]{:S(2)}) copy-start(s32[32]{0:T(128)} %constant.116) | copy-start | bytes 388
  39.0 3.7 %copy-start.5 = (bf16[16,512]{1,0:T(8,128)(2,1)S(1)}, bf16[16,512]{1,0:T(8,128)(2,1)}, u32[]{:S(2)}) copy-start(bf16[16,512]{1,0:T(8,128)(2,1)} %param.19) | copy-start | bytes 49156
  39.0 3.7 %copy-start.11 = (s32[256]{0:T(256)S(1)}, s32[256]{0:T(256)}, u32[]{:S(2)}) copy-start(s32[256]{0:T(256)} %param.17) | copy-start | bytes 3076
  43.0 8.1 %copy-start.12 = (s32[256]{0:T(256)S(1)}, s32[256]{0:T(256)}, u32[]{:S(2)}) copy-start(s32[256]{0:T(256)} %param.16) | copy-start | bytes 3076
  43.0 43.1 %copy-start.2 = (bf16[2,2048,512]{2,1,0:T(8,128)(2,1)S(1)}, bf16[2,2048,512]{2,1,0:T(8,128)(2,1)}, u32[]{:S(2)}) copy-start(bf16[2,2048,512]{2,1,0:T(8,128)(2,1)} %w_out_ref.3) | copy-start | bytes 12582916
  47.9 12.2 %collective-permute-start.12 = (bf16[256,512]{1,0:T(8,128)(2,1)S(1)}, bf16[256,512]{1,0:T(8,128)(2,1)S(1)}, u32[]{:S(2)}, u32[]{:S(2)}) collective-permute-start(bf16[256,512]{1,0:T(8,128)(2,1)S(1)} %get-tuple-element.25), channel_id=1, source_target_pairs={{0,1},{1,2},{2,3},{3,4},{4,5},{5,6},{6,7},{7,0},{8,9},{9,10},{10,1... | collective-permute-start | bytes 786440 | tf_op jit(solution)/shard_map/ppermute | solution.py:153
  51.4 19.6 %collective-permute-start.16 = (bf16[128,512]{1,0:T(8,128)(2,1)S(1)}, bf16[128,512]{1,0:T(8,128)(2,1)S(1)}, u32[]{:S(2)}, u32[]{:S(2)}) collective-permute-start(bf16[128,512]{1,0:T(8,128)(2,1)S(1)} %get-tuple-element.39), channel_id=1, source_target_pairs={{0,6},{1,7},{2,0},{3,1},{4,2},{5,3},{6,4},{7,5},{8,14},{9,15},{10,... | collective-permute-start | bytes 393224 | tf_op jit(solution)/shard_map/ppermute | solution.py:153
  51.5 11.8 %collective-permute-start.13 = (bf16[128,512]{1,0:T(8,128)(2,1)S(1)}, bf16[128,512]{1,0:T(8,128)(2,1)S(1)}, u32[]{:S(2)}, u32[]{:S(2)}) collective-permute-start(bf16[128,512]{1,0:T(8,128)(2,1)S(1)} %get-tuple-element.40), channel_id=1, source_target_pairs={{0,2},{1,3},{2,4},{3,5},{4,6},{5,7},{6,0},{7,1},{8,10},{9,11},{10,... | collective-permute-start | bytes 393224 | tf_op jit(solution)/shard_map/ppermute | solution.py:153
  55.6 18.4 %collective-permute-start.10 = (bf16[256,512]{1,0:T(8,128)(2,1)S(1)}, bf16[256,512]{1,0:T(8,128)(2,1)S(1)}, u32[]{:S(2)}, u32[]{:S(2)}) collective-permute-start(bf16[256,512]{1,0:T(8,128)(2,1)S(1)} %get-tuple-element.22), channel_id=1, source_target_pairs={{0,1},{1,2},{2,3},{3,4},{4,5},{5,6},{6,7},{7,0},{8,9},{9,10},{10,1... | collective-permute-start | bytes 786440 | tf_op jit(solution)/shard_map/ppermute | solution.py:153
  55.6 18.4 %collective-permute-start.11 = (bf16[256,512]{1,0:T(8,128)(2,1)S(1)}, bf16[256,512]{1,0:T(8,128)(2,1)S(1)}, u32[]{:S(2)}, u32[]{:S(2)}) collective-permute-start(bf16[256,512]{1,0:T(8,128)(2,1)S(1)} %get-tuple-element.23), channel_id=1, source_target_pairs={{0,7},{1,0},{2,1},{3,2},{4,3},{5,4},{6,5},{7,6},{8,15},{9,8},{10,9... | collective-permute-start | bytes 786440 | tf_op jit(solution)/shard_map/ppermute | solution.py:153
  60.1 10.8 %collective-permute-start.15 = (bf16[256,512]{1,0:T(8,128)(2,1)S(1)}, bf16[256,512]{1,0:T(8,128)(2,1)S(1)}, u32[]{:S(2)}, u32[]{:S(2)}) collective-permute-start(bf16[256,512]{1,0:T(8,128)(2,1)S(1)} %get-tuple-element.28), channel_id=1, source_target_pairs={{0,7},{1,0},{2,1},{3,2},{4,3},{5,4},{6,5},{7,6},{8,15},{9,8},{10,9... | collective-permute-start | bytes 786440 | tf_op jit(solution)/shard_map/ppermute | solution.py:153
  60.2 12.2 %copy-start.6 = (f32[2,512]{1,0:T(2,128)S(1)}, f32[2,512]{1,0:T(2,128)}, u32[]{:S(2)}) copy-start(f32[2,512]{1,0:T(2,128)} %param.20) | copy-start | bytes 12292
  63.4 22.8 %copy-start.1 = (bf16[2,512,2048]{2,1,0:T(8,128)(2,1)S(1)}, bf16[2,512,2048]{2,1,0:T(8,128)(2,1)}, u32[]{:S(2)}) copy-start(bf16[2,512,2048]{2,1,0:T(8,128)(2,1)} %w_in_ref.3) | copy-start | bytes 12582916
  63.4 22.7 %copy-start.3 = (bf16[256,512]{1,0:T(8,128)(2,1)S(1)}, bf16[256,512]{1,0:T(8,128)(2,1)}, u32[]{:S(2)}) copy-start(bf16[256,512]{1,0:T(8,128)(2,1)} %refs_0_.1) | copy-start | bytes 786436
  63.4 16.4 %collective-permute-start.14 = (bf16[256,512]{1,0:T(8,128)(2,1)S(1)}, bf16[256,512]{1,0:T(8,128)(2,1)S(1)}, u32[]{:S(2)}, u32[]{:S(2)}) collective-permute-start(bf16[256,512]{1,0:T(8,128)(2,1)S(1)} %pad_maximum_fusion.1), channel_id=1, source_target_pairs={{0,2},{1,3},{2,4},{3,5},{4,6},{5,7},{6,0},{7,1},{8,10},{9,11},{10,... | collective-permute-start | bytes 786440 | tf_op jit(solution)/shard_map/ppermute | solution.py:153
  71.1 15.0 %collective-permute-start.17 = (bf16[256,512]{1,0:T(8,128)(2,1)S(1)}, bf16[256,512]{1,0:T(8,128)(2,1)S(1)}, u32[]{:S(2)}, u32[]{:S(2)}) collective-permute-start(bf16[256,512]{1,0:T(8,128)(2,1)S(1)} %pad_maximum_fusion.2), channel_id=1, source_target_pairs={{0,6},{1,7},{2,0},{3,1},{4,2},{5,3},{6,4},{7,5},{8,14},{9,15},{10,... | collective-permute-start | bytes 786440 | tf_op jit(solution)/shard_map/ppermute | solution.py:153
  88.1 8.0 %collective-permute-start.20 = (bf16[256,512]{1,0:T(8,128)(2,1)S(1)}, bf16[256,512]{1,0:T(8,128)(2,1)S(1)}, u32[]{:S(2)}, u32[]{:S(2)}) collective-permute-start(bf16[256,512]{1,0:T(8,128)(2,1)S(1)} %node_mlp.2.refs_0_), channel_id=1, source_target_pairs={{128,0},{40,8},{144,16},{56,24},{160,32},{8,40},{176,48},{24,56},{... | collective-permute-start | bytes 786440 | tf_op jit(solution)/shard_map/ppermute | solution.py:137
  90.9 7.9 %collective-permute-start.19 = (bf16[256,512]{1,0:T(8,128)(2,1)S(1)}, bf16[256,512]{1,0:T(8,128)(2,1)S(1)}, u32[]{:S(2)}, u32[]{:S(2)}) collective-permute-start(bf16[256,512]{1,0:T(8,128)(2,1)S(1)} %node_mlp.2.refs_0_), channel_id=1, source_target_pairs={{192,0},{56,8},{208,16},{8,24},{224,32},{24,40},{240,48},{40,56},{... | collective-permute-start | bytes 786440 | tf_op jit(solution)/shard_map/ppermute | solution.py:137
  92.9 6.4 %collective-permute-start.18 = (bf16[256,512]{1,0:T(8,128)(2,1)S(1)}, bf16[256,512]{1,0:T(8,128)(2,1)S(1)}, u32[]{:S(2)}, u32[]{:S(2)}) collective-permute-start(bf16[256,512]{1,0:T(8,128)(2,1)S(1)} %node_mlp.2.refs_0_), channel_id=1, source_target_pairs={{64,0},{24,8},{80,16},{40,24},{96,32},{56,40},{112,48},{8,56},{128... | collective-permute-start | bytes 786440 | tf_op jit(solution)/shard_map/ppermute | solution.py:137
  99.3 16.5 %collective-permute-start.23 = (bf16[1024,512]{1,0:T(8,128)(2,1)S(1)}, bf16[1024,512]{1,0:T(8,128)(2,1)S(1)}, u32[]{:S(2)}, u32[]{:S(2)}) collective-permute-start(bf16[1024,512]{1,0:T(8,128)(2,1)S(1)} %pad_maximum_fusion.refs_0_), channel_id=1, source_target_pairs={{32,0},{136,8},{48,16},{152,24},{0,32},{168,40},{16,48},{184,56},{... | collective-permute-start | bytes 3145736 | tf_op jit(solution)/shard_map/ppermute | solution.py:137
  101.3 25.7 %collective-permute-start.22 = (bf16[1024,512]{1,0:T(8,128)(2,1)S(1)}, bf16[1024,512]{1,0:T(8,128)(2,1)S(1)}, u32[]{:S(2)}, u32[]{:S(2)}) collective-permute-start(bf16[1024,512]{1,0:T(8,128)(2,1)S(1)} %pad_maximum_fusion.refs_0_), channel_id=1, source_target_pairs={{48,0},{200,8},{0,16},{216,24},{16,32},{232,40},{32,48},{248,56},{... | collective-permute-start | bytes 3145736 | tf_op jit(solution)/shard_map/ppermute | solution.py:137
  114.3 24.1 %collective-permute-start.21 = (bf16[1024,512]{1,0:T(8,128)(2,1)S(1)}, bf16[1024,512]{1,0:T(8,128)(2,1)S(1)}, u32[]{:S(2)}, u32[]{:S(2)}) collective-permute-start(bf16[1024,512]{1,0:T(8,128)(2,1)S(1)} %pad_maximum_fusion.refs_0_), channel_id=1, source_target_pairs={{16,0},{72,8},{32,16},{88,24},{48,32},{104,40},{0,48},{120,56},{80... | collective-permute-start | bytes 3145736 | tf_op jit(solution)/shard_map/ppermute | solution.py:137
  114.3 24.1 %collective-permute-start.24 = (bf16[1024,512]{1,0:T(8,128)(2,1)S(1)}, bf16[1024,512]{1,0:T(8,128)(2,1)S(1)}, u32[]{:S(2)}, u32[]{:S(2)}) collective-permute-start(bf16[1024,512]{1,0:T(8,128)(2,1)S(1)} %pad_maximum_fusion.refs_0_), channel_id=1, source_target_pairs={{0,8},{8,0},{16,24},{24,16},{32,40},{40,32},{48,56},{56,48},{64,72... | collective-permute-start | bytes 3145736 | tf_op jit(solution)/shard_map/ppermute | solution.py:142
  115.8 22.5 %collective-permute-start.27 = (bf16[1024,512]{1,0:T(8,128)(2,1)S(1)}, bf16[1024,512]{1,0:T(8,128)(2,1)S(1)}, u32[]{:S(2)}, u32[]{:S(2)}) collective-permute-start(bf16[1024,512]{1,0:T(8,128)(2,1)S(1)} %collective-permute-done.23.refs_3_), channel_id=1, source_target_pairs={{0,8},{8,0},{16,24},{24,16},{32,40},{40,32},{48,56},{56,48},{64,72... | collective-permute-start | bytes 3145736 | tf_op jit(solution)/shard_map/ppermute | solution.py:142
  127.0 11.4 %collective-permute-start.26 = (bf16[1024,512]{1,0:T(8,128)(2,1)S(1)}, bf16[1024,512]{1,0:T(8,128)(2,1)S(1)}, u32[]{:S(2)}, u32[]{:S(2)}) collective-permute-start(bf16[1024,512]{1,0:T(8,128)(2,1)S(1)} %collective-permute-done.22.refs_2_), channel_id=1, source_target_pairs={{0,8},{8,0},{16,24},{24,16},{32,40},{40,32},{48,56},{56,48},{64,72... | collective-permute-start | bytes 3145736 | tf_op jit(solution)/shard_map/ppermute | solution.py:142
  138.3 2.7 %collective-permute-start.25 = (bf16[1024,512]{1,0:T(8,128)(2,1)S(1)}, bf16[1024,512]{1,0:T(8,128)(2,1)S(1)}, u32[]{:S(2)}, u32[]{:S(2)}) collective-permute-start(bf16[1024,512]{1,0:T(8,128)(2,1)S(1)} %collective-permute-done.21.refs_1_), channel_id=1, source_target_pairs={{0,8},{8,0},{16,24},{24,16},{32,40},{40,32},{48,56},{56,48},{64,72... | collective-permute-start | bytes 3145736 | tf_op jit(solution)/shard_map/ppermute | solution.py:142
  143.1 12.3 %collective-permute-start.30 = (bf16[256,512]{1,0:T(8,128)(2,1)S(1)}, bf16[256,512]{1,0:T(8,128)(2,1)S(1)}, u32[]{:S(2)}, u32[]{:S(2)}) collective-permute-start(bf16[256,512]{1,0:T(8,128)(2,1)S(1)} %get-tuple-element.33), channel_id=1, source_target_pairs={{0,1},{1,2},{2,3},{3,4},{4,5},{5,6},{6,7},{7,0},{8,9},{9,10},{10,1... | collective-permute-start | bytes 786440 | tf_op jit(solution)/shard_map/ppermute | solution.py:153
  143.5 21.9 %collective-permute-start.34 = (bf16[128,512]{1,0:T(8,128)(2,1)S(1)}, bf16[128,512]{1,0:T(8,128)(2,1)S(1)}, u32[]{:S(2)}, u32[]{:S(2)}) collective-permute-start(bf16[128,512]{1,0:T(8,128)(2,1)S(1)} %get-tuple-element.37), channel_id=1, source_target_pairs={{0,6},{1,7},{2,0},{3,1},{4,2},{5,3},{6,4},{7,5},{8,14},{9,15},{10,... | collective-permute-start | bytes 393224 | tf_op jit(solution)/shard_map/ppermute | solution.py:153
  143.6 11.9 %collective-permute-start.31 = (bf16[128,512]{1,0:T(8,128)(2,1)S(1)}, bf16[128,512]{1,0:T(8,128)(2,1)S(1)}, u32[]{:S(2)}, u32[]{:S(2)}) collective-permute-start(bf16[128,512]{1,0:T(8,128)(2,1)S(1)} %get-tuple-element.38), channel_id=1, source_target_pairs={{0,2},{1,3},{2,4},{3,5},{4,6},{5,7},{6,0},{7,1},{8,10},{9,11},{10,... | collective-permute-start | bytes 393224 | tf_op jit(solution)/shard_map/ppermute | solution.py:153
  147.7 18.4 %collective-permute-start.28 = (bf16[256,512]{1,0:T(8,128)(2,1)S(1)}, bf16[256,512]{1,0:T(8,128)(2,1)S(1)}, u32[]{:S(2)}, u32[]{:S(2)}) collective-permute-start(bf16[256,512]{1,0:T(8,128)(2,1)S(1)} %get-tuple-element.30), channel_id=1, source_target_pairs={{0,1},{1,2},{2,3},{3,4},{4,5},{5,6},{6,7},{7,0},{8,9},{9,10},{10,1... | collective-permute-start | bytes 786440 | tf_op jit(solution)/shard_map/ppermute | solution.py:153
  148.2 17.8 %collective-permute-start.29 = (bf16[256,512]{1,0:T(8,128)(2,1)S(1)}, bf16[256,512]{1,0:T(8,128)(2,1)S(1)}, u32[]{:S(2)}, u32[]{:S(2)}) collective-permute-start(bf16[256,512]{1,0:T(8,128)(2,1)S(1)} %get-tuple-element.31), channel_id=1, source_target_pairs={{0,7},{1,0},{2,1},{3,2},{4,3},{5,4},{6,5},{7,6},{8,15},{9,8},{10,9... | collective-permute-start | bytes 786440 | tf_op jit(solution)/shard_map/ppermute | solution.py:153
  155.4 9.8 %collective-permute-start.33 = (bf16[256,512]{1,0:T(8,128)(2,1)S(1)}, bf16[256,512]{1,0:T(8,128)(2,1)S(1)}, u32[]{:S(2)}, u32[]{:S(2)}) collective-permute-start(bf16[256,512]{1,0:T(8,128)(2,1)S(1)} %get-tuple-element.36), channel_id=1, source_target_pairs={{0,7},{1,0},{2,1},{3,2},{4,3},{5,4},{6,5},{7,6},{8,15},{9,8},{10,9... | collective-permute-start | bytes 786440 | tf_op jit(solution)/shard_map/ppermute | solution.py:153
  155.6 14.3 %collective-permute-start.32 = (bf16[256,512]{1,0:T(8,128)(2,1)S(1)}, bf16[256,512]{1,0:T(8,128)(2,1)S(1)}, u32[]{:S(2)}, u32[]{:S(2)}) collective-permute-start(bf16[256,512]{1,0:T(8,128)(2,1)S(1)} %pad_maximum_fusion.3), channel_id=1, source_target_pairs={{0,2},{1,3},{2,4},{3,5},{4,6},{5,7},{6,0},{7,1},{8,10},{9,11},{10,... | collective-permute-start | bytes 786440 | tf_op jit(solution)/shard_map/ppermute | solution.py:153
  165.4 15.4 %collective-permute-start.35 = (bf16[256,512]{1,0:T(8,128)(2,1)S(1)}, bf16[256,512]{1,0:T(8,128)(2,1)S(1)}, u32[]{:S(2)}, u32[]{:S(2)}) collective-permute-start(bf16[256,512]{1,0:T(8,128)(2,1)S(1)} %pad_maximum_fusion.4), channel_id=1, source_target_pairs={{0,6},{1,7},{2,0},{3,1},{4,2},{5,3},{6,4},{7,5},{8,14},{9,15},{10,... | collective-permute-start | bytes 786440 | tf_op jit(solution)/shard_map/ppermute | solution.py:153

commit v3 on v2

--- a/solution.py
+++ b/solution.py
@@ -7,7 +7,7 @@
 
 LAYERS = 2
 PIECES = 1
-VMEM_LIMIT = 22 * 1024 * 1024
+VMEM_LIMIT = 20 * 1024 * 1024
 
 epsilon = 1e-06
 
@@ -19,43 +19,47 @@
     return jnp.dot(onehot, table, preferred_element_type=jnp.float32)
 
 
-def aggregate_tiles(matrix, sources, source_of, source_row, source_slot, slot_index, order):
+def aggregate_tiles(matrix, sources, here, wanted, slot_index, further):
     row_tiles, tile, depth = matrix.shape
     slots = depth // tile
     width = sources[0].shape[-1]
-    gathered = source_row.shape[0]
-    blocks = order.shape[0]
-    per_block = row_tiles // blocks
+    count = lax.axis_size("col")
+    per_block = row_tiles // count
     n_src = len(sources)
     rows = per_block * tile
 
-    def body(row_ref, slot_ref, index_ref, order_ref, matrix_ref, *refs):
+    def body(here_ref, wanted_ref, index_ref, matrix_ref, *refs):
         src = refs[:n_src]
-        outs = refs[n_src : n_src + blocks]
-        (tiles,) = refs[n_src + blocks :]
-        for b in range(gathered):
-            start = pl.multiple_of(row_ref[b], tile)
-            tiles[slot_ref[b]] = src[source_of[b]][pl.ds(start, tile), :]
-        for k in range(blocks):
+        outs = refs[n_src:-1]
+        tiles = refs[-1]
+        x, y, core, col = (here_ref[i] for i in range(4))
+        for array, block, first, second, swapped in BLOCKS:
+            held = core ^ swapped
+            step_x = jnp.where(held == 0, first, second)
+            step_y = jnp.where(held == 0, second, first)
+            p = place(x + step_x + SIDE, y + step_y + SIDE, held)
+            start = pl.multiple_of(block * rows + wanted_ref[p] * tile, tile)
+            tiles[p] = src[array][pl.ds(start, tile), :]
+        for out, k in zip(outs, further, strict=True):
             for j in range(per_block):
-                t = order_ref[k] * per_block + j
+                t = (col + k) % count * per_block + j
                 right = jnp.concatenate(
                     [tiles[index_ref[t * slots + s]] for s in range(slots)], axis=0
                 )
                 value = jnp.dot(matrix_ref[t], right, preferred_element_type=jnp.float32)
-                outs[k][j * tile : (j + 1) * tile, :] = value.astype(jnp.bfloat16)
+                out[j * tile : (j + 1) * tile, :] = value.astype(jnp.bfloat16)
 
     smem = pl.BlockSpec(memory_space=pltpu.SMEM)
     vmem = pl.BlockSpec(memory_space=pltpu.VMEM)
     return pl.pallas_call(
         body,
-        in_specs=[smem] * 4 + [vmem] * (1 + n_src),
-        out_specs=[vmem] * blocks,
-        out_shape=[jax.ShapeDtypeStruct((rows, width), jnp.bfloat16)] * blocks,
-        scratch_shapes=[pltpu.VMEM((gathered, tile, width), jnp.bfloat16)],
+        in_specs=[smem] * 3 + [vmem] * (1 + n_src),
+        out_specs=[vmem] * len(further),
+        out_shape=[jax.ShapeDtypeStruct((rows, width), jnp.bfloat16)] * len(further),
+        scratch_shapes=[pltpu.VMEM((len(BLOCKS), tile, width), jnp.bfloat16)],
         compiler_params=pltpu.CompilerParams(vmem_limit_bytes=VMEM_LIMIT),
         name="aggregate_tiles",
-    )(source_row, source_slot, slot_index, order, matrix, *sources)
+    )(here, wanted, slot_index, matrix, *sources)
 
 
 def node_mlp(layer, states, parts, scale_rows, shift_rows, w_in, w_out, pieces):
@@ -121,6 +125,7 @@
 
 
 BLOCKS = held_blocks()
+SENT = ((3, 5, 4), (2, 6, 1, 7, 0))
 
 
 def place(x, y, core):
@@ -142,10 +147,13 @@
     return lax.ppermute(value, "row", [(i, i ^ 1) for i in range(count)])
 
 
-def gather_blocks(own):
+def gather_blocks(own, ready):
+    after = lax.optimization_barrier
     line = jnp.concatenate([own] + [pull(own, True, e) for e in NEAR], axis=0)
-    arrays = [line] + [pull(line, False, d) for d in NEAR]
-    return arrays + [swap(v) for v in arrays]
+    far = [pull(line, False, d) for d in NEAR]
+    first = swap(line)
+    far, first, ready = after((far, first, ready))
+    return [line] + far + [first] + [swap(v) for v in far], ready
 
 
 def send(value, distance):
@@ -186,39 +194,27 @@
     w_in,
     w_out,
 ):
-    col_count = lax.axis_size("col")
-    span = features.shape[0]
     tile = tile_values.shape[-1]
     slots = tile_values.shape[3]
     row_tiles = tile_values.shape[0]
     matrix = tile_values.reshape(row_tiles, tile, slots * tile)
     slot_index = slot_refs.reshape(-1)
+    wanted = wanted.reshape(-1)
     row = lax.axis_index("row")
-    x, y, core = row // (2 * SIDE), row // 2 % SIDE, row % 2
-    order = (lax.axis_index("col") + jnp.arange(col_count, dtype=jnp.int32)) % col_count
+    here = jnp.stack([row // (2 * SIDE), row // 2 % SIDE, row % 2, lax.axis_index("col")])
     scale_rows = gains[:, None, :] * (1.0 + lookup(cond_ids, cond_table))[None]
     shift_rows = lookup(time_ids, time_table).astype(jnp.bfloat16)
-    table = jnp.array(BLOCKS, dtype=jnp.int32)
-    base, first, second, held = table[:, 1] * span, table[:, 2], table[:, 3], core ^ table[:, 4]
-    source_slot = jnp.where(
-        held == 0, place(x + first, y + second, 0), place(x + second, y + first, 1)
-    )
-    source_row = base + wanted.reshape(-1)[source_slot] * tile
     piece = features.shape[1] // PIECES
     states = [features[:, p * piece : (p + 1) * piece] for p in range(PIECES)]
+    ready = (matrix, wanted, slot_index, here)
     for layer in range(LAYERS):
-        parts = []
-        for state in states:
-            near = aggregate_tiles(
-                matrix,
-                gather_blocks(state),
-                [b[0] for b in BLOCKS],
-                source_row,
-                source_slot,
-                slot_index,
-                order,
-            )
-            parts.append(sum_columns(near, near[0]))
+        arrays, ready = gather_blocks(states[0], ready)
+        matrix, wanted, slot_index, here = ready
+        near = {}
+        for group in SENT:
+            products = aggregate_tiles(matrix, arrays, here, wanted, slot_index, group)
+            near.update(zip(group, products, strict=True))
+        parts = [sum_columns(near, near[0])]
         last = layer == LAYERS - 1
         states = node_mlp(
             layer,

time: 184 us -> 172 us (0.935)
  the two profiles are of different devices: /device:TPU:98 before, /device:TPU:1 now
where the time goes in v3:
time: 172 us
  waiting for transfers between devices  101 us (59%)
  starting transfers between devices  50.1 us (29%)
  Pallas kernels  14.5 us (8%)
  local copies, waits for them, and re-layouts  4.16 us (2%)
    ppermute x12, waiting for transfers between devices, pull(): return lax.ppermute(value, 'row', pairs)  55.6 us
    ppermute x16, waiting for transfers between devices, send(): lax.ppermute(value, 'col', [(i, (i + distance) % count) for i in range(co...  36.4 us
    ppermute x16, starting transfers between devices, send(): lax.ppermute(value, 'col', [(i, (i + distance) % count) for i in range(co...  26.4 us
    ppermute x12, starting transfers between devices, pull(): return lax.ppermute(value, 'row', pairs)  17 us
    pallas_call x4, Pallas kernels, aggregate_tiles(): pl.pallas_call(body, in_specs=[smem] * 3 + [vmem] * (1 + n_src), out_spec...  9.88 us
    ppermute x8, waiting for transfers between devices, swap(): return lax.ppermute(value, 'row', [(i, i ^ 1) for i in range(count)])  9.47 us
    ppermute x8, starting transfers between devices, swap(): return lax.ppermute(value, 'row', [(i, i ^ 1) for i in range(count)])  6.68 us
    pallas_call x2, Pallas kernels, node_mlp(): pl.pallas_call(body, in_specs=[vmem] * (4 + len(flat)), out_specs=[vmem]...  4.62 us
  transfers between devices with their start and end apart: 36, of which 27 were waited for; matrix products, arithmetic and copies ran while one was open for 3% of the time, Pallas kernels for 3%

profile of v3, /device:TPU:1, one launch (start us, length us, event | category | flops | bytes accessed | tf_op | source)
XLA Modules:
  0.0 171.8 jit_solution(10982132570733626403)
XLA Ops:
  0.0 3.6 %collective-permute-start = (bf16[256,512]{1,0:T(8,128)(2,1)}, bf16[256,512]{1,0:T(8,128)(2,1)S(1)}, u32[]{:S(2)}, u32[]{:S(2)}) collective-permute-start(bf16[256,512]{1,0:T(8,128)(2,1)} %refs_0_.1), channel_id=1, source_target_pairs={{64,0},{24,8},{80,16},{40,24},{96,32},{56,40},{112,48},{8,56},{128... | collective-permute-start | bytes 786440 | tf_op jit(solution)/shard_map/ppermute | solution.py:142
  3.6 1.6 collective-permute-start.2
  5.2 1.0 constant_dynamic-update-slice_fusion.3
  6.2 1.0 collective-permute-done
  7.2 6.1 %collective-permute-done.1 = bf16[256,512]{1,0:T(8,128)(2,1)S(1)} collective-permute-done((bf16[256,512]{1,0:T(8,128)(2,1)}, bf16[256,512]{1,0:T(8,128)(2,1)S(1)}, u32[]{:S(2)}, u32[]{:S(2)}) %collective-permute-start.1) | collective-permute-done | bytes 262176 | tf_op jit(solution)/shard_map/ppermute | solution.py:142
  13.4 1.6 collective-permute-start.6
  15.0 1.0 collective-permute-start.5
  16.0 0.3 collective-permute-start.4
  16.3 2.4 %collective-permute-start.3 = (bf16[1024,512]{1,0:T(8,128)(2,1)S(1)}, bf16[1024,512]{1,0:T(8,128)(2,1)}, u32[]{:S(2)}, u32[]{:S(2)}) collective-permute-start(bf16[1024,512]{1,0:T(8,128)(2,1)S(1)} %constant_dynamic-update-slice_fusion.refs_0_), channel_id=1, source_target_pairs={{16,0},{72,8},{32,16},{88,24},{48,32},{104,40},{0,48},{120,56},{80... | collective-permute-start | bytes 3145736 | tf_op jit(solution)/shard_map/ppermute | solution.py:142
  18.9 2.8 %reshape.13.matrix_ref = bf16[16,128,512]{2,1,0:T(8,128)(2,1)S(1)} reshape(bf16[16,1,128,4,128]{4,3,2,1,0:T(4,128)(2,1)} %param.12) | data formatting | bytes 4194304 | tf_op jit(solution)/shard_map/reshape | solution.py:200
  21.8 8.8 %collective-permute-done.5.refs_3_ = bf16[1024,512]{1,0:T(8,128)(2,1)} collective-permute-done((bf16[1024,512]{1,0:T(8,128)(2,1)S(1)}, bf16[1024,512]{1,0:T(8,128)(2,1)}, u32[]{:S(2)}, u32[]{:S(2)}) %collective-permute-start.5) | collective-permute-done | bytes 1048608 | tf_op jit(solution)/shard_map/ppermute | solution.py:142
  30.6 11.2 %collective-permute-done.4.refs_2_ = bf16[1024,512]{1,0:T(8,128)(2,1)} collective-permute-done((bf16[1024,512]{1,0:T(8,128)(2,1)S(1)}, bf16[1024,512]{1,0:T(8,128)(2,1)}, u32[]{:S(2)}, u32[]{:S(2)}) %collective-permute-start.4) | collective-permute-done | bytes 1048608 | tf_op jit(solution)/shard_map/ppermute | solution.py:142
  41.8 1.3 collective-permute-start.7
  43.2 0.5 collective-permute-start.9
  43.7 0.3 convolution_add_fusion
  44.0 1.7 collective-permute-done.7.refs_5_
  45.6 1.5 collective-permute-done.8.refs_6_
  47.1 1.5 collective-permute-done.9.refs_7_
  48.6 3.1 %aggregate_tiles.5 = (bf16[256,512]{1,0:T(8,128)(2,1)S(1)}, bf16[256,512]{1,0:T(8,128)(2,1)S(1)}, bf16[256,512]{1,0:T(8,128)(2,1)S(1)}) custom-call(s32[4]{0:T(128)S(1)} %pad_add_fusion.here_ref, s32[32]{0:T(128)S(1)} %bitcast.9, s32[64]{0:T(128)S(1)} %reshape.15.index_ref, bf16[16,128,512]{2,1,0:T(8,128)(2,1)S(1)} %reshape.13.matrix_ref, ...), custom_call_target="tpu_custom_call" | custom-call | tf_op jit(solution)/shard_map/aggregate_tiles/pallas_call | solution.py:54
  51.8 1.7 collective-permute-start.12
  53.5 0.3 convolution_convert_fusion.shift_ref
  53.8 5.2 %collective-permute-start.16 = (bf16[128,512]{1,0:T(8,128)(2,1)S(1)}, bf16[128,512]{1,0:T(8,128)(2,1)S(1)}, u32[]{:S(2)}, u32[]{:S(2)}) collective-permute-start(bf16[128,512]{1,0:T(8,128)(2,1)S(1)} %get-tuple-element.71), channel_id=1, source_target_pairs={{0,6},{1,7},{2,0},{3,1},{4,2},{5,3},{6,4},{7,5},{8,14},{9,15},{10,... | collective-permute-start | bytes 393224 | tf_op jit(solution)/shard_map/ppermute | solution.py:161
  59.0 2.4 %collective-permute-start.15 = (bf16[256,512]{1,0:T(8,128)(2,1)S(1)}, bf16[256,512]{1,0:T(8,128)(2,1)S(1)}, u32[]{:S(2)}, u32[]{:S(2)}) collective-permute-start(bf16[256,512]{1,0:T(8,128)(2,1)S(1)} %get-tuple-element.52), channel_id=1, source_target_pairs={{0,7},{1,0},{2,1},{3,2},{4,3},{5,4},{6,5},{7,6},{8,15},{9,8},{10,9... | collective-permute-start | bytes 786440 | tf_op jit(solution)/shard_map/ppermute | solution.py:161
  61.4 3.5 %aggregate_tiles.4 = (bf16[256,512]{1,0:T(8,128)(2,1)S(1)}, bf16[256,512]{1,0:T(8,128)(2,1)S(1)}, bf16[256,512]{1,0:T(8,128)(2,1)S(1)}, bf16[256,512]{1,0:T(8,128)(2,1)S(1)}, bf16[256,512]{1,0:T(8,128)(2,1)S(1)}) custom-call(s32[4]{0:T(128)S(1)} %pad_add_fusion.here_ref, s32[32]{0:T(128)S(1)} %bitcast.10, s32[64]{0:T(128)S(1)} %reshape.15.index_ref, ...), custom_call_target="tpu_custom_call" | custom-call | tf_op jit(solution)/shard_map/aggregate_tiles/pallas_call | solution.py:54
  65.2 2.7 %collective-permute-start.11 = (bf16[256,512]{1,0:T(8,128)(2,1)S(1)}, bf16[256,512]{1,0:T(8,128)(2,1)S(1)}, u32[]{:S(2)}, u32[]{:S(2)}) collective-permute-start(bf16[256,512]{1,0:T(8,128)(2,1)S(1)} %get-tuple-element.47), channel_id=1, source_target_pairs={{0,7},{1,0},{2,1},{3,2},{4,3},{5,4},{6,5},{7,6},{8,15},{9,8},{10,9... | collective-permute-start | bytes 786440 | tf_op jit(solution)/shard_map/ppermute | solution.py:161
  68.3 2.0 %collective-permute-done.15 = bf16[256,512]{1,0:T(8,128)(2,1)S(1)} collective-permute-done((bf16[256,512]{1,0:T(8,128)(2,1)S(1)}, bf16[256,512]{1,0:T(8,128)(2,1)S(1)}, u32[]{:S(2)}, u32[]{:S(2)}) %collective-permute-start.15) | collective-permute-done | bytes 262176 | tf_op jit(solution)/shard_map/ppermute | solution.py:161
  70.5 1.7 %collective-permute-start.17 = (bf16[256,512]{1,0:T(8,128)(2,1)S(1)}, bf16[256,512]{1,0:T(8,128)(2,1)S(1)}, u32[]{:S(2)}, u32[]{:S(2)}) collective-permute-start(bf16[256,512]{1,0:T(8,128)(2,1)S(1)} %pad_maximum_fusion.2), channel_id=1, source_target_pairs={{0,6},{1,7},{2,0},{3,1},{4,2},{5,3},{6,4},{7,5},{8,14},{9,15},{10,... | collective-permute-start | bytes 786440 | tf_op jit(solution)/shard_map/ppermute | solution.py:161
  72.4 2.2 %collective-permute-done.10.refs_2_ = bf16[256,512]{1,0:T(8,128)(2,1)S(1)} collective-permute-done((bf16[256,512]{1,0:T(8,128)(2,1)S(1)}, bf16[256,512]{1,0:T(8,128)(2,1)S(1)}, u32[]{:S(2)}, u32[]{:S(2)}) %collective-permute-start.10) | collective-permute-done | bytes 262176 | tf_op jit(solution)/shard_map/ppermute | solution.py:161
  74.5 1.4 collective-permute-done.11.refs_3_
  75.9 10.2 %collective-permute-done.14.refs_4_ = bf16[256,512]{1,0:T(8,128)(2,1)S(1)} collective-permute-done((bf16[256,512]{1,0:T(8,128)(2,1)S(1)}, bf16[256,512]{1,0:T(8,128)(2,1)S(1)}, u32[]{:S(2)}, u32[]{:S(2)}) %collective-permute-start.14) | collective-permute-done | bytes 262176 | tf_op jit(solution)/shard_map/ppermute | solution.py:161
  86.1 1.0 collective-permute-done.17.refs_5_
  87.1 2.0 %node_mlp.2.refs_0_ = bf16[256,512]{1,0:T(8,128)(2,1)S(1)} custom-call(f32[2,256,512]{2,1,0:T(8,128)S(1)} %broadcast_multiply_fusion.scale_ref, bf16[256,512]{1,0:T(8,128)(2,1)S(1)} %convolution_convert_fusion.shift_ref, bf16[2,512,2048]{2,1,0:T(8,128)(2,1)S(1)} %copy-done.1, bf16[2,2048,512]{2,1,0:T(8,128)(2,1)S(1)} %copy-done.2, ...), custom_call_target="tpu_custom_call" | custom-call | tf_op jit(solution)/shard_map/node_mlp/pallas_call | solution.py:102
  89.1 1.8 %collective-permute-start.20 = (bf16[256,512]{1,0:T(8,128)(2,1)S(1)}, bf16[256,512]{1,0:T(8,128)(2,1)S(1)}, u32[]{:S(2)}, u32[]{:S(2)}) collective-permute-start(bf16[256,512]{1,0:T(8,128)(2,1)S(1)} %node_mlp.2.refs_0_), channel_id=1, source_target_pairs={{128,0},{40,8},{144,16},{56,24},{160,32},{8,40},{176,48},{24,56},{... | collective-permute-start | bytes 786440 | tf_op jit(solution)/shard_map/ppermute | solution.py:142
  91.0 1.2 collective-permute-start.19
  92.1 1.5 collective-permute-start.18
  93.6 2.6 %collective-permute-done.20 = bf16[256,512]{1,0:T(8,128)(2,1)S(1)} collective-permute-done((bf16[256,512]{1,0:T(8,128)(2,1)S(1)}, bf16[256,512]{1,0:T(8,128)(2,1)S(1)}, u32[]{:S(2)}, u32[]{:S(2)}) %collective-permute-start.20) | collective-permute-done | bytes 262176 | tf_op jit(solution)/shard_map/ppermute | solution.py:142
  96.2 2.8 %collective-permute-done.19 = bf16[256,512]{1,0:T(8,128)(2,1)S(1)} collective-permute-done((bf16[256,512]{1,0:T(8,128)(2,1)S(1)}, bf16[256,512]{1,0:T(8,128)(2,1)S(1)}, u32[]{:S(2)}, u32[]{:S(2)}) %collective-permute-start.19) | collective-permute-done | bytes 262176 | tf_op jit(solution)/shard_map/ppermute | solution.py:142
  99.1 1.7 %collective-permute-start.24 = (bf16[1024,512]{1,0:T(8,128)(2,1)S(1)}, bf16[1024,512]{1,0:T(8,128)(2,1)S(1)}, u32[]{:S(2)}, u32[]{:S(2)}) collective-permute-start(bf16[1024,512]{1,0:T(8,128)(2,1)S(1)} %pad_maximum_fusion.refs_0_), channel_id=1, source_target_pairs={{0,8},{8,0},{16,24},{24,16},{32,40},{40,32},{48,56},{56,48},{64,72... | collective-permute-start | bytes 3145736 | tf_op jit(solution)/shard_map/ppermute | solution.py:147
  100.8 1.0 collective-permute-start.23
  101.8 0.7 collective-permute-start.22
  102.5 2.0 %collective-permute-start.21 = (bf16[1024,512]{1,0:T(8,128)(2,1)S(1)}, bf16[1024,512]{1,0:T(8,128)(2,1)S(1)}, u32[]{:S(2)}, u32[]{:S(2)}) collective-permute-start(bf16[1024,512]{1,0:T(8,128)(2,1)S(1)} %pad_maximum_fusion.refs_0_), channel_id=1, source_target_pairs={{16,0},{72,8},{32,16},{88,24},{48,32},{104,40},{0,48},{120,56},{80... | collective-permute-start | bytes 3145736 | tf_op jit(solution)/shard_map/ppermute | solution.py:142
  104.5 11.9 %collective-permute-done.23.refs_3_ = bf16[1024,512]{1,0:T(8,128)(2,1)S(1)} collective-permute-done((bf16[1024,512]{1,0:T(8,128)(2,1)S(1)}, bf16[1024,512]{1,0:T(8,128)(2,1)S(1)}, u32[]{:S(2)}, u32[]{:S(2)}) %collective-permute-start.23) | collective-permute-done | bytes 1048608 | tf_op jit(solution)/shard_map/ppermute | solution.py:142
  116.3 11.2 %collective-permute-done.22.refs_2_ = bf16[1024,512]{1,0:T(8,128)(2,1)S(1)} collective-permute-done((bf16[1024,512]{1,0:T(8,128)(2,1)S(1)}, bf16[1024,512]{1,0:T(8,128)(2,1)S(1)}, u32[]{:S(2)}, u32[]{:S(2)}) %collective-permute-start.22) | collective-permute-done | bytes 1048608 | tf_op jit(solution)/shard_map/ppermute | solution.py:142
  127.5 1.0 collective-permute-start.25
  128.5 0.5 collective-permute-start.27
  129.0 1.8 %collective-permute-done.25.refs_5_ = bf16[1024,512]{1,0:T(8,128)(2,1)S(1)} collective-permute-done((bf16[1024,512]{1,0:T(8,128)(2,1)S(1)}, bf16[1024,512]{1,0:T(8,128)(2,1)S(1)}, u32[]{:S(2)}, u32[]{:S(2)}) %collective-permute-start.25) | collective-permute-done | bytes 1048608 | tf_op jit(solution)/shard_map/ppermute | solution.py:147
  130.8 1.5 collective-permute-done.26.refs_6_
  132.3 1.5 collective-permute-done.27.refs_7_
  133.8 1.5 aggregate_tiles.7
  135.3 0.7 collective-permute-start.30
  136.0 4.0 %collective-permute-start.34 = (bf16[128,512]{1,0:T(8,128)(2,1)S(1)}, bf16[128,512]{1,0:T(8,128)(2,1)S(1)}, u32[]{:S(2)}, u32[]{:S(2)}) collective-permute-start(bf16[128,512]{1,0:T(8,128)(2,1)S(1)} %get-tuple-element.69), channel_id=1, source_target_pairs={{0,6},{1,7},{2,0},{3,1},{4,2},{5,3},{6,4},{7,5},{8,14},{9,15},{10,... | collective-permute-start | bytes 393224 | tf_op jit(solution)/shard_map/ppermute | solution.py:161
  140.0 0.3 collective-permute-start.31
  140.3 1.6 collective-permute-start.33
  141.9 1.8 %aggregate_tiles.6 = (bf16[256,512]{1,0:T(8,128)(2,1)S(1)}, bf16[256,512]{1,0:T(8,128)(2,1)S(1)}, bf16[256,512]{1,0:T(8,128)(2,1)S(1)}, bf16[256,512]{1,0:T(8,128)(2,1)S(1)}, bf16[256,512]{1,0:T(8,128)(2,1)S(1)}) custom-call(s32[4]{0:T(128)S(1)} %pad_add_fusion.here_ref, s32[32]{0:T(128)S(1)} %bitcast.12, s32[64]{0:T(128)S(1)} %reshape.15.index_ref, ...), custom_call_target="tpu_custom_call" | custom-call | tf_op jit(solution)/shard_map/aggregate_tiles/pallas_call | solution.py:54
  143.8 0.5 collective-permute-done.30
  144.3 2.2 %collective-permute-start.29 = (bf16[256,512]{1,0:T(8,128)(2,1)S(1)}, bf16[256,512]{1,0:T(8,128)(2,1)S(1)}, u32[]{:S(2)}, u32[]{:S(2)}) collective-permute-start(bf16[256,512]{1,0:T(8,128)(2,1)S(1)} %get-tuple-element.63), channel_id=1, source_target_pairs={{0,7},{1,0},{2,1},{3,2},{4,3},{5,4},{6,5},{7,6},{8,15},{9,8},{10,9... | collective-permute-start | bytes 786440 | tf_op jit(solution)/shard_map/ppermute | solution.py:161
  146.6 2.6 %collective-permute-done.31 = bf16[128,512]{1,0:T(8,128)(2,1)S(1)} collective-permute-done((bf16[128,512]{1,0:T(8,128)(2,1)S(1)}, bf16[128,512]{1,0:T(8,128)(2,1)S(1)}, u32[]{:S(2)}, u32[]{:S(2)}) %collective-permute-start.31) | collective-permute-done | bytes 131104 | tf_op jit(solution)/shard_map/ppermute | solution.py:161
  149.4 1.8 %collective-permute-done.33 = bf16[256,512]{1,0:T(8,128)(2,1)S(1)} collective-permute-done((bf16[256,512]{1,0:T(8,128)(2,1)S(1)}, bf16[256,512]{1,0:T(8,128)(2,1)S(1)}, u32[]{:S(2)}, u32[]{:S(2)}) %collective-permute-start.33) | collective-permute-done | bytes 262176 | tf_op jit(solution)/shard_map/ppermute | solution.py:161
  151.4 3.2 %collective-permute-start.35 = (bf16[256,512]{1,0:T(8,128)(2,1)S(1)}, bf16[256,512]{1,0:T(8,128)(2,1)S(1)}, u32[]{:S(2)}, u32[]{:S(2)}) collective-permute-start(bf16[256,512]{1,0:T(8,128)(2,1)S(1)} %pad_maximum_fusion.4), channel_id=1, source_target_pairs={{0,6},{1,7},{2,0},{3,1},{4,2},{5,3},{6,4},{7,5},{8,14},{9,15},{10,... | collective-permute-start | bytes 786440 | tf_op jit(solution)/shard_map/ppermute | solution.py:161
  154.6 0.9 collective-permute-done.28.refs_2_
  155.5 1.3 collective-permute-done.29.refs_3_
  156.8 7.2 %collective-permute-done.32.refs_4_ = bf16[256,512]{1,0:T(8,128)(2,1)S(1)} collective-permute-done((bf16[256,512]{1,0:T(8,128)(2,1)S(1)}, bf16[256,512]{1,0:T(8,128)(2,1)S(1)}, u32[]{:S(2)}, u32[]{:S(2)}) %collective-permute-start.32) | collective-permute-done | bytes 262176 | tf_op jit(solution)/shard_map/ppermute | solution.py:161
  164.0 5.2 %collective-permute-done.35.refs_5_ = bf16[256,512]{1,0:T(8,128)(2,1)S(1)} collective-permute-done((bf16[256,512]{1,0:T(8,128)(2,1)S(1)}, bf16[256,512]{1,0:T(8,128)(2,1)S(1)}, u32[]{:S(2)}, u32[]{:S(2)}) %collective-permute-start.35) | collective-permute-done | bytes 262176 | tf_op jit(solution)/shard_map/ppermute | solution.py:161
  169.2 2.6 %node_mlp.3 = bf16[256,512]{1,0:T(8,128)(2,1)} custom-call(f32[2,256,512]{2,1,0:T(8,128)S(1)} %broadcast_multiply_fusion.scale_ref, bf16[256,512]{1,0:T(8,128)(2,1)S(1)} %convolution_convert_fusion.shift_ref, bf16[2,512,2048]{2,1,0:T(8,128)(2,1)S(1)} %copy-done.1, bf16[2,2048,512]{2,1,0:T(8,128)(2,1)S(1)} %copy-done.2, ...), custom_call_target="tpu_custom_call" | custom-call | tf_op jit(solution)/shard_map/node_mlp/pallas_call | solution.py:102
  (64 shorter events, 1.8 us)
Async XLA Ops:
  0.0 53.5 %copy-start = (bf16[128,512]{1,0:T(8,128)(2,1)S(1)}, bf16[128,512]{1,0:T(8,128)(2,1)}, u32[]{:S(2)}) copy-start(bf16[128,512]{1,0:T(8,128)(2,1)} %param.17) | copy-start | bytes 393220
  0.0 18.7 %copy-start.7 = (s32[16,1,4]{0,2,1:T(4,128)S(1)}, s32[16,1,4]{0,2,1:T(4,128)}, u32[]{:S(2)}) copy-start(s32[16,1,4]{0,2,1:T(4,128)} %param.13) | copy-start | bytes 772
  0.0 7.2 %collective-permute-start = (bf16[256,512]{1,0:T(8,128)(2,1)}, bf16[256,512]{1,0:T(8,128)(2,1)S(1)}, u32[]{:S(2)}, u32[]{:S(2)}) collective-permute-start(bf16[256,512]{1,0:T(8,128)(2,1)} %refs_0_.1), channel_id=1, source_target_pairs={{64,0},{24,8},{80,16},{40,24},{96,32},{56,40},{112,48},{8,56},{128... | collective-permute-start | bytes 786440 | tf_op jit(solution)/shard_map/ppermute | solution.py:142
  3.6 9.7 %collective-permute-start.1 = (bf16[256,512]{1,0:T(8,128)(2,1)}, bf16[256,512]{1,0:T(8,128)(2,1)S(1)}, u32[]{:S(2)}, u32[]{:S(2)}) collective-permute-start(bf16[256,512]{1,0:T(8,128)(2,1)} %refs_0_.1), channel_id=1, source_target_pairs={{192,0},{56,8},{208,16},{8,24},{224,32},{24,40},{240,48},{40,56},{... | collective-permute-start | bytes 786440 | tf_op jit(solution)/shard_map/ppermute | solution.py:142
  3.6 9.8 %collective-permute-start.2 = (bf16[256,512]{1,0:T(8,128)(2,1)}, bf16[256,512]{1,0:T(8,128)(2,1)S(1)}, u32[]{:S(2)}, u32[]{:S(2)}) collective-permute-start(bf16[256,512]{1,0:T(8,128)(2,1)} %refs_0_.1), channel_id=1, source_target_pairs={{128,0},{40,8},{144,16},{56,24},{160,32},{8,40},{176,48},{24,56},{... | collective-permute-start | bytes 786440 | tf_op jit(solution)/shard_map/ppermute | solution.py:142
  13.4 8.4 %collective-permute-start.6 = (bf16[1024,512]{1,0:T(8,128)(2,1)S(1)}, bf16[1024,512]{1,0:T(8,128)(2,1)}, u32[]{:S(2)}, u32[]{:S(2)}) collective-permute-start(bf16[1024,512]{1,0:T(8,128)(2,1)S(1)} %constant_dynamic-update-slice_fusion.refs_0_), channel_id=1, source_target_pairs={{0,8},{8,0},{16,24},{24,16},{32,40},{40,32},{48,56},{56,48},{64,72... | collective-permute-start | bytes 3145736 | tf_op jit(solution)/shard_map/ppermute | solution.py:147
  15.0 15.6 %collective-permute-start.5 = (bf16[1024,512]{1,0:T(8,128)(2,1)S(1)}, bf16[1024,512]{1,0:T(8,128)(2,1)}, u32[]{:S(2)}, u32[]{:S(2)}) collective-permute-start(bf16[1024,512]{1,0:T(8,128)(2,1)S(1)} %constant_dynamic-update-slice_fusion.refs_0_), channel_id=1, source_target_pairs={{32,0},{136,8},{48,16},{152,24},{0,32},{168,40},{16,48},{184,56},{... | collective-permute-start | bytes 3145736 | tf_op jit(solution)/shard_map/ppermute | solution.py:142
  16.0 25.8 %collective-permute-start.4 = (bf16[1024,512]{1,0:T(8,128)(2,1)S(1)}, bf16[1024,512]{1,0:T(8,128)(2,1)}, u32[]{:S(2)}, u32[]{:S(2)}) collective-permute-start(bf16[1024,512]{1,0:T(8,128)(2,1)S(1)} %constant_dynamic-update-slice_fusion.refs_0_), channel_id=1, source_target_pairs={{48,0},{200,8},{0,16},{216,24},{16,32},{232,40},{32,48},{248,56},{... | collective-permute-start | bytes 3145736 | tf_op jit(solution)/shard_map/ppermute | solution.py:142
  16.3 25.5 %collective-permute-start.3 = (bf16[1024,512]{1,0:T(8,128)(2,1)S(1)}, bf16[1024,512]{1,0:T(8,128)(2,1)}, u32[]{:S(2)}, u32[]{:S(2)}) collective-permute-start(bf16[1024,512]{1,0:T(8,128)(2,1)S(1)} %constant_dynamic-update-slice_fusion.refs_0_), channel_id=1, source_target_pairs={{16,0},{72,8},{32,16},{88,24},{48,32},{104,40},{0,48},{120,56},{80... | collective-permute-start | bytes 3145736 | tf_op jit(solution)/shard_map/ppermute | solution.py:142
  18.9 24.8 %copy-start.5 = (bf16[16,512]{1,0:T(8,128)(2,1)S(1)}, bf16[16,512]{1,0:T(8,128)(2,1)}, u32[]{:S(2)}) copy-start(bf16[16,512]{1,0:T(8,128)(2,1)} %param.18) | copy-start | bytes 49156
  18.9 24.8 %copy-start.8 = (s32[256]{0:T(256)S(1)}, s32[256]{0:T(256)}, u32[]{:S(2)}) copy-start(s32[256]{0:T(256)} %param.16) | copy-start | bytes 3076
  18.9 29.8 %copy-start.4 = (s32[1,1,32,1]{2,3,1,0:T(1,128)S(1)}, s32[1,1,32,1]{2,3,1,0:T(1,128)}, u32[]{:S(2)}) copy-start(s32[1,1,32,1]{2,3,1,0:T(1,128)} %param.14) | copy-start | bytes 388
  41.8 3.8 %collective-permute-start.7 = (bf16[1024,512]{1,0:T(8,128)(2,1)}, bf16[1024,512]{1,0:T(8,128)(2,1)S(1)}, u32[]{:S(2)}, u32[]{:S(2)}) collective-permute-start(bf16[1024,512]{1,0:T(8,128)(2,1)} %collective-permute-done.3.refs_1_), channel_id=1, source_target_pairs={{0,8},{8,0},{16,24},{24,16},{32,40},{40,32},{48,56},{56,48},{64,72... | collective-permute-start | bytes 3145736 | tf_op jit(solution)/shard_map/ppermute | solution.py:147
  43.1 4.0 %collective-permute-start.8 = (bf16[1024,512]{1,0:T(8,128)(2,1)}, bf16[1024,512]{1,0:T(8,128)(2,1)S(1)}, u32[]{:S(2)}, u32[]{:S(2)}) collective-permute-start(bf16[1024,512]{1,0:T(8,128)(2,1)} %collective-permute-done.4.refs_2_), channel_id=1, source_target_pairs={{0,8},{8,0},{16,24},{24,16},{32,40},{40,32},{48,56},{56,48},{64,72... | collective-permute-start | bytes 3145736 | tf_op jit(solution)/shard_map/ppermute | solution.py:147
  43.2 5.5 %collective-permute-start.9 = (bf16[1024,512]{1,0:T(8,128)(2,1)}, bf16[1024,512]{1,0:T(8,128)(2,1)S(1)}, u32[]{:S(2)}, u32[]{:S(2)}) collective-permute-start(bf16[1024,512]{1,0:T(8,128)(2,1)} %collective-permute-done.5.refs_3_), channel_id=1, source_target_pairs={{0,8},{8,0},{16,24},{24,16},{32,40},{40,32},{48,56},{56,48},{64,72... | collective-permute-start | bytes 3145736 | tf_op jit(solution)/shard_map/ppermute | solution.py:147
  43.9 9.5 %copy-start.9 = (s32[256]{0:T(256)S(1)}, s32[256]{0:T(256)}, u32[]{:S(2)}) copy-start(s32[256]{0:T(256)} %param.15) | copy-start | bytes 3076
  51.8 13.5 %collective-permute-start.12 = (bf16[256,512]{1,0:T(8,128)(2,1)S(1)}, bf16[256,512]{1,0:T(8,128)(2,1)S(1)}, u32[]{:S(2)}, u32[]{:S(2)}) collective-permute-start(bf16[256,512]{1,0:T(8,128)(2,1)S(1)} %get-tuple-element.49), channel_id=1, source_target_pairs={{0,1},{1,2},{2,3},{3,4},{4,5},{5,6},{6,7},{7,0},{8,9},{9,10},{10,1... | collective-permute-start | bytes 786440 | tf_op jit(solution)/shard_map/ppermute | solution.py:161
  53.8 16.6 %collective-permute-start.16 = (bf16[128,512]{1,0:T(8,128)(2,1)S(1)}, bf16[128,512]{1,0:T(8,128)(2,1)S(1)}, u32[]{:S(2)}, u32[]{:S(2)}) collective-permute-start(bf16[128,512]{1,0:T(8,128)(2,1)S(1)} %get-tuple-element.71), channel_id=1, source_target_pairs={{0,6},{1,7},{2,0},{3,1},{4,2},{5,3},{6,4},{7,5},{8,14},{9,15},{10,... | collective-permute-start | bytes 393224 | tf_op jit(solution)/shard_map/ppermute | solution.py:161
  59.0 9.1 %collective-permute-start.13 = (bf16[128,512]{1,0:T(8,128)(2,1)S(1)}, bf16[128,512]{1,0:T(8,128)(2,1)S(1)}, u32[]{:S(2)}, u32[]{:S(2)}) collective-permute-start(bf16[128,512]{1,0:T(8,128)(2,1)S(1)} %get-tuple-element.72), channel_id=1, source_target_pairs={{0,2},{1,3},{2,4},{3,5},{4,6},{5,7},{6,0},{7,1},{8,10},{9,11},{10,... | collective-permute-start | bytes 393224 | tf_op jit(solution)/shard_map/ppermute | solution.py:161
  59.0 11.3 %collective-permute-start.15 = (bf16[256,512]{1,0:T(8,128)(2,1)S(1)}, bf16[256,512]{1,0:T(8,128)(2,1)S(1)}, u32[]{:S(2)}, u32[]{:S(2)}) collective-permute-start(bf16[256,512]{1,0:T(8,128)(2,1)S(1)} %get-tuple-element.52), channel_id=1, source_target_pairs={{0,7},{1,0},{2,1},{3,2},{4,3},{5,4},{6,5},{7,6},{8,15},{9,8},{10,9... | collective-permute-start | bytes 786440 | tf_op jit(solution)/shard_map/ppermute | solution.py:161
  61.4 25.7 %copy-start.2 = (bf16[2,2048,512]{2,1,0:T(8,128)(2,1)S(1)}, bf16[2,2048,512]{2,1,0:T(8,128)(2,1)}, u32[]{:S(2)}) copy-start(bf16[2,2048,512]{2,1,0:T(8,128)(2,1)} %w_out_ref.3) | copy-start | bytes 12582916
  64.9 9.6 %collective-permute-start.10 = (bf16[256,512]{1,0:T(8,128)(2,1)S(1)}, bf16[256,512]{1,0:T(8,128)(2,1)S(1)}, u32[]{:S(2)}, u32[]{:S(2)}) collective-permute-start(bf16[256,512]{1,0:T(8,128)(2,1)S(1)} %get-tuple-element.46), channel_id=1, source_target_pairs={{0,1},{1,2},{2,3},{3,4},{4,5},{5,6},{6,7},{7,0},{8,9},{9,10},{10,1... | collective-permute-start | bytes 786440 | tf_op jit(solution)/shard_map/ppermute | solution.py:161
  65.2 10.7 %collective-permute-start.11 = (bf16[256,512]{1,0:T(8,128)(2,1)S(1)}, bf16[256,512]{1,0:T(8,128)(2,1)S(1)}, u32[]{:S(2)}, u32[]{:S(2)}) collective-permute-start(bf16[256,512]{1,0:T(8,128)(2,1)S(1)} %get-tuple-element.47), channel_id=1, source_target_pairs={{0,7},{1,0},{2,1},{3,2},{4,3},{5,4},{6,5},{7,6},{8,15},{9,8},{10,9... | collective-permute-start | bytes 786440 | tf_op jit(solution)/shard_map/ppermute | solution.py:161
  68.0 4.3 %copy-start.6 = (f32[2,512]{1,0:T(2,128)S(1)}, f32[2,512]{1,0:T(2,128)}, u32[]{:S(2)}) copy-start(f32[2,512]{1,0:T(2,128)} %param.19) | copy-start | bytes 12292
  68.1 19.0 %copy-start.1 = (bf16[2,512,2048]{2,1,0:T(8,128)(2,1)S(1)}, bf16[2,512,2048]{2,1,0:T(8,128)(2,1)}, u32[]{:S(2)}) copy-start(bf16[2,512,2048]{2,1,0:T(8,128)(2,1)} %w_in_ref.3) | copy-start | bytes 12582916
  68.2 19.0 %copy-start.3 = (bf16[256,512]{1,0:T(8,128)(2,1)S(1)}, bf16[256,512]{1,0:T(8,128)(2,1)}, u32[]{:S(2)}) copy-start(bf16[256,512]{1,0:T(8,128)(2,1)} %refs_0_.1) | copy-start | bytes 786436
  68.2 17.9 %collective-permute-start.14 = (bf16[256,512]{1,0:T(8,128)(2,1)S(1)}, bf16[256,512]{1,0:T(8,128)(2,1)S(1)}, u32[]{:S(2)}, u32[]{:S(2)}) collective-permute-start(bf16[256,512]{1,0:T(8,128)(2,1)S(1)} %pad_maximum_fusion.1), channel_id=1, source_target_pairs={{0,2},{1,3},{2,4},{3,5},{4,6},{5,7},{6,0},{7,1},{8,10},{9,11},{10,... | collective-permute-start | bytes 786440 | tf_op jit(solution)/shard_map/ppermute | solution.py:161
  70.5 16.7 %collective-permute-start.17 = (bf16[256,512]{1,0:T(8,128)(2,1)S(1)}, bf16[256,512]{1,0:T(8,128)(2,1)S(1)}, u32[]{:S(2)}, u32[]{:S(2)}) collective-permute-start(bf16[256,512]{1,0:T(8,128)(2,1)S(1)} %pad_maximum_fusion.2), channel_id=1, source_target_pairs={{0,6},{1,7},{2,0},{3,1},{4,2},{5,3},{6,4},{7,5},{8,14},{9,15},{10,... | collective-permute-start | bytes 786440 | tf_op jit(solution)/shard_map/ppermute | solution.py:161
  89.1 7.1 %collective-permute-start.20 = (bf16[256,512]{1,0:T(8,128)(2,1)S(1)}, bf16[256,512]{1,0:T(8,128)(2,1)S(1)}, u32[]{:S(2)}, u32[]{:S(2)}) collective-permute-start(bf16[256,512]{1,0:T(8,128)(2,1)S(1)} %node_mlp.2.refs_0_), channel_id=1, source_target_pairs={{128,0},{40,8},{144,16},{56,24},{160,32},{8,40},{176,48},{24,56},{... | collective-permute-start | bytes 786440 | tf_op jit(solution)/shard_map/ppermute | solution.py:142
  91.0 8.1 %collective-permute-start.19 = (bf16[256,512]{1,0:T(8,128)(2,1)S(1)}, bf16[256,512]{1,0:T(8,128)(2,1)S(1)}, u32[]{:S(2)}, u32[]{:S(2)}) collective-permute-start(bf16[256,512]{1,0:T(8,128)(2,1)S(1)} %node_mlp.2.refs_0_), channel_id=1, source_target_pairs={{192,0},{56,8},{208,16},{8,24},{224,32},{24,40},{240,48},{40,56},{... | collective-permute-start | bytes 786440 | tf_op jit(solution)/shard_map/ppermute | solution.py:142
  92.1 6.9 %collective-permute-start.18 = (bf16[256,512]{1,0:T(8,128)(2,1)S(1)}, bf16[256,512]{1,0:T(8,128)(2,1)S(1)}, u32[]{:S(2)}, u32[]{:S(2)}) collective-permute-start(bf16[256,512]{1,0:T(8,128)(2,1)S(1)} %node_mlp.2.refs_0_), channel_id=1, source_target_pairs={{64,0},{24,8},{80,16},{40,24},{96,32},{56,40},{112,48},{8,56},{128... | collective-permute-start | bytes 786440 | tf_op jit(solution)/shard_map/ppermute | solution.py:142
  99.1 5.4 %collective-permute-start.24 = (bf16[1024,512]{1,0:T(8,128)(2,1)S(1)}, bf16[1024,512]{1,0:T(8,128)(2,1)S(1)}, u32[]{:S(2)}, u32[]{:S(2)}) collective-permute-start(bf16[1024,512]{1,0:T(8,128)(2,1)S(1)} %pad_maximum_fusion.refs_0_), channel_id=1, source_target_pairs={{0,8},{8,0},{16,24},{24,16},{32,40},{40,32},{48,56},{56,48},{64,72... | collective-permute-start | bytes 3145736 | tf_op jit(solution)/shard_map/ppermute | solution.py:147
  100.8 15.5 %collective-permute-start.23 = (bf16[1024,512]{1,0:T(8,128)(2,1)S(1)}, bf16[1024,512]{1,0:T(8,128)(2,1)S(1)}, u32[]{:S(2)}, u32[]{:S(2)}) collective-permute-start(bf16[1024,512]{1,0:T(8,128)(2,1)S(1)} %pad_maximum_fusion.refs_0_), channel_id=1, source_target_pairs={{32,0},{136,8},{48,16},{152,24},{0,32},{168,40},{16,48},{184,56},{... | collective-permute-start | bytes 3145736 | tf_op jit(solution)/shard_map/ppermute | solution.py:142
  101.8 25.7 %collective-permute-start.22 = (bf16[1024,512]{1,0:T(8,128)(2,1)S(1)}, bf16[1024,512]{1,0:T(8,128)(2,1)S(1)}, u32[]{:S(2)}, u32[]{:S(2)}) collective-permute-start(bf16[1024,512]{1,0:T(8,128)(2,1)S(1)} %pad_maximum_fusion.refs_0_), channel_id=1, source_target_pairs={{48,0},{200,8},{0,16},{216,24},{16,32},{232,40},{32,48},{248,56},{... | collective-permute-start | bytes 3145736 | tf_op jit(solution)/shard_map/ppermute | solution.py:142
  102.5 25.0 %collective-permute-start.21 = (bf16[1024,512]{1,0:T(8,128)(2,1)S(1)}, bf16[1024,512]{1,0:T(8,128)(2,1)S(1)}, u32[]{:S(2)}, u32[]{:S(2)}) collective-permute-start(bf16[1024,512]{1,0:T(8,128)(2,1)S(1)} %pad_maximum_fusion.refs_0_), channel_id=1, source_target_pairs={{16,0},{72,8},{32,16},{88,24},{48,32},{104,40},{0,48},{120,56},{80... | collective-permute-start | bytes 3145736 | tf_op jit(solution)/shard_map/ppermute | solution.py:142
  127.5 3.2 %collective-permute-start.25 = (bf16[1024,512]{1,0:T(8,128)(2,1)S(1)}, bf16[1024,512]{1,0:T(8,128)(2,1)S(1)}, u32[]{:S(2)}, u32[]{:S(2)}) collective-permute-start(bf16[1024,512]{1,0:T(8,128)(2,1)S(1)} %collective-permute-done.21.refs_1_), channel_id=1, source_target_pairs={{0,8},{8,0},{16,24},{24,16},{32,40},{40,32},{48,56},{56,48},{64,72... | collective-permute-start | bytes 3145736 | tf_op jit(solution)/shard_map/ppermute | solution.py:147
  128.5 3.8 %collective-permute-start.26 = (bf16[1024,512]{1,0:T(8,128)(2,1)S(1)}, bf16[1024,512]{1,0:T(8,128)(2,1)S(1)}, u32[]{:S(2)}, u32[]{:S(2)}) collective-permute-start(bf16[1024,512]{1,0:T(8,128)(2,1)S(1)} %collective-permute-done.22.refs_2_), channel_id=1, source_target_pairs={{0,8},{8,0},{16,24},{24,16},{32,40},{40,32},{48,56},{56,48},{64,72... | collective-permute-start | bytes 3145736 | tf_op jit(solution)/shard_map/ppermute | solution.py:147
  128.5 5.3 %collective-permute-start.27 = (bf16[1024,512]{1,0:T(8,128)(2,1)S(1)}, bf16[1024,512]{1,0:T(8,128)(2,1)S(1)}, u32[]{:S(2)}, u32[]{:S(2)}) collective-permute-start(bf16[1024,512]{1,0:T(8,128)(2,1)S(1)} %collective-permute-done.23.refs_3_), channel_id=1, source_target_pairs={{0,8},{8,0},{16,24},{24,16},{32,40},{40,32},{48,56},{56,48},{64,72... | collective-permute-start | bytes 3145736 | tf_op jit(solution)/shard_map/ppermute | solution.py:147
  135.3 9.0 %collective-permute-start.30 = (bf16[256,512]{1,0:T(8,128)(2,1)S(1)}, bf16[256,512]{1,0:T(8,128)(2,1)S(1)}, u32[]{:S(2)}, u32[]{:S(2)}) collective-permute-start(bf16[256,512]{1,0:T(8,128)(2,1)S(1)} %get-tuple-element.65), channel_id=1, source_target_pairs={{0,1},{1,2},{2,3},{3,4},{4,5},{5,6},{6,7},{7,0},{8,9},{9,10},{10,1... | collective-permute-start | bytes 786440 | tf_op jit(solution)/shard_map/ppermute | solution.py:161
  136.0 15.3 %collective-permute-start.34 = (bf16[128,512]{1,0:T(8,128)(2,1)S(1)}, bf16[128,512]{1,0:T(8,128)(2,1)S(1)}, u32[]{:S(2)}, u32[]{:S(2)}) collective-permute-start(bf16[128,512]{1,0:T(8,128)(2,1)S(1)} %get-tuple-element.69), channel_id=1, source_target_pairs={{0,6},{1,7},{2,0},{3,1},{4,2},{5,3},{6,4},{7,5},{8,14},{9,15},{10,... | collective-permute-start | bytes 393224 | tf_op jit(solution)/shard_map/ppermute | solution.py:161
  140.0 9.3 %collective-permute-start.31 = (bf16[128,512]{1,0:T(8,128)(2,1)S(1)}, bf16[128,512]{1,0:T(8,128)(2,1)S(1)}, u32[]{:S(2)}, u32[]{:S(2)}) collective-permute-start(bf16[128,512]{1,0:T(8,128)(2,1)S(1)} %get-tuple-element.70), channel_id=1, source_target_pairs={{0,2},{1,3},{2,4},{3,5},{4,6},{5,7},{6,0},{7,1},{8,10},{9,11},{10,... | collective-permute-start | bytes 393224 | tf_op jit(solution)/shard_map/ppermute | solution.py:161
  140.3 10.9 %collective-permute-start.33 = (bf16[256,512]{1,0:T(8,128)(2,1)S(1)}, bf16[256,512]{1,0:T(8,128)(2,1)S(1)}, u32[]{:S(2)}, u32[]{:S(2)}) collective-permute-start(bf16[256,512]{1,0:T(8,128)(2,1)S(1)} %get-tuple-element.68), channel_id=1, source_target_pairs={{0,7},{1,0},{2,1},{3,2},{4,3},{5,4},{6,5},{7,6},{8,15},{9,8},{10,9... | collective-permute-start | bytes 786440 | tf_op jit(solution)/shard_map/ppermute | solution.py:161
  143.7 11.9 %collective-permute-start.28 = (bf16[256,512]{1,0:T(8,128)(2,1)S(1)}, bf16[256,512]{1,0:T(8,128)(2,1)S(1)}, u32[]{:S(2)}, u32[]{:S(2)}) collective-permute-start(bf16[256,512]{1,0:T(8,128)(2,1)S(1)} %get-tuple-element.62), channel_id=1, source_target_pairs={{0,1},{1,2},{2,3},{3,4},{4,5},{5,6},{6,7},{7,0},{8,9},{9,10},{10,1... | collective-permute-start | bytes 786440 | tf_op jit(solution)/shard_map/ppermute | solution.py:161
  144.3 12.5 %collective-permute-start.29 = (bf16[256,512]{1,0:T(8,128)(2,1)S(1)}, bf16[256,512]{1,0:T(8,128)(2,1)S(1)}, u32[]{:S(2)}, u32[]{:S(2)}) collective-permute-start(bf16[256,512]{1,0:T(8,128)(2,1)S(1)} %get-tuple-element.63), channel_id=1, source_target_pairs={{0,7},{1,0},{2,1},{3,2},{4,3},{5,4},{6,5},{7,6},{8,15},{9,8},{10,9... | collective-permute-start | bytes 786440 | tf_op jit(solution)/shard_map/ppermute | solution.py:161
  149.3 14.7 %collective-permute-start.32 = (bf16[256,512]{1,0:T(8,128)(2,1)S(1)}, bf16[256,512]{1,0:T(8,128)(2,1)S(1)}, u32[]{:S(2)}, u32[]{:S(2)}) collective-permute-start(bf16[256,512]{1,0:T(8,128)(2,1)S(1)} %pad_maximum_fusion.3), channel_id=1, source_target_pairs={{0,2},{1,3},{2,4},{3,5},{4,6},{5,7},{6,0},{7,1},{8,10},{9,11},{10,... | collective-permute-start | bytes 786440 | tf_op jit(solution)/shard_map/ppermute | solution.py:161
  151.4 17.8 %collective-permute-start.35 = (bf16[256,512]{1,0:T(8,128)(2,1)S(1)}, bf16[256,512]{1,0:T(8,128)(2,1)S(1)}, u32[]{:S(2)}, u32[]{:S(2)}) collective-permute-start(bf16[256,512]{1,0:T(8,128)(2,1)S(1)} %pad_maximum_fusion.4), channel_id=1, source_target_pairs={{0,6},{1,7},{2,0},{3,1},{4,2},{5,3},{6,4},{7,5},{8,14},{9,15},{10,... | collective-permute-start | bytes 786440 | tf_op jit(solution)/shard_map/ppermute | solution.py:161

commit v4 on v3

--- a/solution.py
+++ b/solution.py
@@ -114,7 +114,9 @@
 
 
 def held_blocks():
-    offsets = [[(e, d) for e in (0, *NEAR)] for d in (0, *NEAR)]
+    line = (0, *NEAR)
+    offsets = [[(e, d) for e in line] for d in (0, 1, -1)]
+    offsets += [[(e, 2) for e in line[:2]], [(e, 2) for e in line[2:]]]
     count = len(offsets)
     return [
         (a + swapped * count, k, e, d, swapped)
@@ -150,10 +152,14 @@
 def gather_blocks(own, ready):
     after = lax.optimization_barrier
     line = jnp.concatenate([own] + [pull(own, True, e) for e in NEAR], axis=0)
-    far = [pull(line, False, d) for d in NEAR]
+    half = line.shape[0] // 2
+    far = [pull(line, False, d) for d in (1, -1)]
     first = swap(line)
-    far, first, ready = after((far, first, ready))
-    return [line] + far + [first] + [swap(v) for v in far], ready
+    if ready is not None:
+        far, first, ready = after((far, first, ready))
+    last = [pull(far[0][:half], False, 1), pull(far[1][half:], False, -1)]
+    arrays = [line] + far + last
+    return arrays + [first] + [swap(v) for v in far + last], ready
 
 
 def send(value, distance):
@@ -209,7 +215,9 @@
     ready = (matrix, wanted, slot_index, here)
     for layer in range(LAYERS):
         arrays, ready = gather_blocks(states[0], ready)
-        matrix, wanted, slot_index, here = ready
+        if ready is not None:
+            matrix, wanted, slot_index, here = ready
+            ready = None
         near = {}
         for group in SENT:
             products = aggregate_tiles(matrix, arrays, here, wanted, slot_index, group)

time: 172 us -> 166 us (0.965)
  waiting for transfers between devices: 101 us -> 78.8 us
  starting transfers between devices: 50.1 us -> 62.9 us
  local copies, waits for them, and re-layouts: 4.16 us -> 8.12 us
    ppermute x12 -> x14, waiting for transfers between devices: 55.6 us -> 40.8 us  [pull(): return lax.ppermute(value, 'row', pairs)]
    ppermute x8 -> x10, starting transfers between devices: 6.68 us -> 14.3 us  [swap(): return lax.ppermute(value, 'row', [(i, i ^ 1) for i in range(count)])]
    ppermute x8 -> x10, waiting for transfers between devices: 9.47 us -> 3.89 us  [swap(): return lax.ppermute(value, 'row', [(i, i ^ 1) for i in range(count)])]
    ppermute x12 -> x14, starting transfers between devices: 17 us -> 20 us  [pull(): return lax.ppermute(value, 'row', pairs)]
    ppermute x16, starting transfers between devices: 26.4 us -> 28.6 us  [send(): lax.ppermute(value, 'col', [(i, (i + distance) % count) for i in range(co...]
    ppermute x16, waiting for transfers between devices: 36.4 us -> 34.2 us  [send(): lax.ppermute(value, 'col', [(i, (i + distance) % count) for i in range(co...]
    unnamed x24, local copies, waits for them, and re-layouts: 1.17 us -> 3.27 us
  transfers between devices with their start and end apart: 36 -> 40, of which waited for: 27 -> 23; matrix products, arithmetic and copies ran while one was open for 3% -> 5% of each run, Pallas kernels for 3% -> 3%
where the time goes in v4:
time: 166 us; the launch traced here: 165 us
  waiting for transfers between devices  78.8 us (47%)
  starting transfers between devices  62.9 us (38%)
  Pallas kernels  13.9 us (8%)
  local copies, waits for them, and re-layouts  8.12 us (5%)
    ppermute x14, waiting for transfers between devices, pull(): return lax.ppermute(value, 'row', pairs)  40.8 us
    ppermute x16, waiting for transfers between devices, send(): lax.ppermute(value, 'col', [(i, (i + distance) % count) for i in range(co...  34.2 us
    ppermute x16, starting transfers between devices, send(): lax.ppermute(value, 'col', [(i, (i + distance) % count) for i in range(co...  28.6 us
    ppermute x14, starting transfers between devices, pull(): return lax.ppermute(value, 'row', pairs)  20 us
    ppermute x10, starting transfers between devices, swap(): return lax.ppermute(value, 'row', [(i, i ^ 1) for i in range(count)])  14.3 us
    pallas_call x4, Pallas kernels, aggregate_tiles(): pl.pallas_call(body, in_specs=[smem] * 3 + [vmem] * (1 + n_src), out_spec...  9.27 us
    pallas_call x2, Pallas kernels, node_mlp(): pl.pallas_call(body, in_specs=[vmem] * (4 + len(flat)), out_specs=[vmem]...  4.67 us
    ppermute x10, waiting for transfers between devices, swap(): return lax.ppermute(value, 'row', [(i, i ^ 1) for i in range(count)])  3.89 us
  transfers between devices with their start and end apart: 40, of which 23 were waited for; matrix products, arithmetic and copies ran while one was open for 5% of the time, Pallas kernels for 3%

profile of v4, /device:TPU:1, one launch (start us, length us, event | category | flops | bytes accessed | tf_op | source)
XLA Modules:
  0.0 165.5 jit_solution(1495090142144691584)
XLA Ops:
  0.0 3.6 %collective-permute-start = (bf16[256,512]{1,0:T(8,128)(2,1)}, bf16[256,512]{1,0:T(8,128)(2,1)S(1)}, u32[]{:S(2)}, u32[]{:S(2)}) collective-permute-start(bf16[256,512]{1,0:T(8,128)(2,1)} %refs_0_.1), channel_id=1, source_target_pairs={{64,0},{24,8},{80,16},{40,24},{96,32},{56,40},{112,48},{8,56},{128... | collective-permute-start | bytes 786440 | tf_op jit(solution)/shard_map/ppermute | solution.py:144
  3.6 1.6 collective-permute-start.2
  5.2 1.7 %constant_dynamic-update-slice_fusion.3 = bf16[1024,512]{1,0:T(8,128)(2,1)} fusion(bf16[256,512]{1,0:T(8,128)(2,1)} %refs_0_.1), kind=kLoop, calls=%fused_computation.31 | loop fusion | bytes 524288
  7.2 0.7 constant_dynamic-update-slice_fusion.2
  7.9 5.4 %collective-permute-done.1 = bf16[256,512]{1,0:T(8,128)(2,1)S(1)} collective-permute-done((bf16[256,512]{1,0:T(8,128)(2,1)}, bf16[256,512]{1,0:T(8,128)(2,1)S(1)}, u32[]{:S(2)}, u32[]{:S(2)}) %collective-permute-start.1) | collective-permute-done | bytes 262176 | tf_op jit(solution)/shard_map/ppermute | solution.py:144
  13.3 0.7 constant_dynamic-update-slice_fusion.1
  14.0 0.7 constant_dynamic-update-slice_fusion.refs_0_
  14.7 1.6 collective-permute-start.5
  16.3 2.7 %collective-permute-start.3 = (bf16[1024,512]{1,0:T(8,128)(2,1)}, bf16[1024,512]{1,0:T(8,128)(2,1)}, u32[]{:S(2)}, u32[]{:S(2)}) collective-permute-start(bf16[1024,512]{1,0:T(8,128)(2,1)} %constant_dynamic-update-slice_fusion.refs_0_), channel_id=1, source_target_pairs={{16,0},{72,8},{32,16},{88,24},{48,32},{104,40},{0,48},{120,56},{80... | collective-permute-start | bytes 3145736 | tf_op jit(solution)/shard_map/ppermute | solution.py:144
  19.1 2.8 %reshape.13.matrix_ref = bf16[16,128,512]{2,1,0:T(8,128)(2,1)S(1)} reshape(bf16[16,1,128,4,128]{4,3,2,1,0:T(4,128)(2,1)} %param.12) | data formatting | bytes 4194304 | tf_op jit(solution)/shard_map/reshape | solution.py:206
  22.0 9.6 %collective-permute-done.4.refs_2_ = bf16[1024,512]{1,0:T(8,128)(2,1)S(1)} collective-permute-done((bf16[1024,512]{1,0:T(8,128)(2,1)}, bf16[1024,512]{1,0:T(8,128)(2,1)S(1)}, u32[]{:S(2)}, u32[]{:S(2)}) %collective-permute-start.4) | collective-permute-done | bytes 1048608 | tf_op jit(solution)/shard_map/ppermute | solution.py:144
  31.7 1.1 slice.52
  32.7 1.4 collective-permute-start.8
  34.3 1.6 collective-permute-start.9
  35.9 1.6 collective-permute-start.6
  37.5 6.3 %collective-permute-done.7.refs_4_ = bf16[512,512]{1,0:T(8,128)(2,1)S(1)} collective-permute-done((bf16[512,512]{1,0:T(8,128)(2,1)S(1)}, bf16[512,512]{1,0:T(8,128)(2,1)S(1)}, u32[]{:S(2)}, u32[]{:S(2)}) %collective-permute-start.7) | collective-permute-done | bytes 524320 | tf_op jit(solution)/shard_map/ppermute | solution.py:144
  43.8 0.9 collective-permute-start.11
  45.4 0.9 collective-permute-done.11.refs_9_
  46.2 0.7 collective-permute-done.10.refs_8_
  47.0 2.8 %aggregate_tiles.5 = (bf16[256,512]{1,0:T(8,128)(2,1)S(1)}, bf16[256,512]{1,0:T(8,128)(2,1)S(1)}, bf16[256,512]{1,0:T(8,128)(2,1)S(1)}) custom-call(s32[4]{0:T(128)S(1)} %pad_add_fusion.here_ref, s32[32]{0:T(128)S(1)} %bitcast.9, s32[64]{0:T(128)S(1)} %reshape.15.index_ref, bf16[16,128,512]{2,1,0:T(8,128)(2,1)S(1)} %reshape.13.matrix_ref, ...), custom_call_target="tpu_custom_call" | custom-call | tf_op jit(solution)/shard_map/aggregate_tiles/pallas_call | solution.py:54
  49.8 1.7 %collective-permute-start.14 = (bf16[256,512]{1,0:T(8,128)(2,1)S(1)}, bf16[256,512]{1,0:T(8,128)(2,1)S(1)}, u32[]{:S(2)}, u32[]{:S(2)}) collective-permute-start(bf16[256,512]{1,0:T(8,128)(2,1)S(1)} %get-tuple-element.39), channel_id=1, source_target_pairs={{0,1},{1,2},{2,3},{3,4},{4,5},{5,6},{6,7},{7,0},{8,9},{9,10},{10,1... | collective-permute-start | bytes 786440 | tf_op jit(solution)/shard_map/ppermute | solution.py:167
  51.8 5.2 %collective-permute-start.18 = (bf16[128,512]{1,0:T(8,128)(2,1)S(1)}, bf16[128,512]{1,0:T(8,128)(2,1)S(1)}, u32[]{:S(2)}, u32[]{:S(2)}) collective-permute-start(bf16[128,512]{1,0:T(8,128)(2,1)S(1)} %get-tuple-element.53), channel_id=1, source_target_pairs={{0,6},{1,7},{2,0},{3,1},{4,2},{5,3},{6,4},{7,5},{8,14},{9,15},{10,... | collective-permute-start | bytes 393224 | tf_op jit(solution)/shard_map/ppermute | solution.py:167
  57.0 2.4 %collective-permute-start.17 = (bf16[256,512]{1,0:T(8,128)(2,1)S(1)}, bf16[256,512]{1,0:T(8,128)(2,1)S(1)}, u32[]{:S(2)}, u32[]{:S(2)}) collective-permute-start(bf16[256,512]{1,0:T(8,128)(2,1)S(1)} %get-tuple-element.42), channel_id=1, source_target_pairs={{0,7},{1,0},{2,1},{3,2},{4,3},{5,4},{6,5},{7,6},{8,15},{9,8},{10,9... | collective-permute-start | bytes 786440 | tf_op jit(solution)/shard_map/ppermute | solution.py:167
  59.4 3.2 %aggregate_tiles.4 = (bf16[256,512]{1,0:T(8,128)(2,1)S(1)}, bf16[256,512]{1,0:T(8,128)(2,1)S(1)}, bf16[256,512]{1,0:T(8,128)(2,1)S(1)}, bf16[256,512]{1,0:T(8,128)(2,1)S(1)}, bf16[256,512]{1,0:T(8,128)(2,1)S(1)}) custom-call(s32[4]{0:T(128)S(1)} %pad_add_fusion.here_ref, s32[32]{0:T(128)S(1)} %bitcast.10, s32[64]{0:T(128)S(1)} %reshape.15.index_ref, ...), custom_call_target="tpu_custom_call" | custom-call | tf_op jit(solution)/shard_map/aggregate_tiles/pallas_call | solution.py:54
  62.8 2.7 %collective-permute-start.13 = (bf16[256,512]{1,0:T(8,128)(2,1)S(1)}, bf16[256,512]{1,0:T(8,128)(2,1)S(1)}, u32[]{:S(2)}, u32[]{:S(2)}) collective-permute-start(bf16[256,512]{1,0:T(8,128)(2,1)S(1)} %get-tuple-element.37), channel_id=1, source_target_pairs={{0,7},{1,0},{2,1},{3,2},{4,3},{5,4},{6,5},{7,6},{8,15},{9,8},{10,9... | collective-permute-start | bytes 786440 | tf_op jit(solution)/shard_map/ppermute | solution.py:167
  65.5 0.6 collective-permute-done.15
  66.3 2.0 %collective-permute-done.17 = bf16[256,512]{1,0:T(8,128)(2,1)S(1)} collective-permute-done((bf16[256,512]{1,0:T(8,128)(2,1)S(1)}, bf16[256,512]{1,0:T(8,128)(2,1)S(1)}, u32[]{:S(2)}, u32[]{:S(2)}) %collective-permute-start.17) | collective-permute-done | bytes 262176 | tf_op jit(solution)/shard_map/ppermute | solution.py:167
  68.5 1.7 %collective-permute-start.19 = (bf16[256,512]{1,0:T(8,128)(2,1)S(1)}, bf16[256,512]{1,0:T(8,128)(2,1)S(1)}, u32[]{:S(2)}, u32[]{:S(2)}) collective-permute-start(bf16[256,512]{1,0:T(8,128)(2,1)S(1)} %pad_maximum_fusion.2), channel_id=1, source_target_pairs={{0,6},{1,7},{2,0},{3,1},{4,2},{5,3},{6,4},{7,5},{8,14},{9,15},{10,... | collective-permute-start | bytes 786440 | tf_op jit(solution)/shard_map/ppermute | solution.py:167
  70.3 2.7 %collective-permute-done.12.refs_2_ = bf16[256,512]{1,0:T(8,128)(2,1)S(1)} collective-permute-done((bf16[256,512]{1,0:T(8,128)(2,1)S(1)}, bf16[256,512]{1,0:T(8,128)(2,1)S(1)}, u32[]{:S(2)}, u32[]{:S(2)}) %collective-permute-start.12) | collective-permute-done | bytes 262176 | tf_op jit(solution)/shard_map/ppermute | solution.py:167
  73.0 0.9 collective-permute-done.13.refs_3_
  73.9 8.6 %collective-permute-done.16.refs_4_ = bf16[256,512]{1,0:T(8,128)(2,1)S(1)} collective-permute-done((bf16[256,512]{1,0:T(8,128)(2,1)S(1)}, bf16[256,512]{1,0:T(8,128)(2,1)S(1)}, u32[]{:S(2)}, u32[]{:S(2)}) %collective-permute-start.16) | collective-permute-done | bytes 262176 | tf_op jit(solution)/shard_map/ppermute | solution.py:167
  82.5 2.7 %collective-permute-done.19.refs_5_ = bf16[256,512]{1,0:T(8,128)(2,1)S(1)} collective-permute-done((bf16[256,512]{1,0:T(8,128)(2,1)S(1)}, bf16[256,512]{1,0:T(8,128)(2,1)S(1)}, u32[]{:S(2)}, u32[]{:S(2)}) %collective-permute-start.19) | collective-permute-done | bytes 262176 | tf_op jit(solution)/shard_map/ppermute | solution.py:167
  85.2 2.0 %node_mlp.2.refs_0_ = bf16[256,512]{1,0:T(8,128)(2,1)S(1)} custom-call(f32[2,256,512]{2,1,0:T(8,128)S(1)} %broadcast_multiply_fusion.scale_ref, bf16[256,512]{1,0:T(8,128)(2,1)S(1)} %convolution_convert_fusion.shift_ref, bf16[2,512,2048]{2,1,0:T(8,128)(2,1)S(1)} %copy-done.1, bf16[2,2048,512]{2,1,0:T(8,128)(2,1)S(1)} %copy-done.2, ...), custom_call_target="tpu_custom_call" | custom-call | tf_op jit(solution)/shard_map/node_mlp/pallas_call | solution.py:102
  87.2 2.2 %collective-permute-start.22 = (bf16[256,512]{1,0:T(8,128)(2,1)S(1)}, bf16[256,512]{1,0:T(8,128)(2,1)S(1)}, u32[]{:S(2)}, u32[]{:S(2)}) collective-permute-start(bf16[256,512]{1,0:T(8,128)(2,1)S(1)} %node_mlp.2.refs_0_), channel_id=1, source_target_pairs={{128,0},{40,8},{144,16},{56,24},{160,32},{8,40},{176,48},{24,56},{... | collective-permute-start | bytes 786440 | tf_op jit(solution)/shard_map/ppermute | solution.py:144
  89.3 0.9 collective-permute-start.21
  90.3 1.7 %collective-permute-start.20 = (bf16[256,512]{1,0:T(8,128)(2,1)S(1)}, bf16[256,512]{1,0:T(8,128)(2,1)S(1)}, u32[]{:S(2)}, u32[]{:S(2)}) collective-permute-start(bf16[256,512]{1,0:T(8,128)(2,1)S(1)} %node_mlp.2.refs_0_), channel_id=1, source_target_pairs={{64,0},{24,8},{80,16},{40,24},{96,32},{56,40},{112,48},{8,56},{128... | collective-permute-start | bytes 786440 | tf_op jit(solution)/shard_map/ppermute | solution.py:144
  92.0 2.3 %collective-permute-done.22 = bf16[256,512]{1,0:T(8,128)(2,1)S(1)} collective-permute-done((bf16[256,512]{1,0:T(8,128)(2,1)S(1)}, bf16[256,512]{1,0:T(8,128)(2,1)S(1)}, u32[]{:S(2)}, u32[]{:S(2)}) %collective-permute-start.22) | collective-permute-done | bytes 262176 | tf_op jit(solution)/shard_map/ppermute | solution.py:144
  94.3 2.8 %collective-permute-done.21 = bf16[256,512]{1,0:T(8,128)(2,1)S(1)} collective-permute-done((bf16[256,512]{1,0:T(8,128)(2,1)S(1)}, bf16[256,512]{1,0:T(8,128)(2,1)S(1)}, u32[]{:S(2)}, u32[]{:S(2)}) %collective-permute-start.21) | collective-permute-done | bytes 262176 | tf_op jit(solution)/shard_map/ppermute | solution.py:144
  97.2 1.1 collective-permute-start.24
  98.3 1.7 %collective-permute-start.23 = (bf16[1024,512]{1,0:T(8,128)(2,1)S(1)}, bf16[1024,512]{1,0:T(8,128)(2,1)S(1)}, u32[]{:S(2)}, u32[]{:S(2)}) collective-permute-start(bf16[1024,512]{1,0:T(8,128)(2,1)S(1)} %pad_maximum_fusion.refs_0_), channel_id=1, source_target_pairs={{16,0},{72,8},{32,16},{88,24},{48,32},{104,40},{0,48},{120,56},{80... | collective-permute-start | bytes 3145736 | tf_op jit(solution)/shard_map/ppermute | solution.py:144
  99.9 2.2 %collective-permute-start.27 = (bf16[1024,512]{1,0:T(8,128)(2,1)S(1)}, bf16[1024,512]{1,0:T(8,128)(2,1)S(1)}, u32[]{:S(2)}, u32[]{:S(2)}) collective-permute-start(bf16[1024,512]{1,0:T(8,128)(2,1)S(1)} %pad_maximum_fusion.refs_0_), channel_id=1, source_target_pairs={{0,8},{8,0},{16,24},{24,16},{32,40},{40,32},{48,56},{56,48},{64,72... | collective-permute-start | bytes 3145736 | tf_op jit(solution)/shard_map/ppermute | solution.py:149
  102.1 10.3 %collective-permute-done.24.refs_2_ = bf16[1024,512]{1,0:T(8,128)(2,1)S(1)} collective-permute-done((bf16[1024,512]{1,0:T(8,128)(2,1)S(1)}, bf16[1024,512]{1,0:T(8,128)(2,1)S(1)}, u32[]{:S(2)}, u32[]{:S(2)}) %collective-permute-start.24) | collective-permute-done | bytes 1048608 | tf_op jit(solution)/shard_map/ppermute | solution.py:144
  112.6 2.7 %collective-permute-start.25 = (bf16[512,512]{1,0:T(8,128)(2,1)S(1)}, bf16[512,512]{1,0:T(8,128)(2,1)S(1)}, u32[]{:S(2)}, u32[]{:S(2)}) collective-permute-start(bf16[512,512]{1,0:T(8,128)(2,1)S(1)} %slice.72), channel_id=1, source_target_pairs={{16,0},{72,8},{32,16},{88,24},{48,32},{104,40},{0,48},{120,56},{80... | collective-permute-start | bytes 1572872 | tf_op jit(solution)/shard_map/ppermute | solution.py:144
  115.3 3.0 %collective-permute-start.29 = (bf16[1024,512]{1,0:T(8,128)(2,1)S(1)}, bf16[1024,512]{1,0:T(8,128)(2,1)S(1)}, u32[]{:S(2)}, u32[]{:S(2)}) collective-permute-start(bf16[1024,512]{1,0:T(8,128)(2,1)S(1)} %collective-permute-done.24.refs_2_), channel_id=1, source_target_pairs={{0,8},{8,0},{16,24},{24,16},{32,40},{40,32},{48,56},{56,48},{64,72... | collective-permute-start | bytes 3145736 | tf_op jit(solution)/shard_map/ppermute | solution.py:149
  118.4 3.7 %collective-permute-done.26.refs_4_ = bf16[512,512]{1,0:T(8,128)(2,1)S(1)} collective-permute-done((bf16[512,512]{1,0:T(8,128)(2,1)S(1)}, bf16[512,512]{1,0:T(8,128)(2,1)S(1)}, u32[]{:S(2)}, u32[]{:S(2)}) %collective-permute-start.26) | collective-permute-done | bytes 524320 | tf_op jit(solution)/shard_map/ppermute | solution.py:144
  122.1 3.3 %collective-permute-start.31 = (bf16[512,512]{1,0:T(8,128)(2,1)S(1)}, bf16[512,512]{1,0:T(8,128)(2,1)S(1)}, u32[]{:S(2)}, u32[]{:S(2)}) collective-permute-start(bf16[512,512]{1,0:T(8,128)(2,1)S(1)} %collective-permute-done.26.refs_4_), channel_id=1, source_target_pairs={{0,8},{8,0},{16,24},{24,16},{32,40},{40,32},{48,56},{56,48},{64,72... | collective-permute-start | bytes 1572872 | tf_op jit(solution)/shard_map/ppermute | solution.py:149
  125.4 1.5 collective-permute-done.31.refs_9_
  126.9 0.7 collective-permute-done.30.refs_8_
  127.7 1.5 aggregate_tiles.7
  129.2 1.1 collective-permute-start.34
  130.3 3.4 %collective-permute-start.38 = (bf16[128,512]{1,0:T(8,128)(2,1)S(1)}, bf16[128,512]{1,0:T(8,128)(2,1)S(1)}, u32[]{:S(2)}, u32[]{:S(2)}) collective-permute-start(bf16[128,512]{1,0:T(8,128)(2,1)S(1)} %get-tuple-element.51), channel_id=1, source_target_pairs={{0,6},{1,7},{2,0},{3,1},{4,2},{5,3},{6,4},{7,5},{8,14},{9,15},{10,... | collective-permute-start | bytes 393224 | tf_op jit(solution)/shard_map/ppermute | solution.py:167
  133.7 1.0 collective-permute-start.35
  134.6 1.0 collective-permute-start.37
  135.6 1.8 %aggregate_tiles.6 = (bf16[256,512]{1,0:T(8,128)(2,1)S(1)}, bf16[256,512]{1,0:T(8,128)(2,1)S(1)}, bf16[256,512]{1,0:T(8,128)(2,1)S(1)}, bf16[256,512]{1,0:T(8,128)(2,1)S(1)}, bf16[256,512]{1,0:T(8,128)(2,1)S(1)}) custom-call(s32[4]{0:T(128)S(1)} %pad_add_fusion.here_ref, s32[32]{0:T(128)S(1)} %bitcast.12, s32[64]{0:T(128)S(1)} %reshape.15.index_ref, ...), custom_call_target="tpu_custom_call" | custom-call | tf_op jit(solution)/shard_map/aggregate_tiles/pallas_call | solution.py:54
  137.4 0.6 collective-permute-start.32
  138.0 2.2 %collective-permute-start.33 = (bf16[256,512]{1,0:T(8,128)(2,1)S(1)}, bf16[256,512]{1,0:T(8,128)(2,1)S(1)}, u32[]{:S(2)}, u32[]{:S(2)}) collective-permute-start(bf16[256,512]{1,0:T(8,128)(2,1)S(1)} %get-tuple-element.45), channel_id=1, source_target_pairs={{0,7},{1,0},{2,1},{3,2},{4,3},{5,4},{6,5},{7,6},{8,15},{9,8},{10,9... | collective-permute-start | bytes 786440 | tf_op jit(solution)/shard_map/ppermute | solution.py:167
  140.3 2.5 %collective-permute-done.35 = bf16[128,512]{1,0:T(8,128)(2,1)S(1)} collective-permute-done((bf16[128,512]{1,0:T(8,128)(2,1)S(1)}, bf16[128,512]{1,0:T(8,128)(2,1)S(1)}, u32[]{:S(2)}, u32[]{:S(2)}) %collective-permute-start.35) | collective-permute-done | bytes 131104 | tf_op jit(solution)/shard_map/ppermute | solution.py:167
  142.8 1.9 %collective-permute-start.36 = (bf16[256,512]{1,0:T(8,128)(2,1)S(1)}, bf16[256,512]{1,0:T(8,128)(2,1)S(1)}, u32[]{:S(2)}, u32[]{:S(2)}) collective-permute-start(bf16[256,512]{1,0:T(8,128)(2,1)S(1)} %pad_maximum_fusion.3), channel_id=1, source_target_pairs={{0,2},{1,3},{2,4},{3,5},{4,6},{5,7},{6,0},{7,1},{8,10},{9,11},{10,... | collective-permute-start | bytes 786440 | tf_op jit(solution)/shard_map/ppermute | solution.py:167
  144.9 3.7 %collective-permute-start.39 = (bf16[256,512]{1,0:T(8,128)(2,1)S(1)}, bf16[256,512]{1,0:T(8,128)(2,1)S(1)}, u32[]{:S(2)}, u32[]{:S(2)}) collective-permute-start(bf16[256,512]{1,0:T(8,128)(2,1)S(1)} %pad_maximum_fusion.4), channel_id=1, source_target_pairs={{0,6},{1,7},{2,0},{3,1},{4,2},{5,3},{6,4},{7,5},{8,14},{9,15},{10,... | collective-permute-start | bytes 786440 | tf_op jit(solution)/shard_map/ppermute | solution.py:167
  148.6 0.6 collective-permute-done.32.refs_2_
  149.2 1.0 collective-permute-done.33.refs_3_
  150.2 7.9 %collective-permute-done.36.refs_4_ = bf16[256,512]{1,0:T(8,128)(2,1)S(1)} collective-permute-done((bf16[256,512]{1,0:T(8,128)(2,1)S(1)}, bf16[256,512]{1,0:T(8,128)(2,1)S(1)}, u32[]{:S(2)}, u32[]{:S(2)}) %collective-permute-start.36) | collective-permute-done | bytes 262176 | tf_op jit(solution)/shard_map/ppermute | solution.py:167
  158.2 4.6 %collective-permute-done.39.refs_5_ = bf16[256,512]{1,0:T(8,128)(2,1)S(1)} collective-permute-done((bf16[256,512]{1,0:T(8,128)(2,1)S(1)}, bf16[256,512]{1,0:T(8,128)(2,1)S(1)}, u32[]{:S(2)}, u32[]{:S(2)}) %collective-permute-start.39) | collective-permute-done | bytes 262176 | tf_op jit(solution)/shard_map/ppermute | solution.py:167
  162.8 2.7 %node_mlp.3 = bf16[256,512]{1,0:T(8,128)(2,1)} custom-call(f32[2,256,512]{2,1,0:T(8,128)S(1)} %broadcast_multiply_fusion.scale_ref, bf16[256,512]{1,0:T(8,128)(2,1)S(1)} %convolution_convert_fusion.shift_ref, bf16[2,512,2048]{2,1,0:T(8,128)(2,1)S(1)} %copy-done.1, bf16[2,2048,512]{2,1,0:T(8,128)(2,1)S(1)} %copy-done.2, ...), custom_call_target="tpu_custom_call" | custom-call | tf_op jit(solution)/shard_map/node_mlp/pallas_call | solution.py:102
  (76 shorter events, 2.8 us)
Async XLA Ops:
  0.0 51.5 %copy-start = (bf16[128,512]{1,0:T(8,128)(2,1)S(1)}, bf16[128,512]{1,0:T(8,128)(2,1)}, u32[]{:S(2)}) copy-start(bf16[128,512]{1,0:T(8,128)(2,1)} %param.17) | copy-start | bytes 393220
  0.0 19.0 %copy-start.7 = (s32[16,1,4]{0,2,1:T(4,128)S(1)}, s32[16,1,4]{0,2,1:T(4,128)}, u32[]{:S(2)}) copy-start(s32[16,1,4]{0,2,1:T(4,128)} %param.13) | copy-start | bytes 772
  0.0 7.2 %collective-permute-start = (bf16[256,512]{1,0:T(8,128)(2,1)}, bf16[256,512]{1,0:T(8,128)(2,1)S(1)}, u32[]{:S(2)}, u32[]{:S(2)}) collective-permute-start(bf16[256,512]{1,0:T(8,128)(2,1)} %refs_0_.1), channel_id=1, source_target_pairs={{64,0},{24,8},{80,16},{40,24},{96,32},{56,40},{112,48},{8,56},{128... | collective-permute-start | bytes 786440 | tf_op jit(solution)/shard_map/ppermute | solution.py:144
  3.6 9.7 %collective-permute-start.1 = (bf16[256,512]{1,0:T(8,128)(2,1)}, bf16[256,512]{1,0:T(8,128)(2,1)S(1)}, u32[]{:S(2)}, u32[]{:S(2)}) collective-permute-start(bf16[256,512]{1,0:T(8,128)(2,1)} %refs_0_.1), channel_id=1, source_target_pairs={{192,0},{56,8},{208,16},{8,24},{224,32},{24,40},{240,48},{40,56},{... | collective-permute-start | bytes 786440 | tf_op jit(solution)/shard_map/ppermute | solution.py:144
  3.6 10.4 %collective-permute-start.2 = (bf16[256,512]{1,0:T(8,128)(2,1)}, bf16[256,512]{1,0:T(8,128)(2,1)S(1)}, u32[]{:S(2)}, u32[]{:S(2)}) collective-permute-start(bf16[256,512]{1,0:T(8,128)(2,1)} %refs_0_.1), channel_id=1, source_target_pairs={{128,0},{40,8},{144,16},{56,24},{160,32},{8,40},{176,48},{24,56},{... | collective-permute-start | bytes 786440 | tf_op jit(solution)/shard_map/ppermute | solution.py:144
  14.7 7.3 %collective-permute-start.5 = (bf16[1024,512]{1,0:T(8,128)(2,1)}, bf16[1024,512]{1,0:T(8,128)(2,1)}, u32[]{:S(2)}, u32[]{:S(2)}) collective-permute-start(bf16[1024,512]{1,0:T(8,128)(2,1)} %constant_dynamic-update-slice_fusion.refs_0_), channel_id=1, source_target_pairs={{0,8},{8,0},{16,24},{24,16},{32,40},{40,32},{48,56},{56,48},{64,72... | collective-permute-start | bytes 3145736 | tf_op jit(solution)/shard_map/ppermute | solution.py:149
  16.3 15.4 %collective-permute-start.4 = (bf16[1024,512]{1,0:T(8,128)(2,1)}, bf16[1024,512]{1,0:T(8,128)(2,1)S(1)}, u32[]{:S(2)}, u32[]{:S(2)}) collective-permute-start(bf16[1024,512]{1,0:T(8,128)(2,1)} %constant_dynamic-update-slice_fusion.refs_0_), channel_id=1, source_target_pairs={{48,0},{200,8},{0,16},{216,24},{16,32},{232,40},{32,48},{248,56},{... | collective-permute-start | bytes 3145736 | tf_op jit(solution)/shard_map/ppermute | solution.py:144
  16.3 15.4 %collective-permute-start.3 = (bf16[1024,512]{1,0:T(8,128)(2,1)}, bf16[1024,512]{1,0:T(8,128)(2,1)}, u32[]{:S(2)}, u32[]{:S(2)}) collective-permute-start(bf16[1024,512]{1,0:T(8,128)(2,1)} %constant_dynamic-update-slice_fusion.refs_0_), channel_id=1, source_target_pairs={{16,0},{72,8},{32,16},{88,24},{48,32},{104,40},{0,48},{120,56},{80... | collective-permute-start | bytes 3145736 | tf_op jit(solution)/shard_map/ppermute | solution.py:144
  21.9 23.1 %copy-start.5 = (bf16[16,512]{1,0:T(8,128)(2,1)S(1)}, bf16[16,512]{1,0:T(8,128)(2,1)}, u32[]{:S(2)}) copy-start(bf16[16,512]{1,0:T(8,128)(2,1)} %param.18) | copy-start | bytes 49156
  21.9 23.1 %copy-start.8 = (s32[256]{0:T(256)S(1)}, s32[256]{0:T(256)}, u32[]{:S(2)}) copy-start(s32[256]{0:T(256)} %param.16) | copy-start | bytes 3076
  21.9 25.0 %copy-start.4 = (s32[1,1,32,1]{2,3,1,0:T(1,128)S(1)}, s32[1,1,32,1]{2,3,1,0:T(1,128)}, u32[]{:S(2)}) copy-start(s32[1,1,32,1]{2,3,1,0:T(1,128)} %param.14) | copy-start | bytes 388
  32.7 12.6 %collective-permute-start.8 = (bf16[1024,512]{1,0:T(8,128)(2,1)}, bf16[1024,512]{1,0:T(8,128)(2,1)S(1)}, u32[]{:S(2)}, u32[]{:S(2)}) collective-permute-start(bf16[1024,512]{1,0:T(8,128)(2,1)} %collective-permute-done.3.refs_1_), channel_id=1, source_target_pairs={{0,8},{8,0},{16,24},{24,16},{32,40},{40,32},{48,56},{56,48},{64,72... | collective-permute-start | bytes 3145736 | tf_op jit(solution)/shard_map/ppermute | solution.py:149
  34.2 9.6 %collective-permute-start.7 = (bf16[512,512]{1,0:T(8,128)(2,1)S(1)}, bf16[512,512]{1,0:T(8,128)(2,1)S(1)}, u32[]{:S(2)}, u32[]{:S(2)}) collective-permute-start(bf16[512,512]{1,0:T(8,128)(2,1)S(1)} %slice.53), channel_id=1, source_target_pairs={{48,0},{200,8},{0,16},{216,24},{16,32},{232,40},{32,48},{248,56},{... | collective-permute-start | bytes 1572872 | tf_op jit(solution)/shard_map/ppermute | solution.py:144
  34.3 11.1 %collective-permute-start.9 = (bf16[1024,512]{1,0:T(8,128)(2,1)S(1)}, bf16[1024,512]{1,0:T(8,128)(2,1)S(1)}, u32[]{:S(2)}, u32[]{:S(2)}) collective-permute-start(bf16[1024,512]{1,0:T(8,128)(2,1)S(1)} %collective-permute-done.4.refs_2_), channel_id=1, source_target_pairs={{0,8},{8,0},{16,24},{24,16},{32,40},{40,32},{48,56},{56,48},{64,72... | collective-permute-start | bytes 3145736 | tf_op jit(solution)/shard_map/ppermute | solution.py:149
  35.9 8.8 %collective-permute-start.6 = (bf16[512,512]{1,0:T(8,128)(2,1)S(1)}, bf16[512,512]{1,0:T(8,128)(2,1)S(1)}, u32[]{:S(2)}, u32[]{:S(2)}) collective-permute-start(bf16[512,512]{1,0:T(8,128)(2,1)S(1)} %slice.52), channel_id=1, source_target_pairs={{16,0},{72,8},{32,16},{88,24},{48,32},{104,40},{0,48},{120,56},{80... | collective-permute-start | bytes 1572872 | tf_op jit(solution)/shard_map/ppermute | solution.py:144
  43.8 2.4 %collective-permute-start.11 = (bf16[512,512]{1,0:T(8,128)(2,1)S(1)}, bf16[512,512]{1,0:T(8,128)(2,1)S(1)}, u32[]{:S(2)}, u32[]{:S(2)}) collective-permute-start(bf16[512,512]{1,0:T(8,128)(2,1)S(1)} %collective-permute-done.7.refs_4_), channel_id=1, source_target_pairs={{0,8},{8,0},{16,24},{24,16},{32,40},{40,32},{48,56},{56,48},{64,72... | collective-permute-start | bytes 1572872 | tf_op jit(solution)/shard_map/ppermute | solution.py:149
  44.7 2.3 %collective-permute-start.10 = (bf16[512,512]{1,0:T(8,128)(2,1)S(1)}, bf16[512,512]{1,0:T(8,128)(2,1)S(1)}, u32[]{:S(2)}, u32[]{:S(2)}) collective-permute-start(bf16[512,512]{1,0:T(8,128)(2,1)S(1)} %collective-permute-done.6.refs_3_), channel_id=1, source_target_pairs={{0,8},{8,0},{16,24},{24,16},{32,40},{40,32},{48,56},{56,48},{64,72... | collective-permute-start | bytes 1572872 | tf_op jit(solution)/shard_map/ppermute | solution.py:149
  45.3 6.2 %copy-start.9 = (s32[256]{0:T(256)S(1)}, s32[256]{0:T(256)}, u32[]{:S(2)}) copy-start(s32[256]{0:T(256)} %param.15) | copy-start | bytes 3076
  49.8 13.0 %collective-permute-start.14 = (bf16[256,512]{1,0:T(8,128)(2,1)S(1)}, bf16[256,512]{1,0:T(8,128)(2,1)S(1)}, u32[]{:S(2)}, u32[]{:S(2)}) collective-permute-start(bf16[256,512]{1,0:T(8,128)(2,1)S(1)} %get-tuple-element.39), channel_id=1, source_target_pairs={{0,1},{1,2},{2,3},{3,4},{4,5},{5,6},{6,7},{7,0},{8,9},{9,10},{10,1... | collective-permute-start | bytes 786440 | tf_op jit(solution)/shard_map/ppermute | solution.py:167
  51.8 16.6 %collective-permute-start.18 = (bf16[128,512]{1,0:T(8,128)(2,1)S(1)}, bf16[128,512]{1,0:T(8,128)(2,1)S(1)}, u32[]{:S(2)}, u32[]{:S(2)}) collective-permute-start(bf16[128,512]{1,0:T(8,128)(2,1)S(1)} %get-tuple-element.53), channel_id=1, source_target_pairs={{0,6},{1,7},{2,0},{3,1},{4,2},{5,3},{6,4},{7,5},{8,14},{9,15},{10,... | collective-permute-start | bytes 393224 | tf_op jit(solution)/shard_map/ppermute | solution.py:167
  57.0 9.2 %collective-permute-start.15 = (bf16[128,512]{1,0:T(8,128)(2,1)S(1)}, bf16[128,512]{1,0:T(8,128)(2,1)S(1)}, u32[]{:S(2)}, u32[]{:S(2)}) collective-permute-start(bf16[128,512]{1,0:T(8,128)(2,1)S(1)} %get-tuple-element.54), channel_id=1, source_target_pairs={{0,2},{1,3},{2,4},{3,5},{4,6},{5,7},{6,0},{7,1},{8,10},{9,11},{10,... | collective-permute-start | bytes 393224 | tf_op jit(solution)/shard_map/ppermute | solution.py:167
  57.0 11.3 %collective-permute-start.17 = (bf16[256,512]{1,0:T(8,128)(2,1)S(1)}, bf16[256,512]{1,0:T(8,128)(2,1)S(1)}, u32[]{:S(2)}, u32[]{:S(2)}) collective-permute-start(bf16[256,512]{1,0:T(8,128)(2,1)S(1)} %get-tuple-element.42), channel_id=1, source_target_pairs={{0,7},{1,0},{2,1},{3,2},{4,3},{5,4},{6,5},{7,6},{8,15},{9,8},{10,9... | collective-permute-start | bytes 786440 | tf_op jit(solution)/shard_map/ppermute | solution.py:167
  59.4 25.8 %copy-start.2 = (bf16[2,2048,512]{2,1,0:T(8,128)(2,1)S(1)}, bf16[2,2048,512]{2,1,0:T(8,128)(2,1)}, u32[]{:S(2)}) copy-start(bf16[2,2048,512]{2,1,0:T(8,128)(2,1)} %w_out_ref.3) | copy-start | bytes 12582916
  62.6 10.4 %collective-permute-start.12 = (bf16[256,512]{1,0:T(8,128)(2,1)S(1)}, bf16[256,512]{1,0:T(8,128)(2,1)S(1)}, u32[]{:S(2)}, u32[]{:S(2)}) collective-permute-start(bf16[256,512]{1,0:T(8,128)(2,1)S(1)} %get-tuple-element.36), channel_id=1, source_target_pairs={{0,1},{1,2},{2,3},{3,4},{4,5},{5,6},{6,7},{7,0},{8,9},{9,10},{10,1... | collective-permute-start | bytes 786440 | tf_op jit(solution)/shard_map/ppermute | solution.py:167
  62.8 11.2 %collective-permute-start.13 = (bf16[256,512]{1,0:T(8,128)(2,1)S(1)}, bf16[256,512]{1,0:T(8,128)(2,1)S(1)}, u32[]{:S(2)}, u32[]{:S(2)}) collective-permute-start(bf16[256,512]{1,0:T(8,128)(2,1)S(1)} %get-tuple-element.37), channel_id=1, source_target_pairs={{0,7},{1,0},{2,1},{3,2},{4,3},{5,4},{6,5},{7,6},{8,15},{9,8},{10,9... | collective-permute-start | bytes 786440 | tf_op jit(solution)/shard_map/ppermute | solution.py:167
  65.5 4.7 %copy-start.6 = (f32[2,512]{1,0:T(2,128)S(1)}, f32[2,512]{1,0:T(2,128)}, u32[]{:S(2)}) copy-start(f32[2,512]{1,0:T(2,128)} %param.19) | copy-start | bytes 12292
  66.2 19.0 %copy-start.1 = (bf16[2,512,2048]{2,1,0:T(8,128)(2,1)S(1)}, bf16[2,512,2048]{2,1,0:T(8,128)(2,1)}, u32[]{:S(2)}) copy-start(bf16[2,512,2048]{2,1,0:T(8,128)(2,1)} %w_in_ref.3) | copy-start | bytes 12582916
  66.2 19.0 %copy-start.3 = (bf16[256,512]{1,0:T(8,128)(2,1)S(1)}, bf16[256,512]{1,0:T(8,128)(2,1)}, u32[]{:S(2)}) copy-start(bf16[256,512]{1,0:T(8,128)(2,1)} %refs_0_.1) | copy-start | bytes 786436
  66.2 16.3 %collective-permute-start.16 = (bf16[256,512]{1,0:T(8,128)(2,1)S(1)}, bf16[256,512]{1,0:T(8,128)(2,1)S(1)}, u32[]{:S(2)}, u32[]{:S(2)}) collective-permute-start(bf16[256,512]{1,0:T(8,128)(2,1)S(1)} %pad_maximum_fusion.1), channel_id=1, source_target_pairs={{0,2},{1,3},{2,4},{3,5},{4,6},{5,7},{6,0},{7,1},{8,10},{9,11},{10,... | collective-permute-start | bytes 786440 | tf_op jit(solution)/shard_map/ppermute | solution.py:167
  68.5 16.7 %collective-permute-start.19 = (bf16[256,512]{1,0:T(8,128)(2,1)S(1)}, bf16[256,512]{1,0:T(8,128)(2,1)S(1)}, u32[]{:S(2)}, u32[]{:S(2)}) collective-permute-start(bf16[256,512]{1,0:T(8,128)(2,1)S(1)} %pad_maximum_fusion.2), channel_id=1, source_target_pairs={{0,6},{1,7},{2,0},{3,1},{4,2},{5,3},{6,4},{7,5},{8,14},{9,15},{10,... | collective-permute-start | bytes 786440 | tf_op jit(solution)/shard_map/ppermute | solution.py:167
  87.2 7.1 %collective-permute-start.22 = (bf16[256,512]{1,0:T(8,128)(2,1)S(1)}, bf16[256,512]{1,0:T(8,128)(2,1)S(1)}, u32[]{:S(2)}, u32[]{:S(2)}) collective-permute-start(bf16[256,512]{1,0:T(8,128)(2,1)S(1)} %node_mlp.2.refs_0_), channel_id=1, source_target_pairs={{128,0},{40,8},{144,16},{56,24},{160,32},{8,40},{176,48},{24,56},{... | collective-permute-start | bytes 786440 | tf_op jit(solution)/shard_map/ppermute | solution.py:144
  89.3 7.8 %collective-permute-start.21 = (bf16[256,512]{1,0:T(8,128)(2,1)S(1)}, bf16[256,512]{1,0:T(8,128)(2,1)S(1)}, u32[]{:S(2)}, u32[]{:S(2)}) collective-permute-start(bf16[256,512]{1,0:T(8,128)(2,1)S(1)} %node_mlp.2.refs_0_), channel_id=1, source_target_pairs={{192,0},{56,8},{208,16},{8,24},{224,32},{24,40},{240,48},{40,56},{... | collective-permute-start | bytes 786440 | tf_op jit(solution)/shard_map/ppermute | solution.py:144
  90.3 6.9 %collective-permute-start.20 = (bf16[256,512]{1,0:T(8,128)(2,1)S(1)}, bf16[256,512]{1,0:T(8,128)(2,1)S(1)}, u32[]{:S(2)}, u32[]{:S(2)}) collective-permute-start(bf16[256,512]{1,0:T(8,128)(2,1)S(1)} %node_mlp.2.refs_0_), channel_id=1, source_target_pairs={{64,0},{24,8},{80,16},{40,24},{96,32},{56,40},{112,48},{8,56},{128... | collective-permute-start | bytes 786440 | tf_op jit(solution)/shard_map/ppermute | solution.py:144
  97.2 15.2 %collective-permute-start.24 = (bf16[1024,512]{1,0:T(8,128)(2,1)S(1)}, bf16[1024,512]{1,0:T(8,128)(2,1)S(1)}, u32[]{:S(2)}, u32[]{:S(2)}) collective-permute-start(bf16[1024,512]{1,0:T(8,128)(2,1)S(1)} %pad_maximum_fusion.refs_0_), channel_id=1, source_target_pairs={{48,0},{200,8},{0,16},{216,24},{16,32},{232,40},{32,48},{248,56},{... | collective-permute-start | bytes 3145736 | tf_op jit(solution)/shard_map/ppermute | solution.py:144
  98.3 14.3 %collective-permute-start.23 = (bf16[1024,512]{1,0:T(8,128)(2,1)S(1)}, bf16[1024,512]{1,0:T(8,128)(2,1)S(1)}, u32[]{:S(2)}, u32[]{:S(2)}) collective-permute-start(bf16[1024,512]{1,0:T(8,128)(2,1)S(1)} %pad_maximum_fusion.refs_0_), channel_id=1, source_target_pairs={{16,0},{72,8},{32,16},{88,24},{48,32},{104,40},{0,48},{120,56},{80... | collective-permute-start | bytes 3145736 | tf_op jit(solution)/shard_map/ppermute | solution.py:144
  99.9 25.4 %collective-permute-start.27 = (bf16[1024,512]{1,0:T(8,128)(2,1)S(1)}, bf16[1024,512]{1,0:T(8,128)(2,1)S(1)}, u32[]{:S(2)}, u32[]{:S(2)}) collective-permute-start(bf16[1024,512]{1,0:T(8,128)(2,1)S(1)} %pad_maximum_fusion.refs_0_), channel_id=1, source_target_pairs={{0,8},{8,0},{16,24},{24,16},{32,40},{40,32},{48,56},{56,48},{64,72... | collective-permute-start | bytes 3145736 | tf_op jit(solution)/shard_map/ppermute | solution.py:149
  112.5 9.6 %collective-permute-start.26 = (bf16[512,512]{1,0:T(8,128)(2,1)S(1)}, bf16[512,512]{1,0:T(8,128)(2,1)S(1)}, u32[]{:S(2)}, u32[]{:S(2)}) collective-permute-start(bf16[512,512]{1,0:T(8,128)(2,1)S(1)} %slice.73), channel_id=1, source_target_pairs={{48,0},{200,8},{0,16},{216,24},{16,32},{232,40},{32,48},{248,56},{... | collective-permute-start | bytes 1572872 | tf_op jit(solution)/shard_map/ppermute | solution.py:144
  112.6 12.8 %collective-permute-start.25 = (bf16[512,512]{1,0:T(8,128)(2,1)S(1)}, bf16[512,512]{1,0:T(8,128)(2,1)S(1)}, u32[]{:S(2)}, u32[]{:S(2)}) collective-permute-start(bf16[512,512]{1,0:T(8,128)(2,1)S(1)} %slice.72), channel_id=1, source_target_pairs={{16,0},{72,8},{32,16},{88,24},{48,32},{104,40},{0,48},{120,56},{80... | collective-permute-start | bytes 1572872 | tf_op jit(solution)/shard_map/ppermute | solution.py:144
  115.3 12.3 %collective-permute-start.29 = (bf16[1024,512]{1,0:T(8,128)(2,1)S(1)}, bf16[1024,512]{1,0:T(8,128)(2,1)S(1)}, u32[]{:S(2)}, u32[]{:S(2)}) collective-permute-start(bf16[1024,512]{1,0:T(8,128)(2,1)S(1)} %collective-permute-done.24.refs_2_), channel_id=1, source_target_pairs={{0,8},{8,0},{16,24},{24,16},{32,40},{40,32},{48,56},{56,48},{64,72... | collective-permute-start | bytes 3145736 | tf_op jit(solution)/shard_map/ppermute | solution.py:149
  118.3 9.3 %collective-permute-start.28 = (bf16[1024,512]{1,0:T(8,128)(2,1)S(1)}, bf16[1024,512]{1,0:T(8,128)(2,1)S(1)}, u32[]{:S(2)}, u32[]{:S(2)}) collective-permute-start(bf16[1024,512]{1,0:T(8,128)(2,1)S(1)} %collective-permute-done.23.refs_1_), channel_id=1, source_target_pairs={{0,8},{8,0},{16,24},{24,16},{32,40},{40,32},{48,56},{56,48},{64,72... | collective-permute-start | bytes 3145736 | tf_op jit(solution)/shard_map/ppermute | solution.py:149
  122.1 4.8 %collective-permute-start.31 = (bf16[512,512]{1,0:T(8,128)(2,1)S(1)}, bf16[512,512]{1,0:T(8,128)(2,1)S(1)}, u32[]{:S(2)}, u32[]{:S(2)}) collective-permute-start(bf16[512,512]{1,0:T(8,128)(2,1)S(1)} %collective-permute-done.26.refs_4_), channel_id=1, source_target_pairs={{0,8},{8,0},{16,24},{24,16},{32,40},{40,32},{48,56},{56,48},{64,72... | collective-permute-start | bytes 1572872 | tf_op jit(solution)/shard_map/ppermute | solution.py:149
  125.4 2.3 %collective-permute-start.30 = (bf16[512,512]{1,0:T(8,128)(2,1)S(1)}, bf16[512,512]{1,0:T(8,128)(2,1)S(1)}, u32[]{:S(2)}, u32[]{:S(2)}) collective-permute-start(bf16[512,512]{1,0:T(8,128)(2,1)S(1)} %collective-permute-done.25.refs_3_), channel_id=1, source_target_pairs={{0,8},{8,0},{16,24},{24,16},{32,40},{40,32},{48,56},{56,48},{64,72... | collective-permute-start | bytes 1572872 | tf_op jit(solution)/shard_map/ppermute | solution.py:149
  129.2 8.8 %collective-permute-start.34 = (bf16[256,512]{1,0:T(8,128)(2,1)S(1)}, bf16[256,512]{1,0:T(8,128)(2,1)S(1)}, u32[]{:S(2)}, u32[]{:S(2)}) collective-permute-start(bf16[256,512]{1,0:T(8,128)(2,1)S(1)} %get-tuple-element.47), channel_id=1, source_target_pairs={{0,1},{1,2},{2,3},{3,4},{4,5},{5,6},{6,7},{7,0},{8,9},{9,10},{10,1... | collective-permute-start | bytes 786440 | tf_op jit(solution)/shard_map/ppermute | solution.py:167
  130.3 14.5 %collective-permute-start.38 = (bf16[128,512]{1,0:T(8,128)(2,1)S(1)}, bf16[128,512]{1,0:T(8,128)(2,1)S(1)}, u32[]{:S(2)}, u32[]{:S(2)}) collective-permute-start(bf16[128,512]{1,0:T(8,128)(2,1)S(1)} %get-tuple-element.51), channel_id=1, source_target_pairs={{0,6},{1,7},{2,0},{3,1},{4,2},{5,3},{6,4},{7,5},{8,14},{9,15},{10,... | collective-permute-start | bytes 393224 | tf_op jit(solution)/shard_map/ppermute | solution.py:167
  133.7 9.1 %collective-permute-start.35 = (bf16[128,512]{1,0:T(8,128)(2,1)S(1)}, bf16[128,512]{1,0:T(8,128)(2,1)S(1)}, u32[]{:S(2)}, u32[]{:S(2)}) collective-permute-start(bf16[128,512]{1,0:T(8,128)(2,1)S(1)} %get-tuple-element.52), channel_id=1, source_target_pairs={{0,2},{1,3},{2,4},{3,5},{4,6},{5,7},{6,0},{7,1},{8,10},{9,11},{10,... | collective-permute-start | bytes 393224 | tf_op jit(solution)/shard_map/ppermute | solution.py:167
  134.6 10.1 %collective-permute-start.37 = (bf16[256,512]{1,0:T(8,128)(2,1)S(1)}, bf16[256,512]{1,0:T(8,128)(2,1)S(1)}, u32[]{:S(2)}, u32[]{:S(2)}) collective-permute-start(bf16[256,512]{1,0:T(8,128)(2,1)S(1)} %get-tuple-element.50), channel_id=1, source_target_pairs={{0,7},{1,0},{2,1},{3,2},{4,3},{5,4},{6,5},{7,6},{8,15},{9,8},{10,9... | collective-permute-start | bytes 786440 | tf_op jit(solution)/shard_map/ppermute | solution.py:167
  137.4 11.8 %collective-permute-start.32 = (bf16[256,512]{1,0:T(8,128)(2,1)S(1)}, bf16[256,512]{1,0:T(8,128)(2,1)S(1)}, u32[]{:S(2)}, u32[]{:S(2)}) collective-permute-start(bf16[256,512]{1,0:T(8,128)(2,1)S(1)} %get-tuple-element.44), channel_id=1, source_target_pairs={{0,1},{1,2},{2,3},{3,4},{4,5},{5,6},{6,7},{7,0},{8,9},{9,10},{10,1... | collective-permute-start | bytes 786440 | tf_op jit(solution)/shard_map/ppermute | solution.py:167
  138.0 12.2 %collective-permute-start.33 = (bf16[256,512]{1,0:T(8,128)(2,1)S(1)}, bf16[256,512]{1,0:T(8,128)(2,1)S(1)}, u32[]{:S(2)}, u32[]{:S(2)}) collective-permute-start(bf16[256,512]{1,0:T(8,128)(2,1)S(1)} %get-tuple-element.45), channel_id=1, source_target_pairs={{0,7},{1,0},{2,1},{3,2},{4,3},{5,4},{6,5},{7,6},{8,15},{9,8},{10,9... | collective-permute-start | bytes 786440 | tf_op jit(solution)/shard_map/ppermute | solution.py:167
  142.8 15.3 %collective-permute-start.36 = (bf16[256,512]{1,0:T(8,128)(2,1)S(1)}, bf16[256,512]{1,0:T(8,128)(2,1)S(1)}, u32[]{:S(2)}, u32[]{:S(2)}) collective-permute-start(bf16[256,512]{1,0:T(8,128)(2,1)S(1)} %pad_maximum_fusion.3), channel_id=1, source_target_pairs={{0,2},{1,3},{2,4},{3,5},{4,6},{5,7},{6,0},{7,1},{8,10},{9,11},{10,... | collective-permute-start | bytes 786440 | tf_op jit(solution)/shard_map/ppermute | solution.py:167
  144.9 17.9 %collective-permute-start.39 = (bf16[256,512]{1,0:T(8,128)(2,1)S(1)}, bf16[256,512]{1,0:T(8,128)(2,1)S(1)}, u32[]{:S(2)}, u32[]{:S(2)}) collective-permute-start(bf16[256,512]{1,0:T(8,128)(2,1)S(1)} %pad_maximum_fusion.4), channel_id=1, source_target_pairs={{0,6},{1,7},{2,0},{3,1},{4,2},{5,3},{6,4},{7,5},{8,14},{9,15},{10,... | collective-permute-start | bytes 786440 | tf_op jit(solution)/shard_map/ppermute | solution.py:167

commit v5 on v4

--- a/solution.py
+++ b/solution.py
@@ -110,7 +110,7 @@
 
 
 SIDE = 4
-NEAR = (1, -1, 2)
+NEAR = (2, 1, -1)
 
 
 def held_blocks():

time: 166 us -> 165 us (level)
  starting transfers between devices: 62.9 us -> 59.6 us
  waiting for transfers between devices: 78.8 us -> 81 us
    ppermute x10, starting transfers between devices: 14.3 us -> 11.5 us  [swap(): return lax.ppermute(value, 'row', [(i, i ^ 1) for i in range(count)])]
  transfers between devices with their start and end apart: 40 -> 40, of which waited for: 23 -> 26; matrix products, arithmetic and copies ran while one was open for 5% -> 5% of each run, Pallas kernels for 3% -> 3%
where the time goes in v5:
time: 165 us; the launch traced here: 164 us
  waiting for transfers between devices  81 us (49%)
  starting transfers between devices  59.6 us (36%)
  Pallas kernels  13.9 us (8%)
  local copies, waits for them, and re-layouts  8.12 us (5%)
    ppermute x14, waiting for transfers between devices, pull(): return lax.ppermute(value, 'row', pairs)  41.5 us
    ppermute x16, waiting for transfers between devices, send(): lax.ppermute(value, 'col', [(i, (i + distance) % count) for i in range(co...  35.5 us
    ppermute x16, starting transfers between devices, send(): lax.ppermute(value, 'col', [(i, (i + distance) % count) for i in range(co...  27.3 us
    ppermute x14, starting transfers between devices, pull(): return lax.ppermute(value, 'row', pairs)  20.8 us
    ppermute x10, starting transfers between devices, swap(): return lax.ppermute(value, 'row', [(i, i ^ 1) for i in range(count)])  11.5 us
    pallas_call x4, Pallas kernels, aggregate_tiles(): pl.pallas_call(body, in_specs=[smem] * 3 + [vmem] * (1 + n_src), out_spec...  9.27 us
    pallas_call x2, Pallas kernels, node_mlp(): pl.pallas_call(body, in_specs=[vmem] * (4 + len(flat)), out_specs=[vmem]...  4.67 us
    ppermute x10, waiting for transfers between devices, swap(): return lax.ppermute(value, 'row', [(i, i ^ 1) for i in range(count)])  4.05 us
  transfers between devices with their start and end apart: 40, of which 26 were waited for; matrix products, arithmetic and copies ran while one was open for 5% of the time, Pallas kernels for 3%

profile of v5, /device:TPU:1, one launch (start us, length us, event | category | flops | bytes accessed | tf_op | source)
XLA Modules:
  0.0 164.4 jit_solution(3294901052876004491)
XLA Ops:
  0.0 3.7 %collective-permute-start = (bf16[256,512]{1,0:T(8,128)(2,1)}, bf16[256,512]{1,0:T(8,128)(2,1)S(1)}, u32[]{:S(2)}, u32[]{:S(2)}) collective-permute-start(bf16[256,512]{1,0:T(8,128)(2,1)} %refs_0_.1), channel_id=1, source_target_pairs={{128,0},{40,8},{144,16},{56,24},{160,32},{8,40},{176,48},{24,56},{... | collective-permute-start | bytes 786440 | tf_op jit(solution)/shard_map/ppermute | solution.py:144
  3.7 0.8 collective-permute-start.1
  5.2 1.7 %constant_dynamic-update-slice_fusion.3 = bf16[1024,512]{1,0:T(8,128)(2,1)} fusion(bf16[256,512]{1,0:T(8,128)(2,1)} %refs_0_.1), kind=kLoop, calls=%fused_computation.31 | loop fusion | bytes 524288
  6.9 0.8 collective-permute-done
  7.7 0.7 constant_dynamic-update-slice_fusion.2
  8.4 2.8 %collective-permute-done.1 = bf16[256,512]{1,0:T(8,128)(2,1)S(1)} collective-permute-done((bf16[256,512]{1,0:T(8,128)(2,1)}, bf16[256,512]{1,0:T(8,128)(2,1)S(1)}, u32[]{:S(2)}, u32[]{:S(2)}) %collective-permute-start.1) | collective-permute-done | bytes 262176 | tf_op jit(solution)/shard_map/ppermute | solution.py:144
  12.0 0.7 constant_dynamic-update-slice_fusion.refs_0_
  12.7 2.2 %collective-permute-start.5 = (bf16[1024,512]{1,0:T(8,128)(2,1)}, bf16[1024,512]{1,0:T(8,128)(2,1)}, u32[]{:S(2)}, u32[]{:S(2)}) collective-permute-start(bf16[1024,512]{1,0:T(8,128)(2,1)} %constant_dynamic-update-slice_fusion.refs_0_), channel_id=1, source_target_pairs={{0,8},{8,0},{16,24},{24,16},{32,40},{40,32},{48,56},{56,48},{64,72... | collective-permute-start | bytes 3145736 | tf_op jit(solution)/shard_map/ppermute | solution.py:149
  15.0 2.5 %collective-permute-start.3 = (bf16[1024,512]{1,0:T(8,128)(2,1)}, bf16[1024,512]{1,0:T(8,128)(2,1)}, u32[]{:S(2)}, u32[]{:S(2)}) collective-permute-start(bf16[1024,512]{1,0:T(8,128)(2,1)} %constant_dynamic-update-slice_fusion.refs_0_), channel_id=1, source_target_pairs={{16,0},{72,8},{32,16},{88,24},{48,32},{104,40},{0,48},{120,56},{80... | collective-permute-start | bytes 3145736 | tf_op jit(solution)/shard_map/ppermute | solution.py:144
  17.7 2.8 %reshape.13.matrix_ref = bf16[16,128,512]{2,1,0:T(8,128)(2,1)S(1)} reshape(bf16[16,1,128,4,128]{4,3,2,1,0:T(4,128)(2,1)} %param.12) | data formatting | bytes 4194304 | tf_op jit(solution)/shard_map/reshape | solution.py:206
  20.6 9.6 %collective-permute-done.4.refs_2_ = bf16[1024,512]{1,0:T(8,128)(2,1)S(1)} collective-permute-done((bf16[1024,512]{1,0:T(8,128)(2,1)}, bf16[1024,512]{1,0:T(8,128)(2,1)S(1)}, u32[]{:S(2)}, u32[]{:S(2)}) %collective-permute-start.4) | collective-permute-done | bytes 1048608 | tf_op jit(solution)/shard_map/ppermute | solution.py:144
  30.2 1.1 slice.52
  31.3 0.9 collective-permute-start.8
  32.3 0.7 collective-permute-start.7
  33.0 0.7 collective-permute-start.9
  33.8 2.1 %collective-permute-start.6 = (bf16[512,512]{1,0:T(8,128)(2,1)S(1)}, bf16[512,512]{1,0:T(8,128)(2,1)S(1)}, u32[]{:S(2)}, u32[]{:S(2)}) collective-permute-start(bf16[512,512]{1,0:T(8,128)(2,1)S(1)} %slice.52), channel_id=1, source_target_pairs={{16,0},{72,8},{32,16},{88,24},{48,32},{104,40},{0,48},{120,56},{80... | collective-permute-start | bytes 1572872 | tf_op jit(solution)/shard_map/ppermute | solution.py:144
  35.9 6.0 %collective-permute-done.7.refs_4_ = bf16[512,512]{1,0:T(8,128)(2,1)S(1)} collective-permute-done((bf16[512,512]{1,0:T(8,128)(2,1)S(1)}, bf16[512,512]{1,0:T(8,128)(2,1)S(1)}, u32[]{:S(2)}, u32[]{:S(2)}) %collective-permute-start.7) | collective-permute-done | bytes 524320 | tf_op jit(solution)/shard_map/ppermute | solution.py:144
  41.9 1.0 collective-permute-start.11
  43.4 1.0 collective-permute-done.11.refs_9_
  44.4 0.7 collective-permute-done.10.refs_8_
  45.2 2.8 %aggregate_tiles.5 = (bf16[256,512]{1,0:T(8,128)(2,1)S(1)}, bf16[256,512]{1,0:T(8,128)(2,1)S(1)}, bf16[256,512]{1,0:T(8,128)(2,1)S(1)}) custom-call(s32[4]{0:T(128)S(1)} %pad_add_fusion.here_ref, s32[32]{0:T(128)S(1)} %bitcast.9, s32[64]{0:T(128)S(1)} %reshape.15.index_ref, bf16[16,128,512]{2,1,0:T(8,128)(2,1)S(1)} %reshape.13.matrix_ref, ...), custom_call_target="tpu_custom_call" | custom-call | tf_op jit(solution)/shard_map/aggregate_tiles/pallas_call | solution.py:54
  48.0 1.4 collective-permute-start.14
  49.7 5.2 %collective-permute-start.18 = (bf16[128,512]{1,0:T(8,128)(2,1)S(1)}, bf16[128,512]{1,0:T(8,128)(2,1)S(1)}, u32[]{:S(2)}, u32[]{:S(2)}) collective-permute-start(bf16[128,512]{1,0:T(8,128)(2,1)S(1)} %get-tuple-element.53), channel_id=1, source_target_pairs={{0,6},{1,7},{2,0},{3,1},{4,2},{5,3},{6,4},{7,5},{8,14},{9,15},{10,... | collective-permute-start | bytes 393224 | tf_op jit(solution)/shard_map/ppermute | solution.py:167
  54.9 2.4 %collective-permute-start.17 = (bf16[256,512]{1,0:T(8,128)(2,1)S(1)}, bf16[256,512]{1,0:T(8,128)(2,1)S(1)}, u32[]{:S(2)}, u32[]{:S(2)}) collective-permute-start(bf16[256,512]{1,0:T(8,128)(2,1)S(1)} %get-tuple-element.42), channel_id=1, source_target_pairs={{0,7},{1,0},{2,1},{3,2},{4,3},{5,4},{6,5},{7,6},{8,15},{9,8},{10,9... | collective-permute-start | bytes 786440 | tf_op jit(solution)/shard_map/ppermute | solution.py:167
  57.3 3.2 %aggregate_tiles.4 = (bf16[256,512]{1,0:T(8,128)(2,1)S(1)}, bf16[256,512]{1,0:T(8,128)(2,1)S(1)}, bf16[256,512]{1,0:T(8,128)(2,1)S(1)}, bf16[256,512]{1,0:T(8,128)(2,1)S(1)}, bf16[256,512]{1,0:T(8,128)(2,1)S(1)}) custom-call(s32[4]{0:T(128)S(1)} %pad_add_fusion.here_ref, s32[32]{0:T(128)S(1)} %bitcast.10, s32[64]{0:T(128)S(1)} %reshape.15.index_ref, ...), custom_call_target="tpu_custom_call" | custom-call | tf_op jit(solution)/shard_map/aggregate_tiles/pallas_call | solution.py:54
  60.6 2.7 %collective-permute-start.13 = (bf16[256,512]{1,0:T(8,128)(2,1)S(1)}, bf16[256,512]{1,0:T(8,128)(2,1)S(1)}, u32[]{:S(2)}, u32[]{:S(2)}) collective-permute-start(bf16[256,512]{1,0:T(8,128)(2,1)S(1)} %get-tuple-element.37), channel_id=1, source_target_pairs={{0,7},{1,0},{2,1},{3,2},{4,3},{5,4},{6,5},{7,6},{8,15},{9,8},{10,9... | collective-permute-start | bytes 786440 | tf_op jit(solution)/shard_map/ppermute | solution.py:167
  64.2 2.0 %collective-permute-done.17 = bf16[256,512]{1,0:T(8,128)(2,1)S(1)} collective-permute-done((bf16[256,512]{1,0:T(8,128)(2,1)S(1)}, bf16[256,512]{1,0:T(8,128)(2,1)S(1)}, u32[]{:S(2)}, u32[]{:S(2)}) %collective-permute-start.17) | collective-permute-done | bytes 262176 | tf_op jit(solution)/shard_map/ppermute | solution.py:167
  66.4 1.7 %collective-permute-start.19 = (bf16[256,512]{1,0:T(8,128)(2,1)S(1)}, bf16[256,512]{1,0:T(8,128)(2,1)S(1)}, u32[]{:S(2)}, u32[]{:S(2)}) collective-permute-start(bf16[256,512]{1,0:T(8,128)(2,1)S(1)} %pad_maximum_fusion.2), channel_id=1, source_target_pairs={{0,6},{1,7},{2,0},{3,1},{4,2},{5,3},{6,4},{7,5},{8,14},{9,15},{10,... | collective-permute-start | bytes 786440 | tf_op jit(solution)/shard_map/ppermute | solution.py:167
  68.2 2.7 %collective-permute-done.12.refs_2_ = bf16[256,512]{1,0:T(8,128)(2,1)S(1)} collective-permute-done((bf16[256,512]{1,0:T(8,128)(2,1)S(1)}, bf16[256,512]{1,0:T(8,128)(2,1)S(1)}, u32[]{:S(2)}, u32[]{:S(2)}) %collective-permute-start.12) | collective-permute-done | bytes 262176 | tf_op jit(solution)/shard_map/ppermute | solution.py:167
  70.9 0.9 collective-permute-done.13.refs_3_
  71.8 8.5 %collective-permute-done.16.refs_4_ = bf16[256,512]{1,0:T(8,128)(2,1)S(1)} collective-permute-done((bf16[256,512]{1,0:T(8,128)(2,1)S(1)}, bf16[256,512]{1,0:T(8,128)(2,1)S(1)}, u32[]{:S(2)}, u32[]{:S(2)}) %collective-permute-start.16) | collective-permute-done | bytes 262176 | tf_op jit(solution)/shard_map/ppermute | solution.py:167
  80.3 2.7 %collective-permute-done.19.refs_5_ = bf16[256,512]{1,0:T(8,128)(2,1)S(1)} collective-permute-done((bf16[256,512]{1,0:T(8,128)(2,1)S(1)}, bf16[256,512]{1,0:T(8,128)(2,1)S(1)}, u32[]{:S(2)}, u32[]{:S(2)}) %collective-permute-start.19) | collective-permute-done | bytes 262176 | tf_op jit(solution)/shard_map/ppermute | solution.py:167
  83.0 2.0 %node_mlp.2.refs_0_ = bf16[256,512]{1,0:T(8,128)(2,1)S(1)} custom-call(f32[2,256,512]{2,1,0:T(8,128)S(1)} %broadcast_multiply_fusion.scale_ref, bf16[256,512]{1,0:T(8,128)(2,1)S(1)} %convolution_convert_fusion.shift_ref, bf16[2,512,2048]{2,1,0:T(8,128)(2,1)S(1)} %copy-done.1, bf16[2,2048,512]{2,1,0:T(8,128)(2,1)S(1)} %copy-done.2, ...), custom_call_target="tpu_custom_call" | custom-call | tf_op jit(solution)/shard_map/node_mlp/pallas_call | solution.py:102
  85.0 0.8 collective-permute-start.22
  85.8 2.6 %collective-permute-start.21 = (bf16[256,512]{1,0:T(8,128)(2,1)S(1)}, bf16[256,512]{1,0:T(8,128)(2,1)S(1)}, u32[]{:S(2)}, u32[]{:S(2)}) collective-permute-start(bf16[256,512]{1,0:T(8,128)(2,1)S(1)} %node_mlp.2.refs_0_), channel_id=1, source_target_pairs={{64,0},{24,8},{80,16},{40,24},{96,32},{56,40},{112,48},{8,56},{128... | collective-permute-start | bytes 786440 | tf_op jit(solution)/shard_map/ppermute | solution.py:144
  88.4 1.1 collective-permute-start.20
  89.5 2.9 %collective-permute-done.22 = bf16[256,512]{1,0:T(8,128)(2,1)S(1)} collective-permute-done((bf16[256,512]{1,0:T(8,128)(2,1)S(1)}, bf16[256,512]{1,0:T(8,128)(2,1)S(1)}, u32[]{:S(2)}, u32[]{:S(2)}) %collective-permute-start.22) | collective-permute-done | bytes 262176 | tf_op jit(solution)/shard_map/ppermute | solution.py:144
  92.4 2.2 %collective-permute-done.21 = bf16[256,512]{1,0:T(8,128)(2,1)S(1)} collective-permute-done((bf16[256,512]{1,0:T(8,128)(2,1)S(1)}, bf16[256,512]{1,0:T(8,128)(2,1)S(1)}, u32[]{:S(2)}, u32[]{:S(2)}) %collective-permute-start.21) | collective-permute-done | bytes 262176 | tf_op jit(solution)/shard_map/ppermute | solution.py:144
  94.5 1.8 %collective-permute-done.20 = bf16[256,512]{1,0:T(8,128)(2,1)S(1)} collective-permute-done((bf16[256,512]{1,0:T(8,128)(2,1)S(1)}, bf16[256,512]{1,0:T(8,128)(2,1)S(1)}, u32[]{:S(2)}, u32[]{:S(2)}) %collective-permute-start.20) | collective-permute-done | bytes 262176 | tf_op jit(solution)/shard_map/ppermute | solution.py:144
  96.8 2.4 %collective-permute-start.23 = (bf16[1024,512]{1,0:T(8,128)(2,1)S(1)}, bf16[1024,512]{1,0:T(8,128)(2,1)S(1)}, u32[]{:S(2)}, u32[]{:S(2)}) collective-permute-start(bf16[1024,512]{1,0:T(8,128)(2,1)S(1)} %pad_maximum_fusion.refs_0_), channel_id=1, source_target_pairs={{16,0},{72,8},{32,16},{88,24},{48,32},{104,40},{0,48},{120,56},{80... | collective-permute-start | bytes 3145736 | tf_op jit(solution)/shard_map/ppermute | solution.py:144
  99.2 1.5 collective-permute-start.27
  100.7 10.9 %collective-permute-done.24.refs_2_ = bf16[1024,512]{1,0:T(8,128)(2,1)S(1)} collective-permute-done((bf16[1024,512]{1,0:T(8,128)(2,1)S(1)}, bf16[1024,512]{1,0:T(8,128)(2,1)S(1)}, u32[]{:S(2)}, u32[]{:S(2)}) %collective-permute-start.24) | collective-permute-done | bytes 1048608 | tf_op jit(solution)/shard_map/ppermute | solution.py:144
  111.8 2.7 %collective-permute-start.25 = (bf16[512,512]{1,0:T(8,128)(2,1)S(1)}, bf16[512,512]{1,0:T(8,128)(2,1)S(1)}, u32[]{:S(2)}, u32[]{:S(2)}) collective-permute-start(bf16[512,512]{1,0:T(8,128)(2,1)S(1)} %slice.72), channel_id=1, source_target_pairs={{16,0},{72,8},{32,16},{88,24},{48,32},{104,40},{0,48},{120,56},{80... | collective-permute-start | bytes 1572872 | tf_op jit(solution)/shard_map/ppermute | solution.py:144
  114.6 2.3 %collective-permute-start.29 = (bf16[1024,512]{1,0:T(8,128)(2,1)S(1)}, bf16[1024,512]{1,0:T(8,128)(2,1)S(1)}, u32[]{:S(2)}, u32[]{:S(2)}) collective-permute-start(bf16[1024,512]{1,0:T(8,128)(2,1)S(1)} %collective-permute-done.24.refs_2_), channel_id=1, source_target_pairs={{0,8},{8,0},{16,24},{24,16},{32,40},{40,32},{48,56},{56,48},{64,72... | collective-permute-start | bytes 3145736 | tf_op jit(solution)/shard_map/ppermute | solution.py:149
  116.9 4.4 %collective-permute-done.26.refs_4_ = bf16[512,512]{1,0:T(8,128)(2,1)S(1)} collective-permute-done((bf16[512,512]{1,0:T(8,128)(2,1)S(1)}, bf16[512,512]{1,0:T(8,128)(2,1)S(1)}, u32[]{:S(2)}, u32[]{:S(2)}) %collective-permute-start.26) | collective-permute-done | bytes 524320 | tf_op jit(solution)/shard_map/ppermute | solution.py:144
  121.3 2.6 %collective-permute-start.31 = (bf16[512,512]{1,0:T(8,128)(2,1)S(1)}, bf16[512,512]{1,0:T(8,128)(2,1)S(1)}, u32[]{:S(2)}, u32[]{:S(2)}) collective-permute-start(bf16[512,512]{1,0:T(8,128)(2,1)S(1)} %collective-permute-done.26.refs_4_), channel_id=1, source_target_pairs={{0,8},{8,0},{16,24},{24,16},{32,40},{40,32},{48,56},{56,48},{64,72... | collective-permute-start | bytes 1572872 | tf_op jit(solution)/shard_map/ppermute | solution.py:149
  123.9 1.5 collective-permute-done.31.refs_9_
  125.5 0.7 collective-permute-done.30.refs_8_
  126.2 1.5 aggregate_tiles.7
  127.7 1.2 collective-permute-start.34
  128.9 3.3 %collective-permute-start.38 = (bf16[128,512]{1,0:T(8,128)(2,1)S(1)}, bf16[128,512]{1,0:T(8,128)(2,1)S(1)}, u32[]{:S(2)}, u32[]{:S(2)}) collective-permute-start(bf16[128,512]{1,0:T(8,128)(2,1)S(1)} %get-tuple-element.51), channel_id=1, source_target_pairs={{0,6},{1,7},{2,0},{3,1},{4,2},{5,3},{6,4},{7,5},{8,14},{9,15},{10,... | collective-permute-start | bytes 393224 | tf_op jit(solution)/shard_map/ppermute | solution.py:167
  132.2 0.8 collective-permute-start.35
  133.1 1.1 collective-permute-start.37
  134.1 1.8 %aggregate_tiles.6 = (bf16[256,512]{1,0:T(8,128)(2,1)S(1)}, bf16[256,512]{1,0:T(8,128)(2,1)S(1)}, bf16[256,512]{1,0:T(8,128)(2,1)S(1)}, bf16[256,512]{1,0:T(8,128)(2,1)S(1)}, bf16[256,512]{1,0:T(8,128)(2,1)S(1)}) custom-call(s32[4]{0:T(128)S(1)} %pad_add_fusion.here_ref, s32[32]{0:T(128)S(1)} %bitcast.12, s32[64]{0:T(128)S(1)} %reshape.15.index_ref, ...), custom_call_target="tpu_custom_call" | custom-call | tf_op jit(solution)/shard_map/aggregate_tiles/pallas_call | solution.py:54
  136.5 2.3 %collective-permute-start.33 = (bf16[256,512]{1,0:T(8,128)(2,1)S(1)}, bf16[256,512]{1,0:T(8,128)(2,1)S(1)}, u32[]{:S(2)}, u32[]{:S(2)}) collective-permute-start(bf16[256,512]{1,0:T(8,128)(2,1)S(1)} %get-tuple-element.45), channel_id=1, source_target_pairs={{0,7},{1,0},{2,1},{3,2},{4,3},{5,4},{6,5},{7,6},{8,15},{9,8},{10,9... | collective-permute-start | bytes 786440 | tf_op jit(solution)/shard_map/ppermute | solution.py:167
  138.9 2.5 %collective-permute-done.35 = bf16[128,512]{1,0:T(8,128)(2,1)S(1)} collective-permute-done((bf16[128,512]{1,0:T(8,128)(2,1)S(1)}, bf16[128,512]{1,0:T(8,128)(2,1)S(1)}, u32[]{:S(2)}, u32[]{:S(2)}) %collective-permute-start.35) | collective-permute-done | bytes 131104 | tf_op jit(solution)/shard_map/ppermute | solution.py:167
  141.4 1.0 collective-permute-start.36
  142.4 0.7 collective-permute-done.37
  143.3 3.6 %collective-permute-start.39 = (bf16[256,512]{1,0:T(8,128)(2,1)S(1)}, bf16[256,512]{1,0:T(8,128)(2,1)S(1)}, u32[]{:S(2)}, u32[]{:S(2)}) collective-permute-start(bf16[256,512]{1,0:T(8,128)(2,1)S(1)} %pad_maximum_fusion.4), channel_id=1, source_target_pairs={{0,6},{1,7},{2,0},{3,1},{4,2},{5,3},{6,4},{7,5},{8,14},{9,15},{10,... | collective-permute-start | bytes 786440 | tf_op jit(solution)/shard_map/ppermute | solution.py:167
  146.9 0.9 collective-permute-done.32.refs_2_
  147.8 1.0 collective-permute-done.33.refs_3_
  148.7 7.8 %collective-permute-done.36.refs_4_ = bf16[256,512]{1,0:T(8,128)(2,1)S(1)} collective-permute-done((bf16[256,512]{1,0:T(8,128)(2,1)S(1)}, bf16[256,512]{1,0:T(8,128)(2,1)S(1)}, u32[]{:S(2)}, u32[]{:S(2)}) %collective-permute-start.36) | collective-permute-done | bytes 262176 | tf_op jit(solution)/shard_map/ppermute | solution.py:167
  156.5 5.2 %collective-permute-done.39.refs_5_ = bf16[256,512]{1,0:T(8,128)(2,1)S(1)} collective-permute-done((bf16[256,512]{1,0:T(8,128)(2,1)S(1)}, bf16[256,512]{1,0:T(8,128)(2,1)S(1)}, u32[]{:S(2)}, u32[]{:S(2)}) %collective-permute-start.39) | collective-permute-done | bytes 262176 | tf_op jit(solution)/shard_map/ppermute | solution.py:167
  161.7 2.7 %node_mlp.3 = bf16[256,512]{1,0:T(8,128)(2,1)} custom-call(f32[2,256,512]{2,1,0:T(8,128)S(1)} %broadcast_multiply_fusion.scale_ref, bf16[256,512]{1,0:T(8,128)(2,1)S(1)} %convolution_convert_fusion.shift_ref, bf16[2,512,2048]{2,1,0:T(8,128)(2,1)S(1)} %copy-done.1, bf16[2,2048,512]{2,1,0:T(8,128)(2,1)S(1)} %copy-done.2, ...), custom_call_target="tpu_custom_call" | custom-call | tf_op jit(solution)/shard_map/node_mlp/pallas_call | solution.py:102
  (76 shorter events, 5.4 us)
Async XLA Ops:
  0.0 49.4 %copy-start = (bf16[128,512]{1,0:T(8,128)(2,1)S(1)}, bf16[128,512]{1,0:T(8,128)(2,1)}, u32[]{:S(2)}) copy-start(bf16[128,512]{1,0:T(8,128)(2,1)} %param.17) | copy-start | bytes 393220
  0.0 17.5 %copy-start.7 = (s32[16,1,4]{0,2,1:T(4,128)S(1)}, s32[16,1,4]{0,2,1:T(4,128)}, u32[]{:S(2)}) copy-start(s32[16,1,4]{0,2,1:T(4,128)} %param.13) | copy-start | bytes 772
  0.0 7.7 %collective-permute-start = (bf16[256,512]{1,0:T(8,128)(2,1)}, bf16[256,512]{1,0:T(8,128)(2,1)S(1)}, u32[]{:S(2)}, u32[]{:S(2)}) collective-permute-start(bf16[256,512]{1,0:T(8,128)(2,1)} %refs_0_.1), channel_id=1, source_target_pairs={{128,0},{40,8},{144,16},{56,24},{160,32},{8,40},{176,48},{24,56},{... | collective-permute-start | bytes 786440 | tf_op jit(solution)/shard_map/ppermute | solution.py:144
  3.7 7.5 %collective-permute-start.1 = (bf16[256,512]{1,0:T(8,128)(2,1)}, bf16[256,512]{1,0:T(8,128)(2,1)S(1)}, u32[]{:S(2)}, u32[]{:S(2)}) collective-permute-start(bf16[256,512]{1,0:T(8,128)(2,1)} %refs_0_.1), channel_id=1, source_target_pairs={{64,0},{24,8},{80,16},{40,24},{96,32},{56,40},{112,48},{8,56},{128... | collective-permute-start | bytes 786440 | tf_op jit(solution)/shard_map/ppermute | solution.py:144
  4.5 7.4 %collective-permute-start.2 = (bf16[256,512]{1,0:T(8,128)(2,1)}, bf16[256,512]{1,0:T(8,128)(2,1)S(1)}, u32[]{:S(2)}, u32[]{:S(2)}) collective-permute-start(bf16[256,512]{1,0:T(8,128)(2,1)} %refs_0_.1), channel_id=1, source_target_pairs={{192,0},{56,8},{208,16},{8,24},{224,32},{24,40},{240,48},{40,56},{... | collective-permute-start | bytes 786440 | tf_op jit(solution)/shard_map/ppermute | solution.py:144
  12.7 7.9 %collective-permute-start.5 = (bf16[1024,512]{1,0:T(8,128)(2,1)}, bf16[1024,512]{1,0:T(8,128)(2,1)}, u32[]{:S(2)}, u32[]{:S(2)}) collective-permute-start(bf16[1024,512]{1,0:T(8,128)(2,1)} %constant_dynamic-update-slice_fusion.refs_0_), channel_id=1, source_target_pairs={{0,8},{8,0},{16,24},{24,16},{32,40},{40,32},{48,56},{56,48},{64,72... | collective-permute-start | bytes 3145736 | tf_op jit(solution)/shard_map/ppermute | solution.py:149
  14.9 15.4 %collective-permute-start.4 = (bf16[1024,512]{1,0:T(8,128)(2,1)}, bf16[1024,512]{1,0:T(8,128)(2,1)S(1)}, u32[]{:S(2)}, u32[]{:S(2)}) collective-permute-start(bf16[1024,512]{1,0:T(8,128)(2,1)} %constant_dynamic-update-slice_fusion.refs_0_), channel_id=1, source_target_pairs={{48,0},{200,8},{0,16},{216,24},{16,32},{232,40},{32,48},{248,56},{... | collective-permute-start | bytes 3145736 | tf_op jit(solution)/shard_map/ppermute | solution.py:144
  15.0 15.2 %collective-permute-start.3 = (bf16[1024,512]{1,0:T(8,128)(2,1)}, bf16[1024,512]{1,0:T(8,128)(2,1)}, u32[]{:S(2)}, u32[]{:S(2)}) collective-permute-start(bf16[1024,512]{1,0:T(8,128)(2,1)} %constant_dynamic-update-slice_fusion.refs_0_), channel_id=1, source_target_pairs={{16,0},{72,8},{32,16},{88,24},{48,32},{104,40},{0,48},{120,56},{80... | collective-permute-start | bytes 3145736 | tf_op jit(solution)/shard_map/ppermute | solution.py:144
  20.5 22.6 %copy-start.5 = (bf16[16,512]{1,0:T(8,128)(2,1)S(1)}, bf16[16,512]{1,0:T(8,128)(2,1)}, u32[]{:S(2)}) copy-start(bf16[16,512]{1,0:T(8,128)(2,1)} %param.18) | copy-start | bytes 49156
  20.5 22.6 %copy-start.8 = (s32[256]{0:T(256)S(1)}, s32[256]{0:T(256)}, u32[]{:S(2)}) copy-start(s32[256]{0:T(256)} %param.16) | copy-start | bytes 3076
  20.5 24.7 %copy-start.4 = (s32[1,1,32,1]{2,3,1,0:T(1,128)S(1)}, s32[1,1,32,1]{2,3,1,0:T(1,128)}, u32[]{:S(2)}) copy-start(s32[1,1,32,1]{2,3,1,0:T(1,128)} %param.14) | copy-start | bytes 388
  31.3 12.1 %collective-permute-start.8 = (bf16[1024,512]{1,0:T(8,128)(2,1)}, bf16[1024,512]{1,0:T(8,128)(2,1)S(1)}, u32[]{:S(2)}, u32[]{:S(2)}) collective-permute-start(bf16[1024,512]{1,0:T(8,128)(2,1)} %collective-permute-done.3.refs_1_), channel_id=1, source_target_pairs={{0,8},{8,0},{16,24},{24,16},{32,40},{40,32},{48,56},{56,48},{64,72... | collective-permute-start | bytes 3145736 | tf_op jit(solution)/shard_map/ppermute | solution.py:149
  32.3 9.6 %collective-permute-start.7 = (bf16[512,512]{1,0:T(8,128)(2,1)S(1)}, bf16[512,512]{1,0:T(8,128)(2,1)S(1)}, u32[]{:S(2)}, u32[]{:S(2)}) collective-permute-start(bf16[512,512]{1,0:T(8,128)(2,1)S(1)} %slice.53), channel_id=1, source_target_pairs={{48,0},{200,8},{0,16},{216,24},{16,32},{232,40},{32,48},{248,56},{... | collective-permute-start | bytes 1572872 | tf_op jit(solution)/shard_map/ppermute | solution.py:144
  33.0 10.4 %collective-permute-start.9 = (bf16[1024,512]{1,0:T(8,128)(2,1)S(1)}, bf16[1024,512]{1,0:T(8,128)(2,1)S(1)}, u32[]{:S(2)}, u32[]{:S(2)}) collective-permute-start(bf16[1024,512]{1,0:T(8,128)(2,1)S(1)} %collective-permute-done.4.refs_2_), channel_id=1, source_target_pairs={{0,8},{8,0},{16,24},{24,16},{32,40},{40,32},{48,56},{56,48},{64,72... | collective-permute-start | bytes 3145736 | tf_op jit(solution)/shard_map/ppermute | solution.py:149
  33.8 9.1 %collective-permute-start.6 = (bf16[512,512]{1,0:T(8,128)(2,1)S(1)}, bf16[512,512]{1,0:T(8,128)(2,1)S(1)}, u32[]{:S(2)}, u32[]{:S(2)}) collective-permute-start(bf16[512,512]{1,0:T(8,128)(2,1)S(1)} %slice.52), channel_id=1, source_target_pairs={{16,0},{72,8},{32,16},{88,24},{48,32},{104,40},{0,48},{120,56},{80... | collective-permute-start | bytes 1572872 | tf_op jit(solution)/shard_map/ppermute | solution.py:144
  41.9 2.5 %collective-permute-start.11 = (bf16[512,512]{1,0:T(8,128)(2,1)S(1)}, bf16[512,512]{1,0:T(8,128)(2,1)S(1)}, u32[]{:S(2)}, u32[]{:S(2)}) collective-permute-start(bf16[512,512]{1,0:T(8,128)(2,1)S(1)} %collective-permute-done.7.refs_4_), channel_id=1, source_target_pairs={{0,8},{8,0},{16,24},{24,16},{32,40},{40,32},{48,56},{56,48},{64,72... | collective-permute-start | bytes 1572872 | tf_op jit(solution)/shard_map/ppermute | solution.py:149
  42.9 2.3 %collective-permute-start.10 = (bf16[512,512]{1,0:T(8,128)(2,1)S(1)}, bf16[512,512]{1,0:T(8,128)(2,1)S(1)}, u32[]{:S(2)}, u32[]{:S(2)}) collective-permute-start(bf16[512,512]{1,0:T(8,128)(2,1)S(1)} %collective-permute-done.6.refs_3_), channel_id=1, source_target_pairs={{0,8},{8,0},{16,24},{24,16},{32,40},{40,32},{48,56},{56,48},{64,72... | collective-permute-start | bytes 1572872 | tf_op jit(solution)/shard_map/ppermute | solution.py:149
  43.4 6.0 %copy-start.9 = (s32[256]{0:T(256)S(1)}, s32[256]{0:T(256)}, u32[]{:S(2)}) copy-start(s32[256]{0:T(256)} %param.15) | copy-start | bytes 3076
  48.0 12.7 %collective-permute-start.14 = (bf16[256,512]{1,0:T(8,128)(2,1)S(1)}, bf16[256,512]{1,0:T(8,128)(2,1)S(1)}, u32[]{:S(2)}, u32[]{:S(2)}) collective-permute-start(bf16[256,512]{1,0:T(8,128)(2,1)S(1)} %get-tuple-element.39), channel_id=1, source_target_pairs={{0,1},{1,2},{2,3},{3,4},{4,5},{5,6},{6,7},{7,0},{8,9},{9,10},{10,1... | collective-permute-start | bytes 786440 | tf_op jit(solution)/shard_map/ppermute | solution.py:167
  49.7 16.6 %collective-permute-start.18 = (bf16[128,512]{1,0:T(8,128)(2,1)S(1)}, bf16[128,512]{1,0:T(8,128)(2,1)S(1)}, u32[]{:S(2)}, u32[]{:S(2)}) collective-permute-start(bf16[128,512]{1,0:T(8,128)(2,1)S(1)} %get-tuple-element.53), channel_id=1, source_target_pairs={{0,6},{1,7},{2,0},{3,1},{4,2},{5,3},{6,4},{7,5},{8,14},{9,15},{10,... | collective-permute-start | bytes 393224 | tf_op jit(solution)/shard_map/ppermute | solution.py:167
  54.9 9.2 %collective-permute-start.15 = (bf16[128,512]{1,0:T(8,128)(2,1)S(1)}, bf16[128,512]{1,0:T(8,128)(2,1)S(1)}, u32[]{:S(2)}, u32[]{:S(2)}) collective-permute-start(bf16[128,512]{1,0:T(8,128)(2,1)S(1)} %get-tuple-element.54), channel_id=1, source_target_pairs={{0,2},{1,3},{2,4},{3,5},{4,6},{5,7},{6,0},{7,1},{8,10},{9,11},{10,... | collective-permute-start | bytes 393224 | tf_op jit(solution)/shard_map/ppermute | solution.py:167
  54.9 11.3 %collective-permute-start.17 = (bf16[256,512]{1,0:T(8,128)(2,1)S(1)}, bf16[256,512]{1,0:T(8,128)(2,1)S(1)}, u32[]{:S(2)}, u32[]{:S(2)}) collective-permute-start(bf16[256,512]{1,0:T(8,128)(2,1)S(1)} %get-tuple-element.42), channel_id=1, source_target_pairs={{0,7},{1,0},{2,1},{3,2},{4,3},{5,4},{6,5},{7,6},{8,15},{9,8},{10,9... | collective-permute-start | bytes 786440 | tf_op jit(solution)/shard_map/ppermute | solution.py:167
  57.3 25.7 %copy-start.2 = (bf16[2,2048,512]{2,1,0:T(8,128)(2,1)S(1)}, bf16[2,2048,512]{2,1,0:T(8,128)(2,1)}, u32[]{:S(2)}) copy-start(bf16[2,2048,512]{2,1,0:T(8,128)(2,1)} %w_out_ref.3) | copy-start | bytes 12582916
  60.5 10.4 %collective-permute-start.12 = (bf16[256,512]{1,0:T(8,128)(2,1)S(1)}, bf16[256,512]{1,0:T(8,128)(2,1)S(1)}, u32[]{:S(2)}, u32[]{:S(2)}) collective-permute-start(bf16[256,512]{1,0:T(8,128)(2,1)S(1)} %get-tuple-element.36), channel_id=1, source_target_pairs={{0,1},{1,2},{2,3},{3,4},{4,5},{5,6},{6,7},{7,0},{8,9},{9,10},{10,1... | collective-permute-start | bytes 786440 | tf_op jit(solution)/shard_map/ppermute | solution.py:167
  60.6 11.2 %collective-permute-start.13 = (bf16[256,512]{1,0:T(8,128)(2,1)S(1)}, bf16[256,512]{1,0:T(8,128)(2,1)S(1)}, u32[]{:S(2)}, u32[]{:S(2)}) collective-permute-start(bf16[256,512]{1,0:T(8,128)(2,1)S(1)} %get-tuple-element.37), channel_id=1, source_target_pairs={{0,7},{1,0},{2,1},{3,2},{4,3},{5,4},{6,5},{7,6},{8,15},{9,8},{10,9... | collective-permute-start | bytes 786440 | tf_op jit(solution)/shard_map/ppermute | solution.py:167
  63.4 4.7 %copy-start.6 = (f32[2,512]{1,0:T(2,128)S(1)}, f32[2,512]{1,0:T(2,128)}, u32[]{:S(2)}) copy-start(f32[2,512]{1,0:T(2,128)} %param.19) | copy-start | bytes 12292
  64.1 19.0 %copy-start.1 = (bf16[2,512,2048]{2,1,0:T(8,128)(2,1)S(1)}, bf16[2,512,2048]{2,1,0:T(8,128)(2,1)}, u32[]{:S(2)}) copy-start(bf16[2,512,2048]{2,1,0:T(8,128)(2,1)} %w_in_ref.3) | copy-start | bytes 12582916
  64.1 18.9 %copy-start.3 = (bf16[256,512]{1,0:T(8,128)(2,1)S(1)}, bf16[256,512]{1,0:T(8,128)(2,1)}, u32[]{:S(2)}) copy-start(bf16[256,512]{1,0:T(8,128)(2,1)} %refs_0_.1) | copy-start | bytes 786436
  64.1 16.2 %collective-permute-start.16 = (bf16[256,512]{1,0:T(8,128)(2,1)S(1)}, bf16[256,512]{1,0:T(8,128)(2,1)S(1)}, u32[]{:S(2)}, u32[]{:S(2)}) collective-permute-start(bf16[256,512]{1,0:T(8,128)(2,1)S(1)} %pad_maximum_fusion.1), channel_id=1, source_target_pairs={{0,2},{1,3},{2,4},{3,5},{4,6},{5,7},{6,0},{7,1},{8,10},{9,11},{10,... | collective-permute-start | bytes 786440 | tf_op jit(solution)/shard_map/ppermute | solution.py:167
  66.4 16.7 %collective-permute-start.19 = (bf16[256,512]{1,0:T(8,128)(2,1)S(1)}, bf16[256,512]{1,0:T(8,128)(2,1)S(1)}, u32[]{:S(2)}, u32[]{:S(2)}) collective-permute-start(bf16[256,512]{1,0:T(8,128)(2,1)S(1)} %pad_maximum_fusion.2), channel_id=1, source_target_pairs={{0,6},{1,7},{2,0},{3,1},{4,2},{5,3},{6,4},{7,5},{8,14},{9,15},{10,... | collective-permute-start | bytes 786440 | tf_op jit(solution)/shard_map/ppermute | solution.py:167
  85.0 7.3 %collective-permute-start.22 = (bf16[256,512]{1,0:T(8,128)(2,1)S(1)}, bf16[256,512]{1,0:T(8,128)(2,1)S(1)}, u32[]{:S(2)}, u32[]{:S(2)}) collective-permute-start(bf16[256,512]{1,0:T(8,128)(2,1)S(1)} %node_mlp.2.refs_0_), channel_id=1, source_target_pairs={{192,0},{56,8},{208,16},{8,24},{224,32},{24,40},{240,48},{40,56},{... | collective-permute-start | bytes 786440 | tf_op jit(solution)/shard_map/ppermute | solution.py:144
  85.8 8.7 %collective-permute-start.21 = (bf16[256,512]{1,0:T(8,128)(2,1)S(1)}, bf16[256,512]{1,0:T(8,128)(2,1)S(1)}, u32[]{:S(2)}, u32[]{:S(2)}) collective-permute-start(bf16[256,512]{1,0:T(8,128)(2,1)S(1)} %node_mlp.2.refs_0_), channel_id=1, source_target_pairs={{64,0},{24,8},{80,16},{40,24},{96,32},{56,40},{112,48},{8,56},{128... | collective-permute-start | bytes 786440 | tf_op jit(solution)/shard_map/ppermute | solution.py:144
  88.4 8.0 %collective-permute-start.20 = (bf16[256,512]{1,0:T(8,128)(2,1)S(1)}, bf16[256,512]{1,0:T(8,128)(2,1)S(1)}, u32[]{:S(2)}, u32[]{:S(2)}) collective-permute-start(bf16[256,512]{1,0:T(8,128)(2,1)S(1)} %node_mlp.2.refs_0_), channel_id=1, source_target_pairs={{128,0},{40,8},{144,16},{56,24},{160,32},{8,40},{176,48},{24,56},{... | collective-permute-start | bytes 786440 | tf_op jit(solution)/shard_map/ppermute | solution.py:144
  96.4 15.2 %collective-permute-start.24 = (bf16[1024,512]{1,0:T(8,128)(2,1)S(1)}, bf16[1024,512]{1,0:T(8,128)(2,1)S(1)}, u32[]{:S(2)}, u32[]{:S(2)}) collective-permute-start(bf16[1024,512]{1,0:T(8,128)(2,1)S(1)} %pad_maximum_fusion.refs_0_), channel_id=1, source_target_pairs={{48,0},{200,8},{0,16},{216,24},{16,32},{232,40},{32,48},{248,56},{... | collective-permute-start | bytes 3145736 | tf_op jit(solution)/shard_map/ppermute | solution.py:144
  96.8 15.0 %collective-permute-start.23 = (bf16[1024,512]{1,0:T(8,128)(2,1)S(1)}, bf16[1024,512]{1,0:T(8,128)(2,1)S(1)}, u32[]{:S(2)}, u32[]{:S(2)}) collective-permute-start(bf16[1024,512]{1,0:T(8,128)(2,1)S(1)} %pad_maximum_fusion.refs_0_), channel_id=1, source_target_pairs={{16,0},{72,8},{32,16},{88,24},{48,32},{104,40},{0,48},{120,56},{80... | collective-permute-start | bytes 3145736 | tf_op jit(solution)/shard_map/ppermute | solution.py:144
  99.2 24.8 %collective-permute-start.27 = (bf16[1024,512]{1,0:T(8,128)(2,1)S(1)}, bf16[1024,512]{1,0:T(8,128)(2,1)S(1)}, u32[]{:S(2)}, u32[]{:S(2)}) collective-permute-start(bf16[1024,512]{1,0:T(8,128)(2,1)S(1)} %pad_maximum_fusion.refs_0_), channel_id=1, source_target_pairs={{0,8},{8,0},{16,24},{24,16},{32,40},{40,32},{48,56},{56,48},{64,72... | collective-permute-start | bytes 3145736 | tf_op jit(solution)/shard_map/ppermute | solution.py:149
  111.7 9.6 %collective-permute-start.26 = (bf16[512,512]{1,0:T(8,128)(2,1)S(1)}, bf16[512,512]{1,0:T(8,128)(2,1)S(1)}, u32[]{:S(2)}, u32[]{:S(2)}) collective-permute-start(bf16[512,512]{1,0:T(8,128)(2,1)S(1)} %slice.73), channel_id=1, source_target_pairs={{48,0},{200,8},{0,16},{216,24},{16,32},{232,40},{32,48},{248,56},{... | collective-permute-start | bytes 1572872 | tf_op jit(solution)/shard_map/ppermute | solution.py:144
  111.8 12.1 %collective-permute-start.25 = (bf16[512,512]{1,0:T(8,128)(2,1)S(1)}, bf16[512,512]{1,0:T(8,128)(2,1)S(1)}, u32[]{:S(2)}, u32[]{:S(2)}) collective-permute-start(bf16[512,512]{1,0:T(8,128)(2,1)S(1)} %slice.72), channel_id=1, source_target_pairs={{16,0},{72,8},{32,16},{88,24},{48,32},{104,40},{0,48},{120,56},{80... | collective-permute-start | bytes 1572872 | tf_op jit(solution)/shard_map/ppermute | solution.py:144
  114.6 11.6 %collective-permute-start.29 = (bf16[1024,512]{1,0:T(8,128)(2,1)S(1)}, bf16[1024,512]{1,0:T(8,128)(2,1)S(1)}, u32[]{:S(2)}, u32[]{:S(2)}) collective-permute-start(bf16[1024,512]{1,0:T(8,128)(2,1)S(1)} %collective-permute-done.24.refs_2_), channel_id=1, source_target_pairs={{0,8},{8,0},{16,24},{24,16},{32,40},{40,32},{48,56},{56,48},{64,72... | collective-permute-start | bytes 3145736 | tf_op jit(solution)/shard_map/ppermute | solution.py:149
  116.9 9.3 %collective-permute-start.28 = (bf16[1024,512]{1,0:T(8,128)(2,1)S(1)}, bf16[1024,512]{1,0:T(8,128)(2,1)S(1)}, u32[]{:S(2)}, u32[]{:S(2)}) collective-permute-start(bf16[1024,512]{1,0:T(8,128)(2,1)S(1)} %collective-permute-done.23.refs_1_), channel_id=1, source_target_pairs={{0,8},{8,0},{16,24},{24,16},{32,40},{40,32},{48,56},{56,48},{64,72... | collective-permute-start | bytes 3145736 | tf_op jit(solution)/shard_map/ppermute | solution.py:149
  121.3 4.2 %collective-permute-start.31 = (bf16[512,512]{1,0:T(8,128)(2,1)S(1)}, bf16[512,512]{1,0:T(8,128)(2,1)S(1)}, u32[]{:S(2)}, u32[]{:S(2)}) collective-permute-start(bf16[512,512]{1,0:T(8,128)(2,1)S(1)} %collective-permute-done.26.refs_4_), channel_id=1, source_target_pairs={{0,8},{8,0},{16,24},{24,16},{32,40},{40,32},{48,56},{56,48},{64,72... | collective-permute-start | bytes 1572872 | tf_op jit(solution)/shard_map/ppermute | solution.py:149
  123.9 2.3 %collective-permute-start.30 = (bf16[512,512]{1,0:T(8,128)(2,1)S(1)}, bf16[512,512]{1,0:T(8,128)(2,1)S(1)}, u32[]{:S(2)}, u32[]{:S(2)}) collective-permute-start(bf16[512,512]{1,0:T(8,128)(2,1)S(1)} %collective-permute-done.25.refs_3_), channel_id=1, source_target_pairs={{0,8},{8,0},{16,24},{24,16},{32,40},{40,32},{48,56},{56,48},{64,72... | collective-permute-start | bytes 1572872 | tf_op jit(solution)/shard_map/ppermute | solution.py:149
  127.7 8.8 %collective-permute-start.34 = (bf16[256,512]{1,0:T(8,128)(2,1)S(1)}, bf16[256,512]{1,0:T(8,128)(2,1)S(1)}, u32[]{:S(2)}, u32[]{:S(2)}) collective-permute-start(bf16[256,512]{1,0:T(8,128)(2,1)S(1)} %get-tuple-element.47), channel_id=1, source_target_pairs={{0,1},{1,2},{2,3},{3,4},{4,5},{5,6},{6,7},{7,0},{8,9},{9,10},{10,1... | collective-permute-start | bytes 786440 | tf_op jit(solution)/shard_map/ppermute | solution.py:167
  128.9 14.3 %collective-permute-start.38 = (bf16[128,512]{1,0:T(8,128)(2,1)S(1)}, bf16[128,512]{1,0:T(8,128)(2,1)S(1)}, u32[]{:S(2)}, u32[]{:S(2)}) collective-permute-start(bf16[128,512]{1,0:T(8,128)(2,1)S(1)} %get-tuple-element.51), channel_id=1, source_target_pairs={{0,6},{1,7},{2,0},{3,1},{4,2},{5,3},{6,4},{7,5},{8,14},{9,15},{10,... | collective-permute-start | bytes 393224 | tf_op jit(solution)/shard_map/ppermute | solution.py:167
  132.2 9.1 %collective-permute-start.35 = (bf16[128,512]{1,0:T(8,128)(2,1)S(1)}, bf16[128,512]{1,0:T(8,128)(2,1)S(1)}, u32[]{:S(2)}, u32[]{:S(2)}) collective-permute-start(bf16[128,512]{1,0:T(8,128)(2,1)S(1)} %get-tuple-element.52), channel_id=1, source_target_pairs={{0,2},{1,3},{2,4},{3,5},{4,6},{5,7},{6,0},{7,1},{8,10},{9,11},{10,... | collective-permute-start | bytes 393224 | tf_op jit(solution)/shard_map/ppermute | solution.py:167
  133.1 10.0 %collective-permute-start.37 = (bf16[256,512]{1,0:T(8,128)(2,1)S(1)}, bf16[256,512]{1,0:T(8,128)(2,1)S(1)}, u32[]{:S(2)}, u32[]{:S(2)}) collective-permute-start(bf16[256,512]{1,0:T(8,128)(2,1)S(1)} %get-tuple-element.50), channel_id=1, source_target_pairs={{0,7},{1,0},{2,1},{3,2},{4,3},{5,4},{6,5},{7,6},{8,15},{9,8},{10,9... | collective-permute-start | bytes 786440 | tf_op jit(solution)/shard_map/ppermute | solution.py:167
  135.9 11.8 %collective-permute-start.32 = (bf16[256,512]{1,0:T(8,128)(2,1)S(1)}, bf16[256,512]{1,0:T(8,128)(2,1)S(1)}, u32[]{:S(2)}, u32[]{:S(2)}) collective-permute-start(bf16[256,512]{1,0:T(8,128)(2,1)S(1)} %get-tuple-element.44), channel_id=1, source_target_pairs={{0,1},{1,2},{2,3},{3,4},{4,5},{5,6},{6,7},{7,0},{8,9},{9,10},{10,1... | collective-permute-start | bytes 786440 | tf_op jit(solution)/shard_map/ppermute | solution.py:167
  136.5 12.2 %collective-permute-start.33 = (bf16[256,512]{1,0:T(8,128)(2,1)S(1)}, bf16[256,512]{1,0:T(8,128)(2,1)S(1)}, u32[]{:S(2)}, u32[]{:S(2)}) collective-permute-start(bf16[256,512]{1,0:T(8,128)(2,1)S(1)} %get-tuple-element.45), channel_id=1, source_target_pairs={{0,7},{1,0},{2,1},{3,2},{4,3},{5,4},{6,5},{7,6},{8,15},{9,8},{10,9... | collective-permute-start | bytes 786440 | tf_op jit(solution)/shard_map/ppermute | solution.py:167
  141.4 15.1 %collective-permute-start.36 = (bf16[256,512]{1,0:T(8,128)(2,1)S(1)}, bf16[256,512]{1,0:T(8,128)(2,1)S(1)}, u32[]{:S(2)}, u32[]{:S(2)}) collective-permute-start(bf16[256,512]{1,0:T(8,128)(2,1)S(1)} %pad_maximum_fusion.3), channel_id=1, source_target_pairs={{0,2},{1,3},{2,4},{3,5},{4,6},{5,7},{6,0},{7,1},{8,10},{9,11},{10,... | collective-permute-start | bytes 786440 | tf_op jit(solution)/shard_map/ppermute | solution.py:167
  143.3 18.4 %collective-permute-start.39 = (bf16[256,512]{1,0:T(8,128)(2,1)S(1)}, bf16[256,512]{1,0:T(8,128)(2,1)S(1)}, u32[]{:S(2)}, u32[]{:S(2)}) collective-permute-start(bf16[256,512]{1,0:T(8,128)(2,1)S(1)} %pad_maximum_fusion.4), channel_id=1, source_target_pairs={{0,6},{1,7},{2,0},{3,1},{4,2},{5,3},{6,4},{7,5},{8,14},{9,15},{10,... | collective-permute-start | bytes 786440 | tf_op jit(solution)/shard_map/ppermute | solution.py:167

commit v6 on v5

--- a/solution.py
+++ b/solution.py
@@ -20,9 +20,14 @@
 
 
 def aggregate_tiles(matrix, sources, here, wanted, slot_index, further):
+    return multiply_tiles(matrix, sources, here, wanted, slot_index, further, True)
+
+
+def multiply_tiles(matrix, sources, here, wanted, slot_index, further, gather):
     row_tiles, tile, depth = matrix.shape
     slots = depth // tile
     width = sources[0].shape[-1]
+    n_out = len(further)
     count = lax.axis_size("col")
     per_block = row_tiles // count
     n_src = len(sources)
@@ -30,10 +35,10 @@
 
     def body(here_ref, wanted_ref, index_ref, matrix_ref, *refs):
         src = refs[:n_src]
-        outs = refs[n_src:-1]
-        tiles = refs[-1]
+        outs = refs[n_src : n_src + n_out]
+        tiles = refs[-1] if gather else src[0]
         x, y, core, col = (here_ref[i] for i in range(4))
-        for array, block, first, second, swapped in BLOCKS:
+        for array, block, first, second, swapped in BLOCKS if gather else ():
             held = core ^ swapped
             step_x = jnp.where(held == 0, first, second)
             step_y = jnp.where(held == 0, second, first)
@@ -54,9 +59,9 @@
     return pl.pallas_call(
         body,
         in_specs=[smem] * 3 + [vmem] * (1 + n_src),
-        out_specs=[vmem] * len(further),
-        out_shape=[jax.ShapeDtypeStruct((rows, width), jnp.bfloat16)] * len(further),
-        scratch_shapes=[pltpu.VMEM((len(BLOCKS), tile, width), jnp.bfloat16)],
+        out_specs=[vmem] * (n_out + gather),
+        out_shape=[jax.ShapeDtypeStruct((rows, width), jnp.bfloat16)] * n_out
+        + [jax.ShapeDtypeStruct((len(BLOCKS), tile, width), jnp.bfloat16)] * gather,
         compiler_params=pltpu.CompilerParams(vmem_limit_bytes=VMEM_LIMIT),
         name="aggregate_tiles",
     )(here, wanted, slot_index, matrix, *sources)
@@ -219,9 +224,10 @@
             matrix, wanted, slot_index, here = ready
             ready = None
         near = {}
-        for group in SENT:
-            products = aggregate_tiles(matrix, arrays, here, wanted, slot_index, group)
-            near.update(zip(group, products, strict=True))
+        *products, tiles = aggregate_tiles(matrix, arrays, here, wanted, slot_index, SENT[0])
+        near.update(zip(SENT[0], products, strict=True))
+        products = multiply_tiles(matrix, [tiles], here, wanted, slot_index, SENT[1], False)
+        near.update(zip(SENT[1], products, strict=True))
         parts = [sum_columns(near, near[0])]
         last = layer == LAYERS - 1
         states = node_mlp(

time: 165 us -> 172 us (1.042)
  waiting for transfers between devices: 81 us -> 87.5 us
  Pallas kernels: 13.9 us -> 11.7 us
    ppermute x16, waiting for transfers between devices: 35.5 us -> 43.6 us  [send(): lax.ppermute(value, 'col', [(i, (i + distance) % count) for i in range(co...]
    ppermute x10, starting transfers between devices: 11.5 us -> 14 us  [swap(): return lax.ppermute(value, 'row', [(i, i ^ 1) for i in range(count)])]
    pallas_call x4, Pallas kernels: 9.27 us -> 7.07 us  [multiply_tiles(): pl.pallas_call(body, in_specs=[smem] * 3 + [vmem] * (1 + n_src), out_spec...]
  transfers between devices with their start and end apart: 40 -> 40, of which waited for: 26 -> 23; matrix products, arithmetic and copies ran while one was open for 5% -> 4% of each run, Pallas kernels for 3% -> 2%
where the time goes in v6:
time: 172 us; the launch traced here: 170 us
  waiting for transfers between devices  87.5 us (51%)
  starting transfers between devices  60.9 us (35%)
  Pallas kernels  11.7 us (7%)
  local copies, waits for them, and re-layouts  8.12 us (5%)
    ppermute x16, waiting for transfers between devices, send(): lax.ppermute(value, 'col', [(i, (i + distance) % count) for i in range(co...  43.6 us
    ppermute x14, waiting for transfers between devices, pull(): return lax.ppermute(value, 'row', pairs)  39.8 us
    ppermute x16, starting transfers between devices, send(): lax.ppermute(value, 'col', [(i, (i + distance) % count) for i in range(co...  26.1 us
    ppermute x14, starting transfers between devices, pull(): return lax.ppermute(value, 'row', pairs)  20.8 us
    ppermute x10, starting transfers between devices, swap(): return lax.ppermute(value, 'row', [(i, i ^ 1) for i in range(count)])  14 us
    pallas_call x4, Pallas kernels, multiply_tiles(): pl.pallas_call(body, in_specs=[smem] * 3 + [vmem] * (1 + n_src), out_spec...  7.07 us
    pallas_call x2, Pallas kernels, node_mlp(): pl.pallas_call(body, in_specs=[vmem] * (4 + len(flat)), out_specs=[vmem]...  4.61 us
    ppermute x10, waiting for transfers between devices, swap(): return lax.ppermute(value, 'row', [(i, i ^ 1) for i in range(count)])  4.05 us
  transfers between devices with their start and end apart: 40, of which 23 were waited for; matrix products, arithmetic and copies ran while one was open for 4% of the time, Pallas kernels for 2%

profile of v6, /device:TPU:1, one launch (start us, length us, event | category | flops | bytes accessed | tf_op | source)
XLA Modules:
  0.0 169.8 jit_solution(4456469626399354550)
XLA Ops:
  0.0 3.7 %collective-permute-start = (bf16[256,512]{1,0:T(8,128)(2,1)}, bf16[256,512]{1,0:T(8,128)(2,1)S(1)}, u32[]{:S(2)}, u32[]{:S(2)}) collective-permute-start(bf16[256,512]{1,0:T(8,128)(2,1)} %refs_0_.1), channel_id=1, source_target_pairs={{128,0},{40,8},{144,16},{56,24},{160,32},{8,40},{176,48},{24,56},{... | collective-permute-start | bytes 786440 | tf_op jit(solution)/shard_map/ppermute | solution.py:149
  3.7 0.8 collective-permute-start.1
  4.5 0.7 collective-permute-start.2
  5.2 1.7 %constant_dynamic-update-slice_fusion.3 = bf16[1024,512]{1,0:T(8,128)(2,1)} fusion(bf16[256,512]{1,0:T(8,128)(2,1)} %refs_0_.1), kind=kLoop, calls=%fused_computation.31 | loop fusion | bytes 524288
  6.9 0.8 collective-permute-done
  7.7 0.7 constant_dynamic-update-slice_fusion.2
  8.4 2.8 %collective-permute-done.1 = bf16[256,512]{1,0:T(8,128)(2,1)S(1)} collective-permute-done((bf16[256,512]{1,0:T(8,128)(2,1)}, bf16[256,512]{1,0:T(8,128)(2,1)S(1)}, u32[]{:S(2)}, u32[]{:S(2)}) %collective-permute-start.1) | collective-permute-done | bytes 262176 | tf_op jit(solution)/shard_map/ppermute | solution.py:149
  11.3 0.7 constant_dynamic-update-slice_fusion.1
  12.0 0.7 constant_dynamic-update-slice_fusion.refs_0_
  12.7 2.2 %collective-permute-start.5 = (bf16[1024,512]{1,0:T(8,128)(2,1)}, bf16[1024,512]{1,0:T(8,128)(2,1)}, u32[]{:S(2)}, u32[]{:S(2)}) collective-permute-start(bf16[1024,512]{1,0:T(8,128)(2,1)} %constant_dynamic-update-slice_fusion.refs_0_), channel_id=1, source_target_pairs={{0,8},{8,0},{16,24},{24,16},{32,40},{40,32},{48,56},{56,48},{64,72... | collective-permute-start | bytes 3145736 | tf_op jit(solution)/shard_map/ppermute | solution.py:154
  15.0 2.5 %collective-permute-start.3 = (bf16[1024,512]{1,0:T(8,128)(2,1)}, bf16[1024,512]{1,0:T(8,128)(2,1)}, u32[]{:S(2)}, u32[]{:S(2)}) collective-permute-start(bf16[1024,512]{1,0:T(8,128)(2,1)} %constant_dynamic-update-slice_fusion.refs_0_), channel_id=1, source_target_pairs={{16,0},{72,8},{32,16},{88,24},{48,32},{104,40},{0,48},{120,56},{80... | collective-permute-start | bytes 3145736 | tf_op jit(solution)/shard_map/ppermute | solution.py:149
  17.7 2.8 %reshape.13.matrix_ref = bf16[16,128,512]{2,1,0:T(8,128)(2,1)S(1)} reshape(bf16[16,1,128,4,128]{4,3,2,1,0:T(4,128)(2,1)} %param.12) | data formatting | bytes 4194304 | tf_op jit(solution)/shard_map/reshape | solution.py:211
  20.6 9.6 %collective-permute-done.4.refs_2_ = bf16[1024,512]{1,0:T(8,128)(2,1)S(1)} collective-permute-done((bf16[1024,512]{1,0:T(8,128)(2,1)}, bf16[1024,512]{1,0:T(8,128)(2,1)S(1)}, u32[]{:S(2)}, u32[]{:S(2)}) %collective-permute-start.4) | collective-permute-done | bytes 1048608 | tf_op jit(solution)/shard_map/ppermute | solution.py:149
  30.2 1.1 slice.52
  31.3 0.9 collective-permute-start.8
  32.3 0.7 collective-permute-start.7
  33.0 0.7 collective-permute-start.9
  33.8 2.1 %collective-permute-start.6 = (bf16[512,512]{1,0:T(8,128)(2,1)S(1)}, bf16[512,512]{1,0:T(8,128)(2,1)S(1)}, u32[]{:S(2)}, u32[]{:S(2)}) collective-permute-start(bf16[512,512]{1,0:T(8,128)(2,1)S(1)} %slice.52), channel_id=1, source_target_pairs={{16,0},{72,8},{32,16},{88,24},{48,32},{104,40},{0,48},{120,56},{80... | collective-permute-start | bytes 1572872 | tf_op jit(solution)/shard_map/ppermute | solution.py:149
  35.9 6.0 %collective-permute-done.7.refs_4_ = bf16[512,512]{1,0:T(8,128)(2,1)S(1)} collective-permute-done((bf16[512,512]{1,0:T(8,128)(2,1)S(1)}, bf16[512,512]{1,0:T(8,128)(2,1)S(1)}, u32[]{:S(2)}, u32[]{:S(2)}) %collective-permute-start.7) | collective-permute-done | bytes 524320 | tf_op jit(solution)/shard_map/ppermute | solution.py:149
  41.9 1.0 collective-permute-start.11
  43.4 1.0 collective-permute-done.11.refs_9_
  44.4 0.7 collective-permute-done.10.refs_8_
  45.2 2.8 %aggregate_tiles.4 = (bf16[256,512]{1,0:T(8,128)(2,1)S(1)}, bf16[256,512]{1,0:T(8,128)(2,1)S(1)}, bf16[256,512]{1,0:T(8,128)(2,1)S(1)}, bf16[32,128,512]{2,1,0:T(8,128)(2,1)S(1)}) custom-call(s32[4]{0:T(128)S(1)} %pad_add_fusion.here_ref, s32[32]{0:T(128)S(1)} %bitcast.9, s32[64]{0:T(128)S(1)} %reshape.15.index_ref, ...), custom_call_target="tpu_custom_call" | custom-call | tf_op jit(solution)/shard_map/aggregate_tiles/pallas_call | solution.py:59
  48.0 1.4 collective-permute-start.14
  49.6 1.4 aggregate_tiles.5
  51.1 5.2 %collective-permute-start.18 = (bf16[128,512]{1,0:T(8,128)(2,1)S(1)}, bf16[128,512]{1,0:T(8,128)(2,1)S(1)}, u32[]{:S(2)}, u32[]{:S(2)}) collective-permute-start(bf16[128,512]{1,0:T(8,128)(2,1)S(1)} %get-tuple-element.57), channel_id=1, source_target_pairs={{0,6},{1,7},{2,0},{3,1},{4,2},{5,3},{6,4},{7,5},{8,14},{9,15},{10,... | collective-permute-start | bytes 393224 | tf_op jit(solution)/shard_map/ppermute | solution.py:172
  56.3 1.0 collective-permute-start.12
  57.3 1.7 collective-permute-start.13
  59.0 0.7 collective-permute-done.14
  59.7 1.1 collective-permute-start.17
  60.9 3.2 %collective-permute-done.15 = bf16[128,512]{1,0:T(8,128)(2,1)S(1)} collective-permute-done((bf16[128,512]{1,0:T(8,128)(2,1)S(1)}, bf16[128,512]{1,0:T(8,128)(2,1)S(1)}, u32[]{:S(2)}, u32[]{:S(2)}) %collective-permute-start.15) | collective-permute-done | bytes 131104 | tf_op jit(solution)/shard_map/ppermute | solution.py:172
  64.3 9.0 %collective-permute-done.17 = bf16[256,512]{1,0:T(8,128)(2,1)S(1)} collective-permute-done((bf16[256,512]{1,0:T(8,128)(2,1)S(1)}, bf16[256,512]{1,0:T(8,128)(2,1)S(1)}, u32[]{:S(2)}, u32[]{:S(2)}) %collective-permute-start.17) | collective-permute-done | bytes 262176 | tf_op jit(solution)/shard_map/ppermute | solution.py:172
  73.4 1.7 %collective-permute-start.19 = (bf16[256,512]{1,0:T(8,128)(2,1)S(1)}, bf16[256,512]{1,0:T(8,128)(2,1)S(1)}, u32[]{:S(2)}, u32[]{:S(2)}) collective-permute-start(bf16[256,512]{1,0:T(8,128)(2,1)S(1)} %pad_maximum_fusion.2), channel_id=1, source_target_pairs={{0,6},{1,7},{2,0},{3,1},{4,2},{5,3},{6,4},{7,5},{8,14},{9,15},{10,... | collective-permute-start | bytes 786440 | tf_op jit(solution)/shard_map/ppermute | solution.py:172
  75.3 3.2 %collective-permute-done.16.refs_4_ = bf16[256,512]{1,0:T(8,128)(2,1)S(1)} collective-permute-done((bf16[256,512]{1,0:T(8,128)(2,1)S(1)}, bf16[256,512]{1,0:T(8,128)(2,1)S(1)}, u32[]{:S(2)}, u32[]{:S(2)}) %collective-permute-start.16) | collective-permute-done | bytes 262176 | tf_op jit(solution)/shard_map/ppermute | solution.py:172
  78.5 5.0 %collective-permute-done.19.refs_5_ = bf16[256,512]{1,0:T(8,128)(2,1)S(1)} collective-permute-done((bf16[256,512]{1,0:T(8,128)(2,1)S(1)}, bf16[256,512]{1,0:T(8,128)(2,1)S(1)}, u32[]{:S(2)}, u32[]{:S(2)}) %collective-permute-start.19) | collective-permute-done | bytes 262176 | tf_op jit(solution)/shard_map/ppermute | solution.py:172
  83.5 1.9 %node_mlp.2.refs_0_ = bf16[256,512]{1,0:T(8,128)(2,1)S(1)} custom-call(f32[2,256,512]{2,1,0:T(8,128)S(1)} %broadcast_multiply_fusion.scale_ref, bf16[256,512]{1,0:T(8,128)(2,1)S(1)} %convolution_convert_fusion.shift_ref, bf16[2,512,2048]{2,1,0:T(8,128)(2,1)S(1)} %copy-done.1, bf16[2,2048,512]{2,1,0:T(8,128)(2,1)S(1)} %copy-done.2, ...), custom_call_target="tpu_custom_call" | custom-call | tf_op jit(solution)/shard_map/node_mlp/pallas_call | solution.py:107
  85.5 0.7 collective-permute-start.22
  86.2 2.7 %collective-permute-start.21 = (bf16[256,512]{1,0:T(8,128)(2,1)S(1)}, bf16[256,512]{1,0:T(8,128)(2,1)S(1)}, u32[]{:S(2)}, u32[]{:S(2)}) collective-permute-start(bf16[256,512]{1,0:T(8,128)(2,1)S(1)} %node_mlp.2.refs_0_), channel_id=1, source_target_pairs={{64,0},{24,8},{80,16},{40,24},{96,32},{56,40},{112,48},{8,56},{128... | collective-permute-start | bytes 786440 | tf_op jit(solution)/shard_map/ppermute | solution.py:149
  88.9 1.1 collective-permute-start.20
  90.0 2.9 %collective-permute-done.22 = bf16[256,512]{1,0:T(8,128)(2,1)S(1)} collective-permute-done((bf16[256,512]{1,0:T(8,128)(2,1)S(1)}, bf16[256,512]{1,0:T(8,128)(2,1)S(1)}, u32[]{:S(2)}, u32[]{:S(2)}) %collective-permute-start.22) | collective-permute-done | bytes 262176 | tf_op jit(solution)/shard_map/ppermute | solution.py:149
  92.9 2.2 %collective-permute-done.21 = bf16[256,512]{1,0:T(8,128)(2,1)S(1)} collective-permute-done((bf16[256,512]{1,0:T(8,128)(2,1)S(1)}, bf16[256,512]{1,0:T(8,128)(2,1)S(1)}, u32[]{:S(2)}, u32[]{:S(2)}) %collective-permute-start.21) | collective-permute-done | bytes 262176 | tf_op jit(solution)/shard_map/ppermute | solution.py:149
  95.0 1.8 %collective-permute-done.20 = bf16[256,512]{1,0:T(8,128)(2,1)S(1)} collective-permute-done((bf16[256,512]{1,0:T(8,128)(2,1)S(1)}, bf16[256,512]{1,0:T(8,128)(2,1)S(1)}, u32[]{:S(2)}, u32[]{:S(2)}) %collective-permute-start.20) | collective-permute-done | bytes 262176 | tf_op jit(solution)/shard_map/ppermute | solution.py:149
  97.1 2.5 %collective-permute-start.23 = (bf16[1024,512]{1,0:T(8,128)(2,1)S(1)}, bf16[1024,512]{1,0:T(8,128)(2,1)S(1)}, u32[]{:S(2)}, u32[]{:S(2)}) collective-permute-start(bf16[1024,512]{1,0:T(8,128)(2,1)S(1)} %pad_maximum_fusion.refs_0_), channel_id=1, source_target_pairs={{16,0},{72,8},{32,16},{88,24},{48,32},{104,40},{0,48},{120,56},{80... | collective-permute-start | bytes 3145736 | tf_op jit(solution)/shard_map/ppermute | solution.py:149
  99.7 2.4 %collective-permute-start.27 = (bf16[1024,512]{1,0:T(8,128)(2,1)S(1)}, bf16[1024,512]{1,0:T(8,128)(2,1)S(1)}, u32[]{:S(2)}, u32[]{:S(2)}) collective-permute-start(bf16[1024,512]{1,0:T(8,128)(2,1)S(1)} %pad_maximum_fusion.refs_0_), channel_id=1, source_target_pairs={{0,8},{8,0},{16,24},{24,16},{32,40},{40,32},{48,56},{56,48},{64,72... | collective-permute-start | bytes 3145736 | tf_op jit(solution)/shard_map/ppermute | solution.py:154
  102.0 10.1 %collective-permute-done.24.refs_2_ = bf16[1024,512]{1,0:T(8,128)(2,1)S(1)} collective-permute-done((bf16[1024,512]{1,0:T(8,128)(2,1)S(1)}, bf16[1024,512]{1,0:T(8,128)(2,1)S(1)}, u32[]{:S(2)}, u32[]{:S(2)}) %collective-permute-start.24) | collective-permute-done | bytes 1048608 | tf_op jit(solution)/shard_map/ppermute | solution.py:149
  112.3 2.7 %collective-permute-start.25 = (bf16[512,512]{1,0:T(8,128)(2,1)S(1)}, bf16[512,512]{1,0:T(8,128)(2,1)S(1)}, u32[]{:S(2)}, u32[]{:S(2)}) collective-permute-start(bf16[512,512]{1,0:T(8,128)(2,1)S(1)} %slice.72), channel_id=1, source_target_pairs={{16,0},{72,8},{32,16},{88,24},{48,32},{104,40},{0,48},{120,56},{80... | collective-permute-start | bytes 1572872 | tf_op jit(solution)/shard_map/ppermute | solution.py:149
  115.1 3.1 %collective-permute-start.29 = (bf16[1024,512]{1,0:T(8,128)(2,1)S(1)}, bf16[1024,512]{1,0:T(8,128)(2,1)S(1)}, u32[]{:S(2)}, u32[]{:S(2)}) collective-permute-start(bf16[1024,512]{1,0:T(8,128)(2,1)S(1)} %collective-permute-done.24.refs_2_), channel_id=1, source_target_pairs={{0,8},{8,0},{16,24},{24,16},{32,40},{40,32},{48,56},{56,48},{64,72... | collective-permute-start | bytes 3145736 | tf_op jit(solution)/shard_map/ppermute | solution.py:154
  118.2 3.6 %collective-permute-done.26.refs_4_ = bf16[512,512]{1,0:T(8,128)(2,1)S(1)} collective-permute-done((bf16[512,512]{1,0:T(8,128)(2,1)S(1)}, bf16[512,512]{1,0:T(8,128)(2,1)S(1)}, u32[]{:S(2)}, u32[]{:S(2)}) %collective-permute-start.26) | collective-permute-done | bytes 524320 | tf_op jit(solution)/shard_map/ppermute | solution.py:149
  121.8 3.4 %collective-permute-start.31 = (bf16[512,512]{1,0:T(8,128)(2,1)S(1)}, bf16[512,512]{1,0:T(8,128)(2,1)S(1)}, u32[]{:S(2)}, u32[]{:S(2)}) collective-permute-start(bf16[512,512]{1,0:T(8,128)(2,1)S(1)} %collective-permute-done.26.refs_4_), channel_id=1, source_target_pairs={{0,8},{8,0},{16,24},{24,16},{32,40},{40,32},{48,56},{56,48},{64,72... | collective-permute-start | bytes 1572872 | tf_op jit(solution)/shard_map/ppermute | solution.py:154
  125.3 1.5 collective-permute-done.31.refs_9_
  126.8 0.7 collective-permute-done.30.refs_8_
  127.5 1.5 aggregate_tiles.6
  129.0 5.0 %collective-permute-start.34 = (bf16[256,512]{1,0:T(8,128)(2,1)S(1)}, bf16[256,512]{1,0:T(8,128)(2,1)S(1)}, u32[]{:S(2)}, u32[]{:S(2)}) collective-permute-start(bf16[256,512]{1,0:T(8,128)(2,1)S(1)} %get-tuple-element.51), channel_id=1, source_target_pairs={{0,1},{1,2},{2,3},{3,4},{4,5},{5,6},{6,7},{7,0},{8,9},{9,10},{10,1... | collective-permute-start | bytes 786440 | tf_op jit(solution)/shard_map/ppermute | solution.py:172
  134.0 1.4 aggregate_tiles.7
  135.5 2.7 %collective-permute-start.38 = (bf16[128,512]{1,0:T(8,128)(2,1)S(1)}, bf16[128,512]{1,0:T(8,128)(2,1)S(1)}, u32[]{:S(2)}, u32[]{:S(2)}) collective-permute-start(bf16[128,512]{1,0:T(8,128)(2,1)S(1)} %get-tuple-element.55), channel_id=1, source_target_pairs={{0,6},{1,7},{2,0},{3,1},{4,2},{5,3},{6,4},{7,5},{8,14},{9,15},{10,... | collective-permute-start | bytes 393224 | tf_op jit(solution)/shard_map/ppermute | solution.py:172
  138.2 2.7 %collective-permute-start.33 = (bf16[256,512]{1,0:T(8,128)(2,1)S(1)}, bf16[256,512]{1,0:T(8,128)(2,1)S(1)}, u32[]{:S(2)}, u32[]{:S(2)}) collective-permute-start(bf16[256,512]{1,0:T(8,128)(2,1)S(1)} %get-tuple-element.49), channel_id=1, source_target_pairs={{0,7},{1,0},{2,1},{3,2},{4,3},{5,4},{6,5},{7,6},{8,15},{9,8},{10,9... | collective-permute-start | bytes 786440 | tf_op jit(solution)/shard_map/ppermute | solution.py:172
  140.9 1.0 collective-permute-done.34
  141.9 1.6 collective-permute-start.37
  143.6 4.8 %collective-permute-done.35 = bf16[128,512]{1,0:T(8,128)(2,1)S(1)} collective-permute-done((bf16[128,512]{1,0:T(8,128)(2,1)S(1)}, bf16[128,512]{1,0:T(8,128)(2,1)S(1)}, u32[]{:S(2)}, u32[]{:S(2)}) %collective-permute-start.35) | collective-permute-done | bytes 131104 | tf_op jit(solution)/shard_map/ppermute | solution.py:172
  148.5 7.4 %collective-permute-done.37 = bf16[256,512]{1,0:T(8,128)(2,1)S(1)} collective-permute-done((bf16[256,512]{1,0:T(8,128)(2,1)S(1)}, bf16[256,512]{1,0:T(8,128)(2,1)S(1)}, u32[]{:S(2)}, u32[]{:S(2)}) %collective-permute-start.37) | collective-permute-done | bytes 262176 | tf_op jit(solution)/shard_map/ppermute | solution.py:172
  156.1 1.7 %collective-permute-start.39 = (bf16[256,512]{1,0:T(8,128)(2,1)S(1)}, bf16[256,512]{1,0:T(8,128)(2,1)S(1)}, u32[]{:S(2)}, u32[]{:S(2)}) collective-permute-start(bf16[256,512]{1,0:T(8,128)(2,1)S(1)} %pad_maximum_fusion.4), channel_id=1, source_target_pairs={{0,6},{1,7},{2,0},{3,1},{4,2},{5,3},{6,4},{7,5},{8,14},{9,15},{10,... | collective-permute-start | bytes 786440 | tf_op jit(solution)/shard_map/ppermute | solution.py:172
  157.8 7.4 %collective-permute-done.36.refs_4_ = bf16[256,512]{1,0:T(8,128)(2,1)S(1)} collective-permute-done((bf16[256,512]{1,0:T(8,128)(2,1)S(1)}, bf16[256,512]{1,0:T(8,128)(2,1)S(1)}, u32[]{:S(2)}, u32[]{:S(2)}) %collective-permute-start.36) | collective-permute-done | bytes 262176 | tf_op jit(solution)/shard_map/ppermute | solution.py:172
  165.2 1.9 %collective-permute-done.39.refs_5_ = bf16[256,512]{1,0:T(8,128)(2,1)S(1)} collective-permute-done((bf16[256,512]{1,0:T(8,128)(2,1)S(1)}, bf16[256,512]{1,0:T(8,128)(2,1)S(1)}, u32[]{:S(2)}, u32[]{:S(2)}) %collective-permute-start.39) | collective-permute-done | bytes 262176 | tf_op jit(solution)/shard_map/ppermute | solution.py:172
  167.2 2.7 %node_mlp.3 = bf16[256,512]{1,0:T(8,128)(2,1)} custom-call(f32[2,256,512]{2,1,0:T(8,128)S(1)} %broadcast_multiply_fusion.scale_ref, bf16[256,512]{1,0:T(8,128)(2,1)S(1)} %convolution_convert_fusion.shift_ref, bf16[2,512,2048]{2,1,0:T(8,128)(2,1)S(1)} %copy-done.1, bf16[2,2048,512]{2,1,0:T(8,128)(2,1)S(1)} %copy-done.2, ...), custom_call_target="tpu_custom_call" | custom-call | tf_op jit(solution)/shard_map/node_mlp/pallas_call | solution.py:107
  (76 shorter events, 2.7 us)
Async XLA Ops:
  0.0 49.4 %copy-start = (bf16[128,512]{1,0:T(8,128)(2,1)S(1)}, bf16[128,512]{1,0:T(8,128)(2,1)}, u32[]{:S(2)}) copy-start(bf16[128,512]{1,0:T(8,128)(2,1)} %param.17) | copy-start | bytes 393220
  0.0 17.5 %copy-start.7 = (s32[16,1,4]{0,2,1:T(4,128)S(1)}, s32[16,1,4]{0,2,1:T(4,128)}, u32[]{:S(2)}) copy-start(s32[16,1,4]{0,2,1:T(4,128)} %param.13) | copy-start | bytes 772
  0.0 7.7 %collective-permute-start = (bf16[256,512]{1,0:T(8,128)(2,1)}, bf16[256,512]{1,0:T(8,128)(2,1)S(1)}, u32[]{:S(2)}, u32[]{:S(2)}) collective-permute-start(bf16[256,512]{1,0:T(8,128)(2,1)} %refs_0_.1), channel_id=1, source_target_pairs={{128,0},{40,8},{144,16},{56,24},{160,32},{8,40},{176,48},{24,56},{... | collective-permute-start | bytes 786440 | tf_op jit(solution)/shard_map/ppermute | solution.py:149
  3.7 7.5 %collective-permute-start.1 = (bf16[256,512]{1,0:T(8,128)(2,1)}, bf16[256,512]{1,0:T(8,128)(2,1)S(1)}, u32[]{:S(2)}, u32[]{:S(2)}) collective-permute-start(bf16[256,512]{1,0:T(8,128)(2,1)} %refs_0_.1), channel_id=1, source_target_pairs={{64,0},{24,8},{80,16},{40,24},{96,32},{56,40},{112,48},{8,56},{128... | collective-permute-start | bytes 786440 | tf_op jit(solution)/shard_map/ppermute | solution.py:149
  4.5 7.4 %collective-permute-start.2 = (bf16[256,512]{1,0:T(8,128)(2,1)}, bf16[256,512]{1,0:T(8,128)(2,1)S(1)}, u32[]{:S(2)}, u32[]{:S(2)}) collective-permute-start(bf16[256,512]{1,0:T(8,128)(2,1)} %refs_0_.1), channel_id=1, source_target_pairs={{192,0},{56,8},{208,16},{8,24},{224,32},{24,40},{240,48},{40,56},{... | collective-permute-start | bytes 786440 | tf_op jit(solution)/shard_map/ppermute | solution.py:149
  12.7 7.9 %collective-permute-start.5 = (bf16[1024,512]{1,0:T(8,128)(2,1)}, bf16[1024,512]{1,0:T(8,128)(2,1)}, u32[]{:S(2)}, u32[]{:S(2)}) collective-permute-start(bf16[1024,512]{1,0:T(8,128)(2,1)} %constant_dynamic-update-slice_fusion.refs_0_), channel_id=1, source_target_pairs={{0,8},{8,0},{16,24},{24,16},{32,40},{40,32},{48,56},{56,48},{64,72... | collective-permute-start | bytes 3145736 | tf_op jit(solution)/shard_map/ppermute | solution.py:154
  14.9 15.4 %collective-permute-start.4 = (bf16[1024,512]{1,0:T(8,128)(2,1)}, bf16[1024,512]{1,0:T(8,128)(2,1)S(1)}, u32[]{:S(2)}, u32[]{:S(2)}) collective-permute-start(bf16[1024,512]{1,0:T(8,128)(2,1)} %constant_dynamic-update-slice_fusion.refs_0_), channel_id=1, source_target_pairs={{48,0},{200,8},{0,16},{216,24},{16,32},{232,40},{32,48},{248,56},{... | collective-permute-start | bytes 3145736 | tf_op jit(solution)/shard_map/ppermute | solution.py:149
  15.0 15.2 %collective-permute-start.3 = (bf16[1024,512]{1,0:T(8,128)(2,1)}, bf16[1024,512]{1,0:T(8,128)(2,1)}, u32[]{:S(2)}, u32[]{:S(2)}) collective-permute-start(bf16[1024,512]{1,0:T(8,128)(2,1)} %constant_dynamic-update-slice_fusion.refs_0_), channel_id=1, source_target_pairs={{16,0},{72,8},{32,16},{88,24},{48,32},{104,40},{0,48},{120,56},{80... | collective-permute-start | bytes 3145736 | tf_op jit(solution)/shard_map/ppermute | solution.py:149
  20.5 22.6 %copy-start.5 = (bf16[16,512]{1,0:T(8,128)(2,1)S(1)}, bf16[16,512]{1,0:T(8,128)(2,1)}, u32[]{:S(2)}) copy-start(bf16[16,512]{1,0:T(8,128)(2,1)} %param.18) | copy-start | bytes 49156
  20.5 22.6 %copy-start.8 = (s32[256]{0:T(256)S(1)}, s32[256]{0:T(256)}, u32[]{:S(2)}) copy-start(s32[256]{0:T(256)} %param.16) | copy-start | bytes 3076
  20.5 24.7 %copy-start.4 = (s32[1,1,32,1]{2,3,1,0:T(1,128)S(1)}, s32[1,1,32,1]{2,3,1,0:T(1,128)}, u32[]{:S(2)}) copy-start(s32[1,1,32,1]{2,3,1,0:T(1,128)} %param.14) | copy-start | bytes 388
  31.3 12.1 %collective-permute-start.8 = (bf16[1024,512]{1,0:T(8,128)(2,1)}, bf16[1024,512]{1,0:T(8,128)(2,1)S(1)}, u32[]{:S(2)}, u32[]{:S(2)}) collective-permute-start(bf16[1024,512]{1,0:T(8,128)(2,1)} %collective-permute-done.3.refs_1_), channel_id=1, source_target_pairs={{0,8},{8,0},{16,24},{24,16},{32,40},{40,32},{48,56},{56,48},{64,72... | collective-permute-start | bytes 3145736 | tf_op jit(solution)/shard_map/ppermute | solution.py:154
  32.3 9.6 %collective-permute-start.7 = (bf16[512,512]{1,0:T(8,128)(2,1)S(1)}, bf16[512,512]{1,0:T(8,128)(2,1)S(1)}, u32[]{:S(2)}, u32[]{:S(2)}) collective-permute-start(bf16[512,512]{1,0:T(8,128)(2,1)S(1)} %slice.53), channel_id=1, source_target_pairs={{48,0},{200,8},{0,16},{216,24},{16,32},{232,40},{32,48},{248,56},{... | collective-permute-start | bytes 1572872 | tf_op jit(solution)/shard_map/ppermute | solution.py:149
  33.0 10.4 %collective-permute-start.9 = (bf16[1024,512]{1,0:T(8,128)(2,1)S(1)}, bf16[1024,512]{1,0:T(8,128)(2,1)S(1)}, u32[]{:S(2)}, u32[]{:S(2)}) collective-permute-start(bf16[1024,512]{1,0:T(8,128)(2,1)S(1)} %collective-permute-done.4.refs_2_), channel_id=1, source_target_pairs={{0,8},{8,0},{16,24},{24,16},{32,40},{40,32},{48,56},{56,48},{64,72... | collective-permute-start | bytes 3145736 | tf_op jit(solution)/shard_map/ppermute | solution.py:154
  33.8 9.1 %collective-permute-start.6 = (bf16[512,512]{1,0:T(8,128)(2,1)S(1)}, bf16[512,512]{1,0:T(8,128)(2,1)S(1)}, u32[]{:S(2)}, u32[]{:S(2)}) collective-permute-start(bf16[512,512]{1,0:T(8,128)(2,1)S(1)} %slice.52), channel_id=1, source_target_pairs={{16,0},{72,8},{32,16},{88,24},{48,32},{104,40},{0,48},{120,56},{80... | collective-permute-start | bytes 1572872 | tf_op jit(solution)/shard_map/ppermute | solution.py:149
  41.9 2.5 %collective-permute-start.11 = (bf16[512,512]{1,0:T(8,128)(2,1)S(1)}, bf16[512,512]{1,0:T(8,128)(2,1)S(1)}, u32[]{:S(2)}, u32[]{:S(2)}) collective-permute-start(bf16[512,512]{1,0:T(8,128)(2,1)S(1)} %collective-permute-done.7.refs_4_), channel_id=1, source_target_pairs={{0,8},{8,0},{16,24},{24,16},{32,40},{40,32},{48,56},{56,48},{64,72... | collective-permute-start | bytes 1572872 | tf_op jit(solution)/shard_map/ppermute | solution.py:154
  42.9 2.3 %collective-permute-start.10 = (bf16[512,512]{1,0:T(8,128)(2,1)S(1)}, bf16[512,512]{1,0:T(8,128)(2,1)S(1)}, u32[]{:S(2)}, u32[]{:S(2)}) collective-permute-start(bf16[512,512]{1,0:T(8,128)(2,1)S(1)} %collective-permute-done.6.refs_3_), channel_id=1, source_target_pairs={{0,8},{8,0},{16,24},{24,16},{32,40},{40,32},{48,56},{56,48},{64,72... | collective-permute-start | bytes 1572872 | tf_op jit(solution)/shard_map/ppermute | solution.py:154
  43.4 6.0 %copy-start.9 = (s32[256]{0:T(256)S(1)}, s32[256]{0:T(256)}, u32[]{:S(2)}) copy-start(s32[256]{0:T(256)} %param.15) | copy-start | bytes 3076
  48.0 11.7 %collective-permute-start.14 = (bf16[256,512]{1,0:T(8,128)(2,1)S(1)}, bf16[256,512]{1,0:T(8,128)(2,1)S(1)}, u32[]{:S(2)}, u32[]{:S(2)}) collective-permute-start(bf16[256,512]{1,0:T(8,128)(2,1)S(1)} %get-tuple-element.42), channel_id=1, source_target_pairs={{0,1},{1,2},{2,3},{3,4},{4,5},{5,6},{6,7},{7,0},{8,9},{9,10},{10,1... | collective-permute-start | bytes 786440 | tf_op jit(solution)/shard_map/ppermute | solution.py:172
  49.6 33.9 %copy-start.2 = (bf16[2,2048,512]{2,1,0:T(8,128)(2,1)S(1)}, bf16[2,2048,512]{2,1,0:T(8,128)(2,1)}, u32[]{:S(2)}) copy-start(bf16[2,2048,512]{2,1,0:T(8,128)(2,1)} %w_out_ref.3) | copy-start | bytes 12582916
  51.1 22.3 %collective-permute-start.18 = (bf16[128,512]{1,0:T(8,128)(2,1)S(1)}, bf16[128,512]{1,0:T(8,128)(2,1)S(1)}, u32[]{:S(2)}, u32[]{:S(2)}) collective-permute-start(bf16[128,512]{1,0:T(8,128)(2,1)S(1)} %get-tuple-element.57), channel_id=1, source_target_pairs={{0,6},{1,7},{2,0},{3,1},{4,2},{5,3},{6,4},{7,5},{8,14},{9,15},{10,... | collective-permute-start | bytes 393224 | tf_op jit(solution)/shard_map/ppermute | solution.py:172
  56.3 7.8 %collective-permute-start.15 = (bf16[128,512]{1,0:T(8,128)(2,1)S(1)}, bf16[128,512]{1,0:T(8,128)(2,1)S(1)}, u32[]{:S(2)}, u32[]{:S(2)}) collective-permute-start(bf16[128,512]{1,0:T(8,128)(2,1)S(1)} %get-tuple-element.58), channel_id=1, source_target_pairs={{0,2},{1,3},{2,4},{3,5},{4,6},{5,7},{6,0},{7,1},{8,10},{9,11},{10,... | collective-permute-start | bytes 393224 | tf_op jit(solution)/shard_map/ppermute | solution.py:172
  56.3 19.0 %collective-permute-start.12 = (bf16[256,512]{1,0:T(8,128)(2,1)S(1)}, bf16[256,512]{1,0:T(8,128)(2,1)S(1)}, u32[]{:S(2)}, u32[]{:S(2)}) collective-permute-start(bf16[256,512]{1,0:T(8,128)(2,1)S(1)} %get-tuple-element.39), channel_id=1, source_target_pairs={{0,1},{1,2},{2,3},{3,4},{4,5},{5,6},{6,7},{7,0},{8,9},{9,10},{10,1... | collective-permute-start | bytes 786440 | tf_op jit(solution)/shard_map/ppermute | solution.py:172
  57.3 18.0 %collective-permute-start.13 = (bf16[256,512]{1,0:T(8,128)(2,1)S(1)}, bf16[256,512]{1,0:T(8,128)(2,1)S(1)}, u32[]{:S(2)}, u32[]{:S(2)}) collective-permute-start(bf16[256,512]{1,0:T(8,128)(2,1)S(1)} %get-tuple-element.40), channel_id=1, source_target_pairs={{0,7},{1,0},{2,1},{3,2},{4,3},{5,4},{6,5},{7,6},{8,15},{9,8},{10,9... | collective-permute-start | bytes 786440 | tf_op jit(solution)/shard_map/ppermute | solution.py:172
  59.7 13.6 %collective-permute-start.17 = (bf16[256,512]{1,0:T(8,128)(2,1)S(1)}, bf16[256,512]{1,0:T(8,128)(2,1)S(1)}, u32[]{:S(2)}, u32[]{:S(2)}) collective-permute-start(bf16[256,512]{1,0:T(8,128)(2,1)S(1)} %get-tuple-element.45), channel_id=1, source_target_pairs={{0,7},{1,0},{2,1},{3,2},{4,3},{5,4},{6,5},{7,6},{8,15},{9,8},{10,9... | collective-permute-start | bytes 786440 | tf_op jit(solution)/shard_map/ppermute | solution.py:172
  60.9 14.2 %copy-start.6 = (f32[2,512]{1,0:T(2,128)S(1)}, f32[2,512]{1,0:T(2,128)}, u32[]{:S(2)}) copy-start(f32[2,512]{1,0:T(2,128)} %param.19) | copy-start | bytes 12292
  64.1 19.4 %copy-start.1 = (bf16[2,512,2048]{2,1,0:T(8,128)(2,1)S(1)}, bf16[2,512,2048]{2,1,0:T(8,128)(2,1)}, u32[]{:S(2)}) copy-start(bf16[2,512,2048]{2,1,0:T(8,128)(2,1)} %w_in_ref.3) | copy-start | bytes 12582916
  64.2 19.4 %copy-start.3 = (bf16[256,512]{1,0:T(8,128)(2,1)S(1)}, bf16[256,512]{1,0:T(8,128)(2,1)}, u32[]{:S(2)}) copy-start(bf16[256,512]{1,0:T(8,128)(2,1)} %refs_0_.1) | copy-start | bytes 786436
  64.2 14.3 %collective-permute-start.16 = (bf16[256,512]{1,0:T(8,128)(2,1)S(1)}, bf16[256,512]{1,0:T(8,128)(2,1)S(1)}, u32[]{:S(2)}, u32[]{:S(2)}) collective-permute-start(bf16[256,512]{1,0:T(8,128)(2,1)S(1)} %pad_maximum_fusion.1), channel_id=1, source_target_pairs={{0,2},{1,3},{2,4},{3,5},{4,6},{5,7},{6,0},{7,1},{8,10},{9,11},{10,... | collective-permute-start | bytes 786440 | tf_op jit(solution)/shard_map/ppermute | solution.py:172
  73.4 10.1 %collective-permute-start.19 = (bf16[256,512]{1,0:T(8,128)(2,1)S(1)}, bf16[256,512]{1,0:T(8,128)(2,1)S(1)}, u32[]{:S(2)}, u32[]{:S(2)}) collective-permute-start(bf16[256,512]{1,0:T(8,128)(2,1)S(1)} %pad_maximum_fusion.2), channel_id=1, source_target_pairs={{0,6},{1,7},{2,0},{3,1},{4,2},{5,3},{6,4},{7,5},{8,14},{9,15},{10,... | collective-permute-start | bytes 786440 | tf_op jit(solution)/shard_map/ppermute | solution.py:172
  85.5 7.4 %collective-permute-start.22 = (bf16[256,512]{1,0:T(8,128)(2,1)S(1)}, bf16[256,512]{1,0:T(8,128)(2,1)S(1)}, u32[]{:S(2)}, u32[]{:S(2)}) collective-permute-start(bf16[256,512]{1,0:T(8,128)(2,1)S(1)} %node_mlp.2.refs_0_), channel_id=1, source_target_pairs={{192,0},{56,8},{208,16},{8,24},{224,32},{24,40},{240,48},{40,56},{... | collective-permute-start | bytes 786440 | tf_op jit(solution)/shard_map/ppermute | solution.py:149
  86.2 8.9 %collective-permute-start.21 = (bf16[256,512]{1,0:T(8,128)(2,1)S(1)}, bf16[256,512]{1,0:T(8,128)(2,1)S(1)}, u32[]{:S(2)}, u32[]{:S(2)}) collective-permute-start(bf16[256,512]{1,0:T(8,128)(2,1)S(1)} %node_mlp.2.refs_0_), channel_id=1, source_target_pairs={{64,0},{24,8},{80,16},{40,24},{96,32},{56,40},{112,48},{8,56},{128... | collective-permute-start | bytes 786440 | tf_op jit(solution)/shard_map/ppermute | solution.py:149
  88.9 8.0 %collective-permute-start.20 = (bf16[256,512]{1,0:T(8,128)(2,1)S(1)}, bf16[256,512]{1,0:T(8,128)(2,1)S(1)}, u32[]{:S(2)}, u32[]{:S(2)}) collective-permute-start(bf16[256,512]{1,0:T(8,128)(2,1)S(1)} %node_mlp.2.refs_0_), channel_id=1, source_target_pairs={{128,0},{40,8},{144,16},{56,24},{160,32},{8,40},{176,48},{24,56},{... | collective-permute-start | bytes 786440 | tf_op jit(solution)/shard_map/ppermute | solution.py:149
  96.9 15.2 %collective-permute-start.24 = (bf16[1024,512]{1,0:T(8,128)(2,1)S(1)}, bf16[1024,512]{1,0:T(8,128)(2,1)S(1)}, u32[]{:S(2)}, u32[]{:S(2)}) collective-permute-start(bf16[1024,512]{1,0:T(8,128)(2,1)S(1)} %pad_maximum_fusion.refs_0_), channel_id=1, source_target_pairs={{48,0},{200,8},{0,16},{216,24},{16,32},{232,40},{32,48},{248,56},{... | collective-permute-start | bytes 3145736 | tf_op jit(solution)/shard_map/ppermute | solution.py:149
  97.1 15.1 %collective-permute-start.23 = (bf16[1024,512]{1,0:T(8,128)(2,1)S(1)}, bf16[1024,512]{1,0:T(8,128)(2,1)S(1)}, u32[]{:S(2)}, u32[]{:S(2)}) collective-permute-start(bf16[1024,512]{1,0:T(8,128)(2,1)S(1)} %pad_maximum_fusion.refs_0_), channel_id=1, source_target_pairs={{16,0},{72,8},{32,16},{88,24},{48,32},{104,40},{0,48},{120,56},{80... | collective-permute-start | bytes 3145736 | tf_op jit(solution)/shard_map/ppermute | solution.py:149
  99.7 25.6 %collective-permute-start.27 = (bf16[1024,512]{1,0:T(8,128)(2,1)S(1)}, bf16[1024,512]{1,0:T(8,128)(2,1)S(1)}, u32[]{:S(2)}, u32[]{:S(2)}) collective-permute-start(bf16[1024,512]{1,0:T(8,128)(2,1)S(1)} %pad_maximum_fusion.refs_0_), channel_id=1, source_target_pairs={{0,8},{8,0},{16,24},{24,16},{32,40},{40,32},{48,56},{56,48},{64,72... | collective-permute-start | bytes 3145736 | tf_op jit(solution)/shard_map/ppermute | solution.py:154
  112.2 9.6 %collective-permute-start.26 = (bf16[512,512]{1,0:T(8,128)(2,1)S(1)}, bf16[512,512]{1,0:T(8,128)(2,1)S(1)}, u32[]{:S(2)}, u32[]{:S(2)}) collective-permute-start(bf16[512,512]{1,0:T(8,128)(2,1)S(1)} %slice.73), channel_id=1, source_target_pairs={{48,0},{200,8},{0,16},{216,24},{16,32},{232,40},{32,48},{248,56},{... | collective-permute-start | bytes 1572872 | tf_op jit(solution)/shard_map/ppermute | solution.py:149
  112.3 12.9 %collective-permute-start.25 = (bf16[512,512]{1,0:T(8,128)(2,1)S(1)}, bf16[512,512]{1,0:T(8,128)(2,1)S(1)}, u32[]{:S(2)}, u32[]{:S(2)}) collective-permute-start(bf16[512,512]{1,0:T(8,128)(2,1)S(1)} %slice.72), channel_id=1, source_target_pairs={{16,0},{72,8},{32,16},{88,24},{48,32},{104,40},{0,48},{120,56},{80... | collective-permute-start | bytes 1572872 | tf_op jit(solution)/shard_map/ppermute | solution.py:149
  115.1 12.5 %collective-permute-start.29 = (bf16[1024,512]{1,0:T(8,128)(2,1)S(1)}, bf16[1024,512]{1,0:T(8,128)(2,1)S(1)}, u32[]{:S(2)}, u32[]{:S(2)}) collective-permute-start(bf16[1024,512]{1,0:T(8,128)(2,1)S(1)} %collective-permute-done.24.refs_2_), channel_id=1, source_target_pairs={{0,8},{8,0},{16,24},{24,16},{32,40},{40,32},{48,56},{56,48},{64,72... | collective-permute-start | bytes 3145736 | tf_op jit(solution)/shard_map/ppermute | solution.py:154
  118.2 9.3 %collective-permute-start.28 = (bf16[1024,512]{1,0:T(8,128)(2,1)S(1)}, bf16[1024,512]{1,0:T(8,128)(2,1)S(1)}, u32[]{:S(2)}, u32[]{:S(2)}) collective-permute-start(bf16[1024,512]{1,0:T(8,128)(2,1)S(1)} %collective-permute-done.23.refs_1_), channel_id=1, source_target_pairs={{0,8},{8,0},{16,24},{24,16},{32,40},{40,32},{48,56},{56,48},{64,72... | collective-permute-start | bytes 3145736 | tf_op jit(solution)/shard_map/ppermute | solution.py:154
  121.8 5.0 %collective-permute-start.31 = (bf16[512,512]{1,0:T(8,128)(2,1)S(1)}, bf16[512,512]{1,0:T(8,128)(2,1)S(1)}, u32[]{:S(2)}, u32[]{:S(2)}) collective-permute-start(bf16[512,512]{1,0:T(8,128)(2,1)S(1)} %collective-permute-done.26.refs_4_), channel_id=1, source_target_pairs={{0,8},{8,0},{16,24},{24,16},{32,40},{40,32},{48,56},{56,48},{64,72... | collective-permute-start | bytes 1572872 | tf_op jit(solution)/shard_map/ppermute | solution.py:154
  125.2 2.3 %collective-permute-start.30 = (bf16[512,512]{1,0:T(8,128)(2,1)S(1)}, bf16[512,512]{1,0:T(8,128)(2,1)S(1)}, u32[]{:S(2)}, u32[]{:S(2)}) collective-permute-start(bf16[512,512]{1,0:T(8,128)(2,1)S(1)} %collective-permute-done.25.refs_3_), channel_id=1, source_target_pairs={{0,8},{8,0},{16,24},{24,16},{32,40},{40,32},{48,56},{56,48},{64,72... | collective-permute-start | bytes 1572872 | tf_op jit(solution)/shard_map/ppermute | solution.py:154
  129.0 12.9 %collective-permute-start.34 = (bf16[256,512]{1,0:T(8,128)(2,1)S(1)}, bf16[256,512]{1,0:T(8,128)(2,1)S(1)}, u32[]{:S(2)}, u32[]{:S(2)}) collective-permute-start(bf16[256,512]{1,0:T(8,128)(2,1)S(1)} %get-tuple-element.51), channel_id=1, source_target_pairs={{0,1},{1,2},{2,3},{3,4},{4,5},{5,6},{6,7},{7,0},{8,9},{9,10},{10,1... | collective-permute-start | bytes 786440 | tf_op jit(solution)/shard_map/ppermute | solution.py:172
  135.5 20.5 %collective-permute-start.38 = (bf16[128,512]{1,0:T(8,128)(2,1)S(1)}, bf16[128,512]{1,0:T(8,128)(2,1)S(1)}, u32[]{:S(2)}, u32[]{:S(2)}) collective-permute-start(bf16[128,512]{1,0:T(8,128)(2,1)S(1)} %get-tuple-element.55), channel_id=1, source_target_pairs={{0,6},{1,7},{2,0},{3,1},{4,2},{5,3},{6,4},{7,5},{8,14},{9,15},{10,... | collective-permute-start | bytes 393224 | tf_op jit(solution)/shard_map/ppermute | solution.py:172
  138.2 10.2 %collective-permute-start.35 = (bf16[128,512]{1,0:T(8,128)(2,1)S(1)}, bf16[128,512]{1,0:T(8,128)(2,1)S(1)}, u32[]{:S(2)}, u32[]{:S(2)}) collective-permute-start(bf16[128,512]{1,0:T(8,128)(2,1)S(1)} %get-tuple-element.56), channel_id=1, source_target_pairs={{0,2},{1,3},{2,4},{3,5},{4,6},{5,7},{6,0},{7,1},{8,10},{9,11},{10,... | collective-permute-start | bytes 393224 | tf_op jit(solution)/shard_map/ppermute | solution.py:172
  138.2 19.6 %collective-permute-start.32 = (bf16[256,512]{1,0:T(8,128)(2,1)S(1)}, bf16[256,512]{1,0:T(8,128)(2,1)S(1)}, u32[]{:S(2)}, u32[]{:S(2)}) collective-permute-start(bf16[256,512]{1,0:T(8,128)(2,1)S(1)} %get-tuple-element.48), channel_id=1, source_target_pairs={{0,1},{1,2},{2,3},{3,4},{4,5},{5,6},{6,7},{7,0},{8,9},{9,10},{10,1... | collective-permute-start | bytes 786440 | tf_op jit(solution)/shard_map/ppermute | solution.py:172
  138.2 19.6 %collective-permute-start.33 = (bf16[256,512]{1,0:T(8,128)(2,1)S(1)}, bf16[256,512]{1,0:T(8,128)(2,1)S(1)}, u32[]{:S(2)}, u32[]{:S(2)}) collective-permute-start(bf16[256,512]{1,0:T(8,128)(2,1)S(1)} %get-tuple-element.49), channel_id=1, source_target_pairs={{0,7},{1,0},{2,1},{3,2},{4,3},{5,4},{6,5},{7,6},{8,15},{9,8},{10,9... | collective-permute-start | bytes 786440 | tf_op jit(solution)/shard_map/ppermute | solution.py:172
  141.9 14.0 %collective-permute-start.37 = (bf16[256,512]{1,0:T(8,128)(2,1)S(1)}, bf16[256,512]{1,0:T(8,128)(2,1)S(1)}, u32[]{:S(2)}, u32[]{:S(2)}) collective-permute-start(bf16[256,512]{1,0:T(8,128)(2,1)S(1)} %get-tuple-element.54), channel_id=1, source_target_pairs={{0,7},{1,0},{2,1},{3,2},{4,3},{5,4},{6,5},{7,6},{8,15},{9,8},{10,9... | collective-permute-start | bytes 786440 | tf_op jit(solution)/shard_map/ppermute | solution.py:172
  148.4 16.8 %collective-permute-start.36 = (bf16[256,512]{1,0:T(8,128)(2,1)S(1)}, bf16[256,512]{1,0:T(8,128)(2,1)S(1)}, u32[]{:S(2)}, u32[]{:S(2)}) collective-permute-start(bf16[256,512]{1,0:T(8,128)(2,1)S(1)} %pad_maximum_fusion.3), channel_id=1, source_target_pairs={{0,2},{1,3},{2,4},{3,5},{4,6},{5,7},{6,0},{7,1},{8,10},{9,11},{10,... | collective-permute-start | bytes 786440 | tf_op jit(solution)/shard_map/ppermute | solution.py:172
  156.1 11.1 %collective-permute-start.39 = (bf16[256,512]{1,0:T(8,128)(2,1)S(1)}, bf16[256,512]{1,0:T(8,128)(2,1)S(1)}, u32[]{:S(2)}, u32[]{:S(2)}) collective-permute-start(bf16[256,512]{1,0:T(8,128)(2,1)S(1)} %pad_maximum_fusion.4), channel_id=1, source_target_pairs={{0,6},{1,7},{2,0},{3,1},{4,2},{5,3},{6,4},{7,5},{8,14},{9,15},{10,... | collective-permute-start | bytes 786440 | tf_op jit(solution)/shard_map/ppermute | solution.py:172
